TPU v7x, 128 devices: a whole 4x4x4 slice. The times are simulated.
128 devices in a mesh: dp: 32 (over y, z, core), section: 4 (over x).
Axes of the slice: x: 4, y: 4, z: 4, core: 2. Of those that a mesh axis runs over, the one named last changes fastest.
Arguments:
- hidden_in: bfloat16 [16384, 4096], P(('dp', 'section')), may hold values from -17 to 17
- segments: int32 [128, 128], P(('dp', 'section')), may hold values from 0 to 1, never falling along the last dimension, each value on 1 to 96 neighbouring positions
- forget_flags: int32 [128, 2], P(('dp', 'section')), may hold values 0 or 1
- block_plan: int32 [128], replicated, may hold values from 0 to 127, each once
- layer_gains: bfloat16 [4, 4096], P('section'), may hold values from 0.25 to 1.75
- kv_weights: bfloat16 [4, 4096, 1024], P('section', 'dp'), may hold values from -2 to 2
- frozen_states: bfloat16 [16384, 4096], P(('dp', 'section')), may hold values from -18 to 18
Outputs:
- hidden_out: bfloat16 [16384, 4096], P(('dp', 'section'))
- objective: float32 [], replicated
Inputs may be any that keep to these rules, and one draw needn't show every extreme that they name: `segments`: in each block the segment numbers never fall; each of the 2 sequences has 1 to 96 tokens. `block_plan`: a permutation of the 128 block positions.
All inputs are finite; a program needn't handle non-finite values. No bound on the sum of `forget_flags` on one device may be relied on, other than what follows from the above.
Results may differ from a plain program's by a relative error of at most 0.02.
Values may be sent and summed in bfloat16 or wider, within the bound.
No kernel may reach another device: no remote copies, remote signals or barrier semaphores. Data moves between devices by JAX's collectives and lax.ppermute only.
A program may use at most 128 MiB of HBM per device.

v0:
```python
import math

import jax
import jax.numpy as jnp
from jax import lax
from jax.sharding import PartitionSpec as P

QH = 32
KVH = 4
HS = 128
GROUP = 8


forget_weight = 0.5


def shifted(array, axis, by):
    peers = lax.axis_size(axis)
    pairs = [(i, i + by) for i in range(peers) if 0 <= i + by < peers]
    return lax.ppermute(array, axis, pairs)


def attention_layer(states, token_tags, weights, gain_row):
    widened = states.astype(jnp.float32)
    inverse_rms = lax.rsqrt(jnp.mean(widened * widened, axis=-1, keepdims=True) + 1e-05)
    normed = (widened * inverse_rms * gain_row.astype(jnp.float32)).astype(jnp.bfloat16)
    keys_values = jnp.dot(normed, weights, preferred_element_type=jnp.float32).astype(jnp.bfloat16)
    row_count = states.shape[0]
    head_width = KVH * HS
    key_heads = keys_values[:, :head_width].reshape(row_count, KVH, HS)
    value_heads = keys_values[:, head_width:].reshape(row_count, KVH, HS)
    query_heads = normed.reshape(row_count, KVH, GROUP, HS)
    scores = jnp.einsum(
        "tkgd,skd->kgts", query_heads, key_heads, preferred_element_type=jnp.float32
    ) / math.sqrt(HS)
    segment_ids = token_tags // 2
    positions = jnp.arange(row_count, dtype=jnp.int32)
    allowed = (segment_ids[:, None] == segment_ids[None, :]) & (
        positions[None, :] <= positions[:, None]
    )
    scores = jnp.where(allowed[None, None], scores, -jnp.inf)
    soft_weights = jax.nn.softmax(scores, axis=-1).astype(jnp.bfloat16)
    mixture = jnp.einsum(
        "kgts,skd->tkgd", soft_weights, value_heads, preferred_element_type=jnp.float32
    )
    return (widened + mixture.reshape(row_count, QH * HS)).astype(jnp.bfloat16)


def route(block_rows, tag_rows, block_plan):
    feature_count = block_rows.shape[1]
    along_dp = lax.axis_size("dp")
    along_section = lax.axis_size("section")
    device_count = along_dp * along_section
    piece_rows = block_rows.shape[0] // device_count
    pieces = block_rows.reshape(device_count, piece_rows, feature_count)
    piece_tags = tag_rows.reshape(device_count, piece_rows)
    landed, landed_tags = (
        lax.all_to_all(pieces, ("dp", "section"), split_axis=0, concat_axis=0, tiled=True),
        lax.all_to_all(piece_tags, ("dp", "section"), split_axis=0, concat_axis=0, tiled=True),
    )
    slot_ids = jnp.arange(device_count, dtype=jnp.int32)
    sources = jnp.sum(
        jnp.where(block_plan[None, :] == slot_ids[:, None], slot_ids[None, :], 0), axis=1
    )
    ordered = jnp.take(landed, sources, axis=0)
    ordered_tags = jnp.take(landed_tags, sources, axis=0)
    arrived, arrived_tags = (
        lax.all_to_all(ordered, ("dp", "section"), split_axis=0, concat_axis=0, tiled=True),
        lax.all_to_all(ordered_tags, ("dp", "section"), split_axis=0, concat_axis=0, tiled=True),
    )
    return (
        arrived.reshape(device_count * piece_rows, feature_count),
        arrived_tags.reshape(device_count * piece_rows),
    )


def local(hidden_in, segments, forget_flags, block_plan, layer_gains, kv_weights, frozen_states):
    segment_ids = segments[0]
    seg_range = jnp.arange(forget_flags.shape[1], dtype=jnp.int32)
    token_flags = jnp.sum(
        jnp.where(segment_ids[:, None] == seg_range[None, :], forget_flags[0][None, :], 0), axis=1
    )
    token_tags = segment_ids * 2 + token_flags
    block_rows, tag_rows = route(hidden_in, token_tags, block_plan)
    own_weights = lax.all_gather(kv_weights, "dp", axis=1, tiled=True)
    section_count = lax.axis_size("section")
    weights = own_weights[0]
    gain_row = layer_gains[0]
    section_here = lax.axis_index("section")
    current, current_tags = (block_rows, tag_rows)
    finished = jnp.zeros_like(block_rows)
    for moment in range(2 * section_count - 1):
        if 0 < moment < section_count:
            fed_rows, fed_tags = shifted((block_rows, tag_rows), "section", -moment)
            at_entry = section_here == 0
            current = jnp.where(at_entry, fed_rows, current)
            current_tags = jnp.where(at_entry, fed_tags, current_tags)
        produced = attention_layer(current, current_tags, weights, gain_row)
        micro_index = moment - (section_count - 1)
        if 0 <= micro_index < section_count - 1:
            landed_out = shifted(produced, "section", micro_index - (section_count - 1))
            finished = jnp.where(section_here == micro_index, landed_out, finished)
        elif micro_index == section_count - 1:
            finished = jnp.where(section_here == micro_index, produced, finished)
        if moment < 2 * section_count - 2:
            current, current_tags = shifted((produced, current_tags), "section", 1)
    difference = finished.astype(jnp.float32) - frozen_states.astype(jnp.float32)
    distance = jnp.mean(difference * difference, axis=1)
    routed_flags = (tag_rows % 2).astype(jnp.float32)
    retain_part = jnp.sum((1.0 - routed_flags) * distance)
    forget_part = jnp.sum(routed_flags * distance)
    retain_total, forget_total = lax.psum((retain_part, forget_part), ("dp", "section"))
    token_total = finished.shape[0] * lax.axis_size("dp") * lax.axis_size("section")
    objective = (retain_total - forget_weight * forget_total) / token_total
    return (finished, objective)


def solution(mesh):
    in_specs = (
        P(("dp", "section"), None),
        P(("dp", "section"), None),
        P(("dp", "section"), None),
        P(),
        P("section", None),
        P("section", "dp", None),
        P(("dp", "section"), None),
    )
    out_specs = (P(("dp", "section"), None), P())
    return jax.shard_map(local, mesh=mesh, in_specs=in_specs, out_specs=out_specs, check_vma=False)
```

profile of v0, /device:TPU:1, one launch (start us, length us, event | category | flops | bytes accessed | tf_op | source)
XLA Modules:
  0.0 481.3 jit_solution(4722382592948686103)
XLA Ops:
  10.1 11.5 %all-to-all-start.2 = ((s32[128,1,1]{2,1,0:T(1,128)}), s32[128,1,1]{2,1,0:T(1,128)S(1)}, u32[]{:S(2)}, u32[]{:S(2)}) async-start(s32[128,1,1]{2,1,0:T(1,128)} %copy.160), calls=%async_computation.2 | async-start | bytes 131072 | tf_op jit(solution)/shard_map/all_to_all | solution.py:59
  22.1 2.7 reduce.2
  26.4 5.1 %all-to-all-done.2 = s32[128,1,1]{2,1,0:T(1,128)S(1)} async-done(((s32[128,1,1]{2,1,0:T(1,128)}), s32[128,1,1]{2,1,0:T(1,128)S(1)}, u32[]{:S(2)}, u32[]{:S(2)}) %all-to-all-start.2) | async-done | bytes 544 | tf_op jit(solution)/shard_map/all_to_all | solution.py:59
  31.4 4.7 all-to-all-start
  36.3 2.4 reduce
  40.6 15.3 %all-to-all-done = bf16[128,2,2048]{2,1,0:T(2,128)(2,1)S(1)} async-done(((bf16[128,2,2048]{2,1,0:T(2,128)(2,1)}), bf16[128,2,2048]{2,1,0:T(2,128)(2,1)S(1)}, u32[]{:S(2)}, u32[]{:S(2)}) %all-to-all-start) | async-done | bytes 1048608 | tf_op jit(solution)/shard_map/all_to_all | solution.py:58
  56.9 3.8 all-to-all-start.3
  60.7 6.5 %reshape.684 = bf16[128,1,4096]{2,1,0:T(2,128)(2,1)S(1)} reshape(bf16[128,2,2048]{2,1,0:T(2,128)(2,1)} %copy-done) | data formatting | bytes 2097152
  72.8 10.0 %all-to-all-start.1 = ((bf16[128,2,2048]{2,1,0:T(2,128)(2,1)}), bf16[128,2,2048]{2,1,0:T(2,128)(2,1)S(1)}, u32[]{:S(2)}, u32[]{:S(2)}) async-start(bf16[128,2,2048]{2,1,0:T(2,128)(2,1)} %reshape.685), calls=%async_computation.1 | async-start | bytes 2097152 | tf_op jit(solution)/shard_map/all_to_all | solution.py:68
  86.5 16.0 %all-to-all-done.1 = bf16[128,2,2048]{2,1,0:T(2,128)(2,1)S(1)} async-done(((bf16[128,2,2048]{2,1,0:T(2,128)(2,1)}), bf16[128,2,2048]{2,1,0:T(2,128)(2,1)S(1)}, u32[]{:S(2)}, u32[]{:S(2)}) %all-to-all-start.1) | async-done | bytes 1048608 | tf_op jit(solution)/shard_map/all_to_all | solution.py:68
  107.3 4.7 fusion.58
  116.2 3.7 fusion.114
  123.0 5.1 %collective-permute-start.3 = (bf16[128,4096]{1,0:T(8,128)(2,1)}, bf16[128,4096]{1,0:T(8,128)(2,1)}, u32[]{:S(2)}, u32[]{:S(2)}) collective-permute-start(bf16[128,4096]{1,0:T(8,128)(2,1)} %fusion.22), channel_id=1, source_target_pairs={{0,1},{1,2},{2,3},{4,5},{5,6},{6,7},{8,9},{9,10},{10,11},{12,13},{... | collective-permute-start | bytes 3145736 | tf_op jit(solution)/shard_map/ppermute | solution.py:20
  129.4 4.0 collective-permute-start.5
  133.4 15.9 %collective-permute-done.5 = s32[128]{0:T(128)S(1)} collective-permute-done((s32[128]{0:T(128)S(1)}, s32[128]{0:T(128)S(1)}, u32[]{:S(2)}, u32[]{:S(2)}) %collective-permute-start.5) | collective-permute-done | bytes 544 | tf_op jit(solution)/shard_map/ppermute | solution.py:20
  155.4 4.7 fusion.61
  160.2 3.6 fusion.256
  163.8 3.3 fusion.115
  167.1 3.0 copy.171
  171.9 4.2 collective-permute-start.6
  177.4 3.0 collective-permute-start.8
  180.4 21.1 %collective-permute-done.7 = s32[128]{0:T(128)S(1)} collective-permute-done((s32[128]{0:T(128)S(1)}, s32[128]{0:T(128)S(1)}, u32[]{:S(2)}, u32[]{:S(2)}) %collective-permute-start.7) | collective-permute-done | bytes 544 | tf_op jit(solution)/shard_map/ppermute | solution.py:20
  205.1 4.7 fusion.64
  210.0 3.0 fusion.261
  213.0 3.4 fusion.116
  216.4 2.9 copy.176
  225.8 3.6 collective-permute-done.10
  229.4 12.9 %collective-permute-done.11 = s32[128]{0:T(128)S(1)} collective-permute-done((s32[128]{0:T(128)S(1)}, s32[128]{0:T(128)S(1)}, u32[]{:S(2)}, u32[]{:S(2)}) %collective-permute-start.11) | collective-permute-done | bytes 544 | tf_op jit(solution)/shard_map/ppermute | solution.py:20
  244.7 4.7 fusion.67
  251.9 3.3 fusion.117
  257.4 2.9 collective-permute-start.12
  260.3 4.9 %collective-permute-start.13 = (s32[128]{0:T(128)S(1)}, s32[128]{0:T(128)S(1)}, u32[]{:S(2)}, u32[]{:S(2)}) collective-permute-start(s32[128]{0:T(128)S(1)} %get-tuple-element.9), channel_id=1, source_target_pairs={{0,1},{1,2},{2,3},{4,5},{5,6},{6,7},{8,9},{9,10},{10,11},{12,13},{... | collective-permute-start | bytes 1544 | tf_op jit(solution)/shard_map/ppermute | solution.py:20
  265.3 13.8 %collective-permute-done.13 = s32[128]{0:T(128)S(1)} collective-permute-done((s32[128]{0:T(128)S(1)}, s32[128]{0:T(128)S(1)}, u32[]{:S(2)}, u32[]{:S(2)}) %collective-permute-start.13) | collective-permute-done | bytes 544 | tf_op jit(solution)/shard_map/ppermute | solution.py:20
  280.1 4.7 fusion.70
  287.4 3.3 fusion.118
  292.8 4.6 collective-permute-start.14
  297.4 4.2 collective-permute-start.15
  301.6 13.2 %collective-permute-done.15 = s32[128]{0:T(128)S(1)} collective-permute-done((s32[128]{0:T(128)S(1)}, s32[128]{0:T(128)S(1)}, u32[]{:S(2)}, u32[]{:S(2)}) %collective-permute-start.15) | collective-permute-done | bytes 544 | tf_op jit(solution)/shard_map/ppermute | solution.py:20
  315.9 4.7 fusion.73
  323.1 3.3 fusion.119
  329.5 4.1 collective-permute-start.16
  333.6 4.0 collective-permute-start.17
  337.6 12.7 %collective-permute-done.17 = s32[128]{0:T(128)S(1)} collective-permute-done((s32[128]{0:T(128)S(1)}, s32[128]{0:T(128)S(1)}, u32[]{:S(2)}, u32[]{:S(2)}) %collective-permute-start.17) | collective-permute-done | bytes 544 | tf_op jit(solution)/shard_map/ppermute | solution.py:20
  354.6 4.7 fusion.76
  362.4 3.3 fusion.120
  367.7 32.1 %collective-permute-done.20 = bf16[128,4096]{1,0:T(8,128)(2,1)} collective-permute-done((bf16[128,4096]{1,0:T(8,128)(2,1)}, bf16[128,4096]{1,0:T(8,128)(2,1)}, u32[]{:S(2)}, u32[]{:S(2)}) %collective-permute-start.20) | collective-permute-done | bytes 1048608 | tf_op jit(solution)/shard_map/ppermute | solution.py:20
  399.8 3.4 multiply_reduce_fusion
  404.0 67.9 %all-reduce = (f32[]{:T(128)}, f32[]{:T(128)}) all-reduce(f32[]{:T(128)} %get-tuple-element.3, f32[]{:T(128)} %get-tuple-element.2), channel_id=1, replica_groups=mesh['dp'=32,'section'=4] {'dp','section'}, use_global_device_ids=true, to_apply=%region_25.26 | all-reduce | flops 2 | bytes 16 | tf_op jit(solution)/shard_map/psum | solution.py:112
  (159 shorter events, 79.4 us)
Async XLA Ops:
  7.2 100.1 %all-gather.2.cloned.1.call-start = ((), (), s32[]{:S(2)}) async-start(), calls=%async_computation.4 | async-start | bytes 8650752 | tf_op jit(solution)/shard_map/all_gather | solution.py:85
  10.1 21.4 %all-to-all-start.2 = ((s32[128,1,1]{2,1,0:T(1,128)}), s32[128,1,1]{2,1,0:T(1,128)S(1)}, u32[]{:S(2)}, u32[]{:S(2)}) async-start(s32[128,1,1]{2,1,0:T(1,128)} %copy.160), calls=%async_computation.2 | async-start | bytes 131072 | tf_op jit(solution)/shard_map/all_to_all | solution.py:59
  24.8 11.4 %copy-start.14 = (s32[128]{0:T(128)S(1)}, s32[128]{0:T(128)}, u32[]{:S(2)}) copy-start(s32[128]{0:T(128)} %param.10) | copy-start | bytes 1540
  31.4 24.4 %all-to-all-start = ((bf16[128,2,2048]{2,1,0:T(2,128)(2,1)}), bf16[128,2,2048]{2,1,0:T(2,128)(2,1)S(1)}, u32[]{:S(2)}, u32[]{:S(2)}) async-start(bf16[128,2,2048]{2,1,0:T(2,128)(2,1)} %reshape.683), calls=%async_computation | async-start | bytes 2097152 | tf_op jit(solution)/shard_map/all_to_all | solution.py:58
  55.9 1.0 copy-start
  56.9 15.9 %all-to-all-start.3 = ((s32[128,1,1]{2,1,0:T(1,128)}), s32[128,1,1]{2,1,0:T(1,128)S(1)}, u32[]{:S(2)}, u32[]{:S(2)}) async-start(s32[128,1,1]{2,1,0:T(1,128)} %copy.161), calls=%async_computation.3 | async-start | bytes 131072 | tf_op jit(solution)/shard_map/all_to_all | solution.py:69
  71.2 11.7 %copy-start.4 = (bf16[1,4096]{1,0:T(2,128)(2,1)S(1)}, bf16[1,4096]{1,0:T(2,128)(2,1)}, u32[]{:S(2)}) copy-start(bf16[1,4096]{1,0:T(2,128)(2,1)} %param.11) | copy-start | bytes 24580
  72.8 29.7 %all-to-all-start.1 = ((bf16[128,2,2048]{2,1,0:T(2,128)(2,1)}), bf16[128,2,2048]{2,1,0:T(2,128)(2,1)S(1)}, u32[]{:S(2)}, u32[]{:S(2)}) async-start(bf16[128,2,2048]{2,1,0:T(2,128)(2,1)} %reshape.685), calls=%async_computation.1 | async-start | bytes 2097152 | tf_op jit(solution)/shard_map/all_to_all | solution.py:68
  85.2 1.3 copy-start.6
  105.6 46.4 %collective-permute-start.2 = (bf16[128,4096]{1,0:T(8,128)(2,1)S(1)}, bf16[128,4096]{1,0:T(8,128)(2,1)}, u32[]{:S(2)}, u32[]{:S(2)}) collective-permute-start(bf16[128,4096]{1,0:T(8,128)(2,1)S(1)} %bitcast.211), channel_id=1, source_target_pairs={{1,0},{2,1},{3,2},{5,4},{6,5},{7,6},{9,8},{10,9},{11,10},{13,12},{... | collective-permute-start | bytes 3145736 | tf_op jit(solution)/shard_map/ppermute | solution.py:20
  107.2 4.7 copy-start.10
  112.2 3.5 copy-start.5
  114.2 1.4 copy-start.1
  121.8 6.2 %copy-start.7 = (s32[128]{0:T(128)S(1)}, s32[128]{0:T(128)}, u32[]{:S(2)}) copy-start(s32[128]{0:T(128)} %copy-done.6) | copy-start | bytes 1540
  123.0 29.0 %collective-permute-start.3 = (bf16[128,4096]{1,0:T(8,128)(2,1)}, bf16[128,4096]{1,0:T(8,128)(2,1)}, u32[]{:S(2)}, u32[]{:S(2)}) collective-permute-start(bf16[128,4096]{1,0:T(8,128)(2,1)} %fusion.22), channel_id=1, source_target_pairs={{0,1},{1,2},{2,3},{4,5},{5,6},{6,7},{8,9},{9,10},{10,11},{12,13},{... | collective-permute-start | bytes 3145736 | tf_op jit(solution)/shard_map/ppermute | solution.py:20
  128.1 5.3 %collective-permute-start.4 = (s32[128]{0:T(128)S(1)}, s32[128]{0:T(128)S(1)}, u32[]{:S(2)}, u32[]{:S(2)}) collective-permute-start(s32[128]{0:T(128)S(1)} %copy-done.7), channel_id=1, source_target_pairs={{1,0},{2,1},{3,2},{5,4},{6,5},{7,6},{9,8},{10,9},{11,10},{13,12},{... | collective-permute-start | bytes 1544 | tf_op jit(solution)/shard_map/ppermute | solution.py:20
  129.4 19.9 %collective-permute-start.5 = (s32[128]{0:T(128)S(1)}, s32[128]{0:T(128)S(1)}, u32[]{:S(2)}, u32[]{:S(2)}) collective-permute-start(s32[128]{0:T(128)S(1)} %copy-done.7), channel_id=1, source_target_pairs={{0,1},{1,2},{2,3},{4,5},{5,6},{6,7},{8,9},{9,10},{10,11},{12,13},{... | collective-permute-start | bytes 1544 | tf_op jit(solution)/shard_map/ppermute | solution.py:20
  150.5 53.5 %collective-permute-start.1 = (bf16[128,4096]{1,0:T(8,128)(2,1)S(1)}, bf16[128,4096]{1,0:T(8,128)(2,1)S(1)}, u32[]{:S(2)}, u32[]{:S(2)}) collective-permute-start(bf16[128,4096]{1,0:T(8,128)(2,1)S(1)} %bitcast.212), channel_id=1, source_target_pairs={{2,0},{3,1},{6,4},{7,5},{10,8},{11,9},{14,12},{15,13},{18,16},{19,... | collective-permute-start | bytes 3145736 | tf_op jit(solution)/shard_map/ppermute | solution.py:20
  170.1 6.0 %copy-start.8 = (s32[128]{0:T(128)S(1)}, s32[128]{0:T(128)}, u32[]{:S(2)}) copy-start(s32[128]{0:T(128)} %copy-done.6) | copy-start | bytes 1540
  170.1 7.3 %copy-start.12 = (s32[128]{0:T(128)S(1)}, s32[128]{0:T(128)}, u32[]{:S(2)}) copy-start(s32[128]{0:T(128)} %get-tuple-element.17) | copy-start | bytes 1540
  171.9 32.1 %collective-permute-start.6 = (bf16[128,4096]{1,0:T(8,128)(2,1)S(1)}, bf16[128,4096]{1,0:T(8,128)(2,1)S(1)}, u32[]{:S(2)}, u32[]{:S(2)}) collective-permute-start(bf16[128,4096]{1,0:T(8,128)(2,1)S(1)} %fusion.28), channel_id=1, source_target_pairs={{0,1},{1,2},{2,3},{4,5},{5,6},{6,7},{8,9},{9,10},{10,11},{12,13},{... | collective-permute-start | bytes 3145736 | tf_op jit(solution)/shard_map/ppermute | solution.py:20
  176.1 25.4 %collective-permute-start.7 = (s32[128]{0:T(128)S(1)}, s32[128]{0:T(128)S(1)}, u32[]{:S(2)}, u32[]{:S(2)}) collective-permute-start(s32[128]{0:T(128)S(1)} %copy-done.8), channel_id=1, source_target_pairs={{2,0},{3,1},{6,4},{7,5},{10,8},{11,9},{14,12},{15,13},{18,16},{19,... | collective-permute-start | bytes 1544 | tf_op jit(solution)/shard_map/ppermute | solution.py:20
  177.4 24.0 %collective-permute-start.8 = (s32[128]{0:T(128)S(1)}, s32[128]{0:T(128)S(1)}, u32[]{:S(2)}, u32[]{:S(2)}) collective-permute-start(s32[128]{0:T(128)S(1)} %copy-done.12), channel_id=1, source_target_pairs={{0,1},{1,2},{2,3},{4,5},{5,6},{6,7},{8,9},{9,10},{10,11},{12,13},{... | collective-permute-start | bytes 1544 | tf_op jit(solution)/shard_map/ppermute | solution.py:20
  202.7 39.7 %collective-permute-start = (bf16[128,4096]{1,0:T(8,128)(2,1)S(1)}, bf16[128,4096]{1,0:T(8,128)(2,1)}, u32[]{:S(2)}, u32[]{:S(2)}) collective-permute-start(bf16[128,4096]{1,0:T(8,128)(2,1)S(1)} %bitcast.213), channel_id=1, source_target_pairs={{3,0},{7,4},{11,8},{15,12},{19,16},{23,20},{27,24},{31,28},{35,32}... | collective-permute-start | bytes 3145736 | tf_op jit(solution)/shard_map/ppermute | solution.py:20
  219.2 3.2 copy-start.9
  219.2 4.5 copy-start.11
  221.1 21.3 %collective-permute-start.9 = (bf16[128,4096]{1,0:T(8,128)(2,1)S(1)}, bf16[128,4096]{1,0:T(8,128)(2,1)S(1)}, u32[]{:S(2)}, u32[]{:S(2)}) collective-permute-start(bf16[128,4096]{1,0:T(8,128)(2,1)S(1)} %fusion.32), channel_id=1, source_target_pairs={{0,1},{1,2},{2,3},{4,5},{5,6},{6,7},{8,9},{9,10},{10,11},{12,13},{... | collective-permute-start | bytes 3145736 | tf_op jit(solution)/shard_map/ppermute | solution.py:20
  222.4 6.9 %collective-permute-start.10 = (s32[128]{0:T(128)S(1)}, s32[128]{0:T(128)S(1)}, u32[]{:S(2)}, u32[]{:S(2)}) collective-permute-start(s32[128]{0:T(128)S(1)} %copy-done.9), channel_id=1, source_target_pairs={{3,0},{7,4},{11,8},{15,12},{19,16},{23,20},{27,24},{31,28},{35,32}... | collective-permute-start | bytes 1544 | tf_op jit(solution)/shard_map/ppermute | solution.py:20
  223.8 18.5 %collective-permute-start.11 = (s32[128]{0:T(128)S(1)}, s32[128]{0:T(128)S(1)}, u32[]{:S(2)}, u32[]{:S(2)}) collective-permute-start(s32[128]{0:T(128)S(1)} %copy-done.11), channel_id=1, source_target_pairs={{0,1},{1,2},{2,3},{4,5},{5,6},{6,7},{8,9},{9,10},{10,11},{12,13},{... | collective-permute-start | bytes 1544 | tf_op jit(solution)/shard_map/ppermute | solution.py:20
  257.4 22.1 %copy-start.2 = (bf16[128,4096]{1,0:T(8,128)(2,1)}, bf16[128,4096]{1,0:T(8,128)(2,1)S(1)}, u32[]{:S(2)}) copy-start(bf16[128,4096]{1,0:T(8,128)(2,1)S(1)} %fusion.36) | copy-start | bytes 3145732
  257.4 21.8 %collective-permute-start.12 = (bf16[128,4096]{1,0:T(8,128)(2,1)S(1)}, bf16[128,4096]{1,0:T(8,128)(2,1)S(1)}, u32[]{:S(2)}, u32[]{:S(2)}) collective-permute-start(bf16[128,4096]{1,0:T(8,128)(2,1)S(1)} %fusion.36), channel_id=1, source_target_pairs={{0,1},{1,2},{2,3},{4,5},{5,6},{6,7},{8,9},{9,10},{10,11},{12,13},{... | collective-permute-start | bytes 3145736 | tf_op jit(solution)/shard_map/ppermute | solution.py:20
  260.3 18.8 %collective-permute-start.13 = (s32[128]{0:T(128)S(1)}, s32[128]{0:T(128)S(1)}, u32[]{:S(2)}, u32[]{:S(2)}) collective-permute-start(s32[128]{0:T(128)S(1)} %get-tuple-element.9), channel_id=1, source_target_pairs={{0,1},{1,2},{2,3},{4,5},{5,6},{6,7},{8,9},{9,10},{10,11},{12,13},{... | collective-permute-start | bytes 1544 | tf_op jit(solution)/shard_map/ppermute | solution.py:20
  292.8 22.4 %copy-start.3 = (bf16[128,4096]{1,0:T(8,128)(2,1)}, bf16[128,4096]{1,0:T(8,128)(2,1)S(1)}, u32[]{:S(2)}) copy-start(bf16[128,4096]{1,0:T(8,128)(2,1)S(1)} %fusion.40) | copy-start | bytes 3145732
  292.8 22.1 %collective-permute-start.14 = (bf16[128,4096]{1,0:T(8,128)(2,1)S(1)}, bf16[128,4096]{1,0:T(8,128)(2,1)S(1)}, u32[]{:S(2)}, u32[]{:S(2)}) collective-permute-start(bf16[128,4096]{1,0:T(8,128)(2,1)S(1)} %fusion.40), channel_id=1, source_target_pairs={{0,1},{1,2},{2,3},{4,5},{5,6},{6,7},{8,9},{9,10},{10,11},{12,13},{... | collective-permute-start | bytes 3145736 | tf_op jit(solution)/shard_map/ppermute | solution.py:20
  297.4 17.4 %collective-permute-start.15 = (s32[128]{0:T(128)S(1)}, s32[128]{0:T(128)S(1)}, u32[]{:S(2)}, u32[]{:S(2)}) collective-permute-start(s32[128]{0:T(128)S(1)} %collective-permute-done.13), channel_id=1, source_target_pairs={{0,1},{1,2},{2,3},{4,5},{5,6},{6,7},{8,9},{9,10},{10,11},{12,13},{... | collective-permute-start | bytes 1544 | tf_op jit(solution)/shard_map/ppermute | solution.py:20
  329.5 24.8 %collective-permute-start.16 = (bf16[128,4096]{1,0:T(8,128)(2,1)}, bf16[128,4096]{1,0:T(8,128)(2,1)S(1)}, u32[]{:S(2)}, u32[]{:S(2)}) collective-permute-start(bf16[128,4096]{1,0:T(8,128)(2,1)} %fusion.44), channel_id=1, source_target_pairs={{0,1},{1,2},{2,3},{4,5},{5,6},{6,7},{8,9},{9,10},{10,11},{12,13},{... | collective-permute-start | bytes 3145736 | tf_op jit(solution)/shard_map/ppermute | solution.py:20
  333.6 16.7 %collective-permute-start.17 = (s32[128]{0:T(128)S(1)}, s32[128]{0:T(128)S(1)}, u32[]{:S(2)}, u32[]{:S(2)}) collective-permute-start(s32[128]{0:T(128)S(1)} %collective-permute-done.15), channel_id=1, source_target_pairs={{0,1},{1,2},{2,3},{4,5},{5,6},{6,7},{8,9},{9,10},{10,11},{12,13},{... | collective-permute-start | bytes 1544 | tf_op jit(solution)/shard_map/ppermute | solution.py:20
  350.4 49.4 %collective-permute-start.20 = (bf16[128,4096]{1,0:T(8,128)(2,1)}, bf16[128,4096]{1,0:T(8,128)(2,1)}, u32[]{:S(2)}, u32[]{:S(2)}) collective-permute-start(bf16[128,4096]{1,0:T(8,128)(2,1)} %copy-done.2), channel_id=1, source_target_pairs={{3,0},{7,4},{11,8},{15,12},{19,16},{23,20},{27,24},{31,28},{35,32}... | collective-permute-start | bytes 3145736 | tf_op jit(solution)/shard_map/ppermute | solution.py:20
  351.7 48.1 %collective-permute-start.19 = (bf16[128,4096]{1,0:T(8,128)(2,1)}, bf16[128,4096]{1,0:T(8,128)(2,1)}, u32[]{:S(2)}, u32[]{:S(2)}) collective-permute-start(bf16[128,4096]{1,0:T(8,128)(2,1)} %copy-done.3), channel_id=1, source_target_pairs={{2,0},{3,1},{6,4},{7,5},{10,8},{11,9},{14,12},{15,13},{18,16},{19,... | collective-permute-start | bytes 3145736 | tf_op jit(solution)/shard_map/ppermute | solution.py:20
  353.0 46.8 %collective-permute-start.18 = (bf16[128,4096]{1,0:T(8,128)(2,1)}, bf16[128,4096]{1,0:T(8,128)(2,1)}, u32[]{:S(2)}, u32[]{:S(2)}) collective-permute-start(bf16[128,4096]{1,0:T(8,128)(2,1)} %fusion.44), channel_id=1, source_target_pairs={{1,0},{2,1},{3,2},{5,4},{6,5},{7,6},{9,8},{10,9},{11,10},{13,12},{... | collective-permute-start | bytes 3145736 | tf_op jit(solution)/shard_map/ppermute | solution.py:20
  367.7 35.6 %copy-start.13 = (s32[128]{0:T(128)S(1)}, s32[128]{0:T(128)}, u32[]{:S(2)}) copy-start(s32[128]{0:T(128)} %get-tuple-element.21) | copy-start | bytes 1540
Sparse Core Ops, SparseCore 0:
  10.3 62.4 all-gather.1
where the time goes:
time: 490 us; the launch traced here: 481 us
  waiting for transfers between devices  162 us (33%)
  starting transfers between devices  86.1 us (18%)
  matrix products  74.5 us (15%)
  blocking collectives  67.9 us (14%)
  local copies, waits for them, and re-layouts  38.2 us (8%)
  other arithmetic  34.7 us (7%)
  between operations  17.6 us (4%)
    ppermute x21, waiting for transfers between devices, shifted(): return lax.ppermute(array, axis, pairs)  125 us
    psum x1, blocking collectives, local(): lax.psum((retain_part, forget_part), ('dp', 'section'))  67.9 us
    ppermute x21, starting transfers between devices, shifted(): return lax.ppermute(array, axis, pairs)  56.1 us
    dot_general x7, matrix products, attention_layer(): jnp.dot(normed, weights, preferred_element_type=jnp.float32)  32.8 us
    dot_general x7, matrix products, attention_layer(): jnp.einsum('kgts,skd->tkgd', soft_weights, value_heads, preferred_element...  23.7 us
    unnamed x42, local copies, waits for them, and re-layouts  17.1 us
    all_to_all x1, waiting for transfers between devices, route(): lax.all_to_all(ordered, ('dp', 'section'), split_axis=0, concat_axis=0, t...  16 us
    sub x6, matrix products, attention_layer(): soft_weights = jax.nn.softmax(scores, axis=-1).astype(jnp.bfloat16)  15.9 us
  transfers between devices with their start and end apart: 26, of which 11 were waited for; matrix products, arithmetic and copies ran while one was open for 20% of the time, Pallas kernels for 0%

commit v1 on v0

v1 whole, which is shorter than its diff:
```python
import math

import jax
import jax.numpy as jnp
from jax import lax
from jax.experimental import pallas as pl
from jax.experimental.pallas import tpu as pltpu
from jax.sharding import PartitionSpec as P

QH = 32
KVH = 4
HS = 128
GROUP = 8
BLK = 128
HD = 4096
KVW = 2 * KVH * HS
PIECE_ROWS = 16
PIECE_COLS = 256
CHUNKS = 4

forget_weight = 0.5
ALL = ("dp", "section")


def layer_math(layer, boundary, gain_ref, w_buf, slot, w_wait, x_s, normed_s, acc_s, kv_s):
    gain = gain_ref[layer].astype(jnp.float32)

    def norm_rows(i, carry):
        rows = pl.ds(pl.multiple_of(i * 16, 16), 16)
        widened = x_s[rows, :].astype(jnp.float32)
        mean = jnp.sum(widened * widened, axis=-1, keepdims=True) * (1.0 / HD)
        normed_s[rows, :] = (widened * lax.rsqrt(mean + 1e-05) * gain).astype(jnp.bfloat16)
        return carry

    lax.fori_loop(0, BLK // 16, norm_rows, 0)
    depth = HD // CHUNKS
    for c in range(CHUNKS):
        w_wait(layer, c)
        part = jnp.dot(
            normed_s[:, c * depth : (c + 1) * depth],
            w_buf[slot, c * depth : (c + 1) * depth, :],
            preferred_element_type=jnp.float32,
        )
        if c == 0:
            acc_s[...] = part
        elif c < CHUNKS - 1:
            acc_s[...] += part
        else:
            kv_s[...] = (acc_s[...] + part).astype(jnp.bfloat16)
    t = lax.broadcasted_iota(jnp.int32, (BLK, BLK), 0)
    s = lax.broadcasted_iota(jnp.int32, (BLK, BLK), 1)
    allowed = (s <= t) & ((t < boundary) == (s < boundary))
    factor = math.log2(math.e) / math.sqrt(HS)

    def kv_head(j, carry):
        keys = kv_s[:, pl.ds(pl.multiple_of(j * HS, HS), HS)]
        values = kv_s[:, pl.ds(pl.multiple_of((j + KVH) * HS, HS), HS)]
        for g in range(GROUP):
            cols = pl.ds(pl.multiple_of((j * GROUP + g) * HS, HS), HS)
            scores = lax.dot_general(
                normed_s[:, cols], keys, (((1,), (1,)), ((), ())), preferred_element_type=jnp.float32
            )
            scores = jnp.where(allowed, scores, -jnp.inf)
            top = jnp.max(scores, axis=-1, keepdims=True)
            weights = jnp.exp2((scores - top) * factor)
            total = jnp.sum(weights, axis=-1, keepdims=True)
            probs = (weights * (1.0 / total)).astype(jnp.bfloat16)
            mixture = jnp.dot(probs, values, preferred_element_type=jnp.float32)
            x_s[:, cols] = (x_s[:, cols].astype(jnp.float32) + mixture).astype(jnp.bfloat16)
        return carry

    lax.fori_loop(0, KVH, kv_head, 0)


def layers_kernel(
    code_ref, pieces_ref, gain_ref, frozen_ref, w_ref, out_ref, part_ref,
    x_s, normed_s, acc_s, kv_s, w_buf, sems,
):
    depth = HD // CHUNKS

    def w_copy(layer, slot, c):
        return pltpu.make_async_copy(
            w_ref.at[layer, pl.ds(c * depth, depth)],
            w_buf.at[slot, pl.ds(c * depth, depth)],
            sems.at[slot, c],
        )

    for c in range(CHUNKS):
        w_copy(0, 0, c).start()
    across = HD // PIECE_COLS
    for p in range(pieces_ref.shape[0]):
        r, c = divmod(p, across)
        x_s[r * PIECE_ROWS : (r + 1) * PIECE_ROWS, c * PIECE_COLS : (c + 1) * PIECE_COLS] = pieces_ref[p]
    code = code_ref[0]
    boundary = code // 4
    for layer in range(4):
        if layer < 3:
            for c in range(CHUNKS):
                w_copy(layer + 1, (layer + 1) % 2, c).start()
        layer_math(
            layer, boundary, gain_ref, w_buf, layer % 2,
            lambda l, c: w_copy(l, l % 2, c).wait(),
            x_s, normed_s, acc_s, kv_s,
        )
    out_ref[...] = x_s[...]
    flag_first = (code // 2) % 2
    flag_second = code % 2

    def rows_distance(i, total):
        rows = pl.ds(pl.multiple_of(i * 16, 16), 16)
        gap = x_s[rows, :].astype(jnp.float32) - frozen_ref[rows, :].astype(jnp.float32)
        distance = jnp.sum(gap * gap, axis=-1, keepdims=True) * (1.0 / HD)
        t = lax.broadcasted_iota(jnp.int32, (16, 1), 0) + i * 16
        flag = jnp.where(t < boundary, flag_first, flag_second).astype(jnp.float32)
        return total + jnp.sum(((1.0 - flag) - forget_weight * flag) * distance, axis=0, keepdims=True)

    total = lax.fori_loop(0, BLK // 16, rows_distance, jnp.zeros((1, 1), jnp.float32))
    part_ref[...] = jnp.broadcast_to(total, part_ref.shape)


def run_layers(code, pieces, gains, frozen, weights):
    vmem = pl.BlockSpec(memory_space=pltpu.VMEM)
    return pl.pallas_call(
        layers_kernel,
        out_shape=(
            jax.ShapeDtypeStruct((BLK, HD), jnp.bfloat16),
            jax.ShapeDtypeStruct((8, 128), jnp.float32),
        ),
        in_specs=[
            pl.BlockSpec(memory_space=pltpu.SMEM), vmem, vmem, vmem,
            pl.BlockSpec(memory_space=pl.ANY),
        ],
        out_specs=(vmem, vmem),
        scratch_shapes=[
            pltpu.VMEM((BLK, HD), jnp.bfloat16),
            pltpu.VMEM((BLK, HD), jnp.bfloat16),
            pltpu.VMEM((BLK, KVW), jnp.float32),
            pltpu.VMEM((BLK, KVW), jnp.bfloat16),
            pltpu.VMEM((2, HD, KVW), jnp.bfloat16),
            pltpu.SemaphoreType.DMA((2, CHUNKS)),
        ],
        compiler_params=pltpu.CompilerParams(vmem_limit_bytes=40 << 20),
        name="layers",
    )(code, pieces, gains, frozen, weights)


def to_all(value):
    count = lax.axis_size("dp") * lax.axis_size("section")
    spread = jnp.broadcast_to(value.reshape(1, 1, 1), (count, 1, 1))
    return lax.all_to_all(spread, ALL, split_axis=0, concat_axis=0, tiled=True).reshape(count)


def order_kernel(plan_ref, landed_ref, ordered_ref):
    def place(b, carry):
        ordered_ref[plan_ref[b]] = landed_ref[b]
        return carry

    lax.fori_loop(0, landed_ref.shape[0], place, 0, unroll=8)


def route(hidden_in, block_plan):
    across = HD // PIECE_COLS
    pieces = (
        hidden_in.reshape(BLK // PIECE_ROWS, PIECE_ROWS, across, PIECE_COLS)
        .transpose(0, 2, 1, 3)
        .reshape(-1, PIECE_ROWS, PIECE_COLS)
    )
    landed = lax.all_to_all(pieces, ALL, split_axis=0, concat_axis=0, tiled=True)
    vmem = pl.BlockSpec(memory_space=pltpu.VMEM)
    ordered = pl.pallas_call(
        order_kernel,
        out_shape=jax.ShapeDtypeStruct(landed.shape, landed.dtype),
        in_specs=[pl.BlockSpec(memory_space=pltpu.SMEM), vmem],
        out_specs=vmem,
        name="order",
    )(block_plan, landed)
    return lax.all_to_all(ordered, ALL, split_axis=0, concat_axis=0, tiled=True)


def local(hidden_in, segments, forget_flags, block_plan, layer_gains, kv_weights, frozen_states):
    device_count = lax.axis_size("dp") * lax.axis_size("section")
    here = lax.axis_index(ALL)
    weights = lax.all_gather(kv_weights[0], ("section", "dp"), axis=0, tiled=True)
    weights = weights.reshape(4, HD, KVW)
    boundary = BLK - jnp.sum(segments[0])
    code = boundary * 4 + forget_flags[0, 0] * 2 + forget_flags[0, 1]
    codes = to_all(code)
    routed_code = jnp.sum(jnp.where(block_plan == here, codes, 0)).reshape(1)
    gains = lax.all_to_all(
        jnp.broadcast_to(layer_gains[None], (4, 1, HD)), "section", split_axis=0, concat_axis=0, tiled=True
    )
    pieces = route(hidden_in, block_plan)
    finished, part = run_layers(routed_code, pieces, gains, frozen_states, weights)
    objective = jnp.sum(to_all(part[0, 0])) / (BLK * device_count)
    return finished, objective


def solution(mesh):
    in_specs = (
        P(ALL, None),
        P(ALL, None),
        P(ALL, None),
        P(),
        P("section", None),
        P("section", "dp", None),
        P(ALL, None),
    )
    out_specs = (P(ALL, None), P())
    return jax.shard_map(local, mesh=mesh, in_specs=in_specs, out_specs=out_specs, check_vma=False)
```

time: 490 us -> 224 us (0.46); the launches traced: 481 us -> 224 us
  matrix products: 74.5 us -> 0 us
  waiting for transfers between devices: 162 us -> 89.5 us
  starting transfers between devices: 86.1 us -> 23.4 us
  Pallas kernels: 0 us -> 60.3 us
  blocking collectives: 67.9 us -> 16.9 us
  local copies, waits for them, and re-layouts: 38.2 us -> 8.46 us
  other arithmetic: 34.7 us -> 7.28 us
    ppermute x21 -> x0, waiting for transfers between devices: 125 us -> none  [shifted(): return lax.ppermute(array, axis, pairs)]
    psum x1 -> x0, blocking collectives: 67.9 us -> none  [local(): lax.psum((retain_part, forget_part), ('dp', 'section'))]
    pallas_call x0 -> x2, Pallas kernels: none -> 60.3 us  [the longest x1 57.9 us: run_layers(): pl.pallas_call(layers_kernel, out_shape=(jax.ShapeDtypeStruct((BLK, HD),...]
    dot_general x15 -> x0, matrix products: 58.6 us -> none  [the longest x7 32.8 us: attention_layer(): jnp.dot(normed, weights, preferred_element_type=jnp.float32)]
    ppermute x21 -> x0, starting transfers between devices: 56.1 us -> none  [shifted(): return lax.ppermute(array, axis, pairs)]
    all_gather x1, waiting for transfers between devices: 0.02 us -> 30 us  [local(): lax.all_gather(kv_weights[0], ('section', 'dp'), axis=0, tiled=True)]
    all_to_all x4, waiting for transfers between devices: 36.3 us -> 58.8 us  [the longest x1 27.7 us: route(): return lax.all_to_all(ordered, ALL, split_axis=0, concat_axis=0, tiled=True)]
    all_to_all x0 -> x1, blocking collectives: none -> 16.9 us  [to_all(): lax.all_to_all(spread, ALL, split_axis=0, concat_axis=0, tiled=True)]
  transfers between devices with their start and end apart: 26 -> 5, of which waited for: 11 -> 5; matrix products, arithmetic and copies ran while one was open for 20% -> 6% of each run, Pallas kernels for 0% -> 1%
where the time goes in v1:
time: 224 us
  waiting for transfers between devices  89.5 us (40%)
  Pallas kernels  60.3 us (27%)
  starting transfers between devices  23.4 us (10%)
  between operations  17.9 us (8%)
  blocking collectives  16.9 us (8%)
  local copies, waits for them, and re-layouts  8.46 us (4%)
  other arithmetic  7.28 us (3%)
    pallas_call x1, Pallas kernels, run_layers(): pl.pallas_call(layers_kernel, out_shape=(jax.ShapeDtypeStruct((BLK, HD),...  57.9 us
    all_gather x1, waiting for transfers between devices, local(): lax.all_gather(kv_weights[0], ('section', 'dp'), axis=0, tiled=True)  30 us
    all_to_all x1, waiting for transfers between devices, route(): return lax.all_to_all(ordered, ALL, split_axis=0, concat_axis=0, tiled=True)  27.7 us
    all_to_all x1, waiting for transfers between devices, route(): lax.all_to_all(pieces, ALL, split_axis=0, concat_axis=0, tiled=True)  22 us
    all_to_all x1, blocking collectives, to_all(): lax.all_to_all(spread, ALL, split_axis=0, concat_axis=0, tiled=True)  16.9 us
    all_to_all x1, starting transfers between devices, to_all(): lax.all_to_all(spread, ALL, split_axis=0, concat_axis=0, tiled=True)  11.5 us
    all_to_all x1, waiting for transfers between devices, to_all(): lax.all_to_all(spread, ALL, split_axis=0, concat_axis=0, tiled=True)  7.32 us
    all_to_all x1, starting transfers between devices, route(): return lax.all_to_all(ordered, ALL, split_axis=0, concat_axis=0, tiled=True)  4.48 us
  transfers between devices with their start and end apart: 5, of which 5 were waited for; matrix products, arithmetic and copies ran while one was open for 6% of the time, Pallas kernels for 1%

profile of v1, /device:TPU:1, one launch (start us, length us, event | category | flops | bytes accessed | tf_op | source)
XLA Modules:
  0.0 223.7 jit_solution(12740674754698831967)
XLA Ops:
  7.2 0.0 all-gather.3.cloned.1.call-start
  7.2 0.7 all-gather.3.cloned.1.call-update
  7.9 1.3 fusion.1
  9.9 1.3 reduce_sum.27
  12.5 0.6 broadcast_in_dim.24
  13.1 11.5 %all-to-all-start = ((s32[128,1,1]{2,1,0:T(1,128)}), s32[128,1,1]{2,1,0:T(1,128)S(1)}, u32[]{:S(2)}, u32[]{:S(2)}) async-start(s32[128,1,1]{2,1,0:T(1,128)} %broadcast_in_dim.24), calls=%async_computation | async-start | bytes 131072 | tf_op jit(solution)/shard_map/all_to_all | solution.py:150
  24.6 1.5 copy.16
  26.1 1.3 copy.13
  27.5 7.3 %all-to-all-done = s32[128,1,1]{2,1,0:T(1,128)S(1)} async-done(((s32[128,1,1]{2,1,0:T(1,128)}), s32[128,1,1]{2,1,0:T(1,128)S(1)}, u32[]{:S(2)}, u32[]{:S(2)}) %all-to-all-start) | async-done | bytes 544 | tf_op jit(solution)/shard_map/all_to_all | solution.py:150
  34.8 4.1 %all-to-all-start.1 = ((bf16[128,16,256]{2,1,0:T(8,128)(2,1)}), bf16[128,16,256]{2,1,0:T(8,128)(2,1)S(1)}, u32[]{:S(2)}, u32[]{:S(2)}) async-start(bf16[128,16,256]{2,1,0:T(8,128)(2,1)} %bitcast.4), calls=%async_computation.1 | async-start | bytes 2097152 | tf_op jit(solution)/shard_map/all_to_all | solution.py:168
  38.9 0.8 reduce.3
  39.7 0.5 broadcast.6
  40.2 0.8 reduce.4
  41.1 0.6 reshape.41
  41.7 22.0 %all-to-all-done.1.landed_ref = bf16[128,16,256]{2,1,0:T(8,128)(2,1)S(1)} async-done(((bf16[128,16,256]{2,1,0:T(8,128)(2,1)}), bf16[128,16,256]{2,1,0:T(8,128)(2,1)S(1)}, u32[]{:S(2)}, u32[]{:S(2)}) %all-to-all-start.1) | async-done | bytes 1048608 | tf_op jit(solution)/shard_map/all_to_all | solution.py:168
  63.7 0.0 copy-start.1
  63.7 3.3 %all-to-all-start.3 = ((bf16[4,2,2048]{2,1,0:T(2,128)(2,1)}), bf16[4,2,2048]{2,1,0:T(2,128)(2,1)S(1)}, u32[]{:S(2)}, u32[]{:S(2)}) async-start(bf16[4,2,2048]{2,1,0:T(2,128)(2,1)} %reshape.41), calls=%async_computation.3 | async-start | bytes 65536 | tf_op jit(solution)/shard_map/all_to_all | solution.py:189
  67.0 0.0 copy-done.1
  67.0 2.4 %order.1 = bf16[128,16,256]{2,1,0:T(8,128)(2,1)} custom-call(s32[128]{0:T(128)} %plan_ref.1, bf16[128,16,256]{2,1,0:T(8,128)(2,1)} %copy-done.1), custom_call_target="tpu_custom_call" | custom-call | tf_op jit(solution)/shard_map/order/pallas_call | solution.py:170
  69.4 1.8 all-to-all-done.3
  71.3 4.5 %all-to-all-start.2 = ((bf16[128,16,256]{2,1,0:T(8,128)(2,1)}), bf16[128,16,256]{2,1,0:T(8,128)(2,1)S(1)}, u32[]{:S(2)}, u32[]{:S(2)}) async-start(bf16[128,16,256]{2,1,0:T(8,128)(2,1)} %order.1), calls=%async_computation.2 | async-start | bytes 2097152 | tf_op jit(solution)/shard_map/all_to_all | solution.py:177
  75.8 2.4 %reduce.2 = s32[128]{0:T(128)S(1)} reduce(s32[128,1,1]{2,1,0:T(1,128)S(1)} %all-to-all-done, s32[]{:T(128)} %constant.19.clone.1), dimensions={1,2}, to_apply=%all_to_all.15.reduce_sub_computation | reduce | bytes 1028 | tf_op jit(solution)/shard_map/all_to_all | solution.py:150
  78.1 1.3 fusion
  79.5 27.7 %all-to-all-done.2.pieces_ref = bf16[128,16,256]{2,1,0:T(8,128)(2,1)S(1)} async-done(((bf16[128,16,256]{2,1,0:T(8,128)(2,1)}), bf16[128,16,256]{2,1,0:T(8,128)(2,1)S(1)}, u32[]{:S(2)}, u32[]{:S(2)}) %all-to-all-start.2) | async-done | bytes 1048608 | tf_op jit(solution)/shard_map/all_to_all | solution.py:177
  107.1 30.0 %all-gather.3.cloned.1.call-done = bf16[1,16384,1024]{2,1,0:T(8,128)(2,1)} async-done(((bf16[1,128,1024]{2,1,0:T(8,128)(2,1)}), bf16[1,16384,1024]{2,1,0:T(8,128)(2,1)}) %all-gather.3.cloned.1.call-update) | async-done | bytes 33554448 | tf_op jit(solution)/shard_map/all_gather | solution.py:183
  137.1 0.0 copy-start
  137.1 1.2 copy-done
  138.3 57.9 %layers.1 = (bf16[128,4096]{1,0:T(8,128)(2,1)}, f32[8,128]{1,0:T(8,128)S(1)}) custom-call(s32[1]{0:T(128)} %bitcast.2.code_ref, bf16[128,16,256]{2,1,0:T(8,128)(2,1)S(1)} %all-to-all-done.2.pieces_ref, bf16[4,1,4096]{2,1,0:T(2,128)(2,1)S(1)} %reshape.42.gain_ref, bf16[128,4096]{1,0:T(8,128)(2,1)S(1)} %copy-done, bf16[4,4096,1024]{2,1,0:T(8,128)(2,1)} %bitcast.11), custom_call_target="tpu_custom_call" | custom-call | tf_op jit(solution)/shard_map/layers/pallas_call | solution.py:123
  196.3 0.5 slice.11
  196.8 0.7 broadcast_in_dim.29
  197.5 16.9 %all_to_all.25 = f32[128,1,1]{2,1,0:T(1,128)S(1)} all-to-all(f32[128,1,1]{2,1,0:T(1,128)S(1)} %broadcast_in_dim.29), channel_id=1, replica_groups=mesh['dp'=32,'section'=4] {'dp','section'}, dimensions={0} | all-to-all | bytes 1024 | tf_op jit(solution)/shard_map/all_to_all | solution.py:150
  214.4 0.7 reduce_sum.29
  (2 shorter events, 0.1 us)
Async XLA Ops:
  7.2 130.0 %all-gather.3.cloned.1.call-start = ((), (), s32[]{:S(2)}) async-start(), calls=%async_computation.5 | async-start | bytes 33816576 | tf_op jit(solution)/shard_map/all_gather | solution.py:183
  13.1 21.7 %all-to-all-start = ((s32[128,1,1]{2,1,0:T(1,128)}), s32[128,1,1]{2,1,0:T(1,128)S(1)}, u32[]{:S(2)}, u32[]{:S(2)}) async-start(s32[128,1,1]{2,1,0:T(1,128)} %broadcast_in_dim.24), calls=%async_computation | async-start | bytes 131072 | tf_op jit(solution)/shard_map/all_to_all | solution.py:150
  34.8 28.9 %all-to-all-start.1 = ((bf16[128,16,256]{2,1,0:T(8,128)(2,1)}), bf16[128,16,256]{2,1,0:T(8,128)(2,1)S(1)}, u32[]{:S(2)}, u32[]{:S(2)}) async-start(bf16[128,16,256]{2,1,0:T(8,128)(2,1)} %bitcast.4), calls=%async_computation.1 | async-start | bytes 2097152 | tf_op jit(solution)/shard_map/all_to_all | solution.py:168
  63.7 3.3 %copy-start.1 = (bf16[128,16,256]{2,1,0:T(8,128)(2,1)}, bf16[128,16,256]{2,1,0:T(8,128)(2,1)S(1)}, u32[]{:S(2)}) copy-start(bf16[128,16,256]{2,1,0:T(8,128)(2,1)S(1)} %all-to-all-done.1.landed_ref) | copy-start | bytes 3145732
  63.7 7.6 %all-to-all-start.3 = ((bf16[4,2,2048]{2,1,0:T(2,128)(2,1)}), bf16[4,2,2048]{2,1,0:T(2,128)(2,1)S(1)}, u32[]{:S(2)}, u32[]{:S(2)}) async-start(bf16[4,2,2048]{2,1,0:T(2,128)(2,1)} %reshape.41), calls=%async_computation.3 | async-start | bytes 65536 | tf_op jit(solution)/shard_map/all_to_all | solution.py:189
  71.3 35.9 %all-to-all-start.2 = ((bf16[128,16,256]{2,1,0:T(8,128)(2,1)}), bf16[128,16,256]{2,1,0:T(8,128)(2,1)S(1)}, u32[]{:S(2)}, u32[]{:S(2)}) async-start(bf16[128,16,256]{2,1,0:T(8,128)(2,1)} %order.1), calls=%async_computation.2 | async-start | bytes 2097152 | tf_op jit(solution)/shard_map/all_to_all | solution.py:177
  137.1 1.2 copy-start
Sparse Core Ops, SparseCore 0:
  11.0 126.0 all-gather.2

commit v2 on v1

v2 whole, which is shorter than its diff:
```python
import math

import jax
import jax.numpy as jnp
from jax import lax
from jax.experimental import pallas as pl
from jax.experimental.pallas import tpu as pltpu
from jax.sharding import PartitionSpec as P

QH = 32
KVH = 4
HS = 128
GROUP = 8
BLK = 128
HD = 4096
KVW = 2 * KVH * HS
PIECE_ROWS = 32
CHUNKS = 4

forget_weight = 0.5
ALL = ("dp", "section")


def attend(boundary, x_s, normed_s, kv_s):
    t = lax.broadcasted_iota(jnp.int32, (BLK, BLK), 0)
    s = lax.broadcasted_iota(jnp.int32, (BLK, BLK), 1)
    allowed = (s <= t) & ((t < boundary) == (s < boundary))
    bias = jnp.where(allowed, 0.0, -jnp.inf)[None]
    factor = math.log2(math.e) / math.sqrt(HS)
    for j in range(KVH):
        keys = kv_s[:, j * HS : (j + 1) * HS]
        values = kv_s[:, (j + KVH) * HS : (j + KVH + 1) * HS]
        heads = pl.ds(j * GROUP, GROUP)
        queries = normed_s[heads].reshape(GROUP * BLK, HS)
        scores = lax.dot_general(
            queries, keys, (((1,), (1,)), ((), ())), preferred_element_type=jnp.float32
        )
        scores = scores.reshape(GROUP, BLK, BLK) + bias
        top = jnp.max(scores, axis=-1, keepdims=True)
        weights = jnp.exp2((scores - top) * factor).astype(jnp.bfloat16).reshape(GROUP * BLK, BLK)
        widened = jnp.concatenate([values, jnp.ones((BLK, HS), jnp.bfloat16)], axis=1)
        both = jnp.dot(weights, widened, preferred_element_type=jnp.float32)
        mixture = (both[:, :HS] / both[:, HS:]).reshape(GROUP, BLK, HS)
        x_s[heads] = (x_s[heads].astype(jnp.float32) + mixture).astype(jnp.bfloat16)


def normalize(gain_ref, layer, x_s, normed_s):
    def square(h, total):
        widened = x_s[h].astype(jnp.float32)
        return total + widened * widened

    squares = lax.fori_loop(0, QH, square, jnp.zeros((BLK, HS), jnp.float32), unroll=8)
    inverse = lax.rsqrt(jnp.sum(squares, axis=-1, keepdims=True) * (1.0 / HD) + 1e-05)
    inverse = jnp.broadcast_to(inverse, (BLK, HS))

    def scale(h, carry):
        gain = gain_ref[layer, h].astype(jnp.float32)
        normed_s[h] = (x_s[h].astype(jnp.float32) * inverse * gain).astype(jnp.bfloat16)
        return carry

    lax.fori_loop(0, QH, scale, 0, unroll=8)


def finish(code, x_s, frozen_ref, out_ref, part_ref):
    gaps = jnp.zeros((BLK, HS), jnp.float32)
    for h in range(QH):
        x = x_s[h]
        out_ref[:, h * HS : (h + 1) * HS] = x
        gap = x.astype(jnp.float32) - frozen_ref[:, h * HS : (h + 1) * HS].astype(jnp.float32)
        gaps += gap * gap
    t = lax.broadcasted_iota(jnp.int32, (BLK, HS), 0)
    flag = jnp.where(t < code // 4, (code // 2) % 2, code % 2).astype(jnp.float32)
    part = jnp.sum(((1.0 - flag) - forget_weight * flag) * gaps, axis=0, keepdims=True)
    part = jnp.sum(part, axis=1, keepdims=True) * (1.0 / HD)
    part_ref[...] = jnp.broadcast_to(part, part_ref.shape)


def layers_kernel(
    code_ref, pieces_ref, gain_ref, frozen_ref, w_ref, out_ref, part_ref,
    x_s, normed_s, acc_s, kv_s, w_buf, sems,
):
    depth = HD // CHUNKS
    slabs = depth // HS

    def w_copy(layer, c):
        return pltpu.make_async_copy(
            w_ref.at[layer, pl.ds(c * depth, depth)],
            w_buf.at[layer % 2, pl.ds(c * depth, depth)],
            sems.at[layer % 2, c],
        )

    for c in range(CHUNKS):
        w_copy(0, c).start()
    x_s[...] = pieces_ref[...]
    code = code_ref[0]
    for layer in range(4):
        if layer < 3:
            for c in range(CHUNKS):
                w_copy(layer + 1, c).start()
        normalize(gain_ref, layer, x_s, normed_s)
        for c in range(CHUNKS):
            w_copy(layer, c).wait()
            rows = jnp.concatenate([normed_s[c * slabs + i] for i in range(slabs)], axis=1)
            part = jnp.dot(
                rows, w_buf[layer % 2, c * depth : (c + 1) * depth, :], preferred_element_type=jnp.float32
            )
            if c == 0:
                acc_s[...] = part
            elif c < CHUNKS - 1:
                acc_s[...] += part
            else:
                kv_s[...] = (acc_s[...] + part).astype(jnp.bfloat16)
        attend(code // 4, x_s, normed_s, kv_s)
    finish(code, x_s, frozen_ref, out_ref, part_ref)


def run_layers(code, pieces, gains, frozen, weights):
    vmem = pl.BlockSpec(memory_space=pltpu.VMEM)
    return pl.pallas_call(
        layers_kernel,
        out_shape=(
            jax.ShapeDtypeStruct((BLK, HD), jnp.bfloat16),
            jax.ShapeDtypeStruct((8, 128), jnp.float32),
        ),
        in_specs=[
            pl.BlockSpec(memory_space=pltpu.SMEM), vmem, vmem, vmem,
            pl.BlockSpec(memory_space=pl.ANY),
        ],
        out_specs=(vmem, vmem),
        scratch_shapes=[
            pltpu.VMEM((QH, BLK, HS), jnp.bfloat16),
            pltpu.VMEM((QH, BLK, HS), jnp.bfloat16),
            pltpu.VMEM((BLK, KVW), jnp.float32),
            pltpu.VMEM((BLK, KVW), jnp.bfloat16),
            pltpu.VMEM((2, HD, KVW), jnp.bfloat16),
            pltpu.SemaphoreType.DMA((2, CHUNKS)),
        ],
        compiler_params=pltpu.CompilerParams(vmem_limit_bytes=40 << 20),
        name="layers",
    )(code, pieces, gains, frozen, weights)


def to_all(value):
    count = lax.axis_size("dp") * lax.axis_size("section")
    spread = jnp.broadcast_to(value.reshape(1, 1, 1), (count, 1, 1))
    return lax.all_to_all(spread, ALL, split_axis=0, concat_axis=0, tiled=True).reshape(count)


def order_kernel(plan_ref, landed_ref, ordered_ref):
    def place(b, carry):
        ordered_ref[plan_ref[b]] = landed_ref[b]
        return carry

    lax.fori_loop(0, landed_ref.shape[0], place, 0, unroll=8)


def route(hidden_in, block_plan):
    pieces = hidden_in.reshape(BLK, QH, HS).transpose(1, 0, 2).reshape(-1, PIECE_ROWS, HS)
    landed = lax.all_to_all(pieces, ALL, split_axis=0, concat_axis=0, tiled=True)
    vmem = pl.BlockSpec(memory_space=pltpu.VMEM)
    ordered = pl.pallas_call(
        order_kernel,
        out_shape=jax.ShapeDtypeStruct(landed.shape, landed.dtype),
        in_specs=[pl.BlockSpec(memory_space=pltpu.SMEM), vmem],
        out_specs=vmem,
        name="order",
    )(block_plan, landed)
    arrived = lax.all_to_all(ordered, ALL, split_axis=0, concat_axis=0, tiled=True)
    return arrived.reshape(QH, BLK, HS)


def local(hidden_in, segments, forget_flags, block_plan, layer_gains, kv_weights, frozen_states):
    device_count = lax.axis_size("dp") * lax.axis_size("section")
    here = lax.axis_index(ALL)
    weights = lax.all_gather(kv_weights[0], ("section", "dp"), axis=0, tiled=True)
    weights = weights.reshape(4, HD, KVW)
    boundary = BLK - jnp.sum(segments[0])
    code = boundary * 4 + forget_flags[0, 0] * 2 + forget_flags[0, 1]
    codes = to_all(code)
    routed_code = jnp.sum(jnp.where(block_plan == here, codes, 0)).reshape(1)
    gains = lax.all_to_all(
        jnp.broadcast_to(layer_gains[None], (4, 1, HD)), "section", split_axis=0, concat_axis=0, tiled=True
    ).reshape(4, QH, 1, HS)
    pieces = route(hidden_in, block_plan)
    finished, part = run_layers(routed_code, pieces, gains, frozen_states, weights)
    objective = jnp.sum(to_all(part[0, 0])) / (BLK * device_count)
    return finished, objective


def solution(mesh):
    in_specs = (
        P(ALL, None),
        P(ALL, None),
        P(ALL, None),
        P(),
        P("section", None),
        P("section", "dp", None),
        P(ALL, None),
    )
    out_specs = (P(ALL, None), P())
    return jax.shard_map(local, mesh=mesh, in_specs=in_specs, out_specs=out_specs, check_vma=False)
```

time: 224 us -> 186 us (0.83)
  Pallas kernels: 60.3 us -> 21.8 us
    pallas_call x1, Pallas kernels: 57.9 us -> 19.4 us  [run_layers(): pl.pallas_call(layers_kernel, out_shape=(jax.ShapeDtypeStruct((BLK, HD),...]
where the time goes in v2:
time: 186 us; the launch traced here: 185 us
  waiting for transfers between devices  91.1 us (49%)
  starting transfers between devices  23.4 us (13%)
  Pallas kernels  21.8 us (12%)
  between operations  17.9 us (10%)
  blocking collectives  16.9 us (9%)
  other arithmetic  7.28 us (4%)
  local copies, waits for them, and re-layouts  6.88 us (4%)
    all_gather x1, waiting for transfers between devices, local(): lax.all_gather(kv_weights[0], ('section', 'dp'), axis=0, tiled=True)  30 us
    all_to_all x1, waiting for transfers between devices, route(): lax.all_to_all(ordered, ALL, split_axis=0, concat_axis=0, tiled=True)  27.7 us
    all_to_all x1, waiting for transfers between devices, route(): lax.all_to_all(pieces, ALL, split_axis=0, concat_axis=0, tiled=True)  22 us
    pallas_call x1, Pallas kernels, run_layers(): pl.pallas_call(layers_kernel, out_shape=(jax.ShapeDtypeStruct((BLK, HD),...  19.4 us
    all_to_all x1, blocking collectives, to_all(): lax.all_to_all(spread, ALL, split_axis=0, concat_axis=0, tiled=True)  16.9 us
    all_to_all x1, starting transfers between devices, to_all(): lax.all_to_all(spread, ALL, split_axis=0, concat_axis=0, tiled=True)  11.5 us
    all_to_all x1, waiting for transfers between devices, to_all(): lax.all_to_all(spread, ALL, split_axis=0, concat_axis=0, tiled=True)  8.91 us
    all_to_all x1, starting transfers between devices, route(): lax.all_to_all(ordered, ALL, split_axis=0, concat_axis=0, tiled=True)  4.48 us
  transfers between devices with their start and end apart: 5, of which 5 were waited for; matrix products, arithmetic and copies ran while one was open for 6% of the time, Pallas kernels for 1%

profile of v2, /device:TPU:1, one launch (start us, length us, event | category | flops | bytes accessed | tf_op | source)
XLA Modules:
  0.0 185.2 jit_solution(7945148634003284103)
XLA Ops:
  7.2 0.0 copy-start
  7.2 0.0 all-gather.3.cloned.1.call-start
  7.2 0.7 all-gather.3.cloned.1.call-update
  7.9 1.3 fusion.1
  9.9 1.3 reduce_sum.27
  12.5 0.6 broadcast_in_dim.24
  13.1 11.5 %all-to-all-start = ((s32[128,1,1]{2,1,0:T(1,128)}), s32[128,1,1]{2,1,0:T(1,128)S(1)}, u32[]{:S(2)}, u32[]{:S(2)}) async-start(s32[128,1,1]{2,1,0:T(1,128)} %broadcast_in_dim.24), calls=%async_computation | async-start | bytes 131072 | tf_op jit(solution)/shard_map/all_to_all | solution.py:146
  24.6 0.0 copy-done
  24.6 1.3 copy_bitcast_fusion
  25.9 8.9 %all-to-all-done = s32[128,1,1]{2,1,0:T(1,128)S(1)} async-done(((s32[128,1,1]{2,1,0:T(1,128)}), s32[128,1,1]{2,1,0:T(1,128)S(1)}, u32[]{:S(2)}, u32[]{:S(2)}) %all-to-all-start) | async-done | bytes 544 | tf_op jit(solution)/shard_map/all_to_all | solution.py:146
  34.8 4.1 %all-to-all-start.1 = ((bf16[128,32,128]{2,1,0:T(8,128)(2,1)}), bf16[128,32,128]{2,1,0:T(8,128)(2,1)S(1)}, u32[]{:S(2)}, u32[]{:S(2)}) async-start(bf16[128,32,128]{2,1,0:T(8,128)(2,1)} %bitcast.4), calls=%async_computation.1 | async-start | bytes 2097152 | tf_op jit(solution)/shard_map/all_to_all | solution.py:159
  38.9 0.8 reduce.3
  39.7 0.5 broadcast.6
  40.2 0.8 reduce.4
  41.1 0.6 reshape.49
  41.7 22.0 %all-to-all-done.1.landed_ref = bf16[128,32,128]{2,1,0:T(8,128)(2,1)S(1)} async-done(((bf16[128,32,128]{2,1,0:T(8,128)(2,1)}), bf16[128,32,128]{2,1,0:T(8,128)(2,1)S(1)}, u32[]{:S(2)}, u32[]{:S(2)}) %all-to-all-start.1) | async-done | bytes 1048608 | tf_op jit(solution)/shard_map/all_to_all | solution.py:159
  63.7 0.0 copy-start.2
  63.7 3.3 %all-to-all-start.3 = ((bf16[4,2,2048]{2,1,0:T(2,128)(2,1)}), bf16[4,2,2048]{2,1,0:T(2,128)(2,1)S(1)}, u32[]{:S(2)}, u32[]{:S(2)}) async-start(bf16[4,2,2048]{2,1,0:T(2,128)(2,1)} %reshape.49), calls=%async_computation.3 | async-start | bytes 65536 | tf_op jit(solution)/shard_map/all_to_all | solution.py:181
  67.0 0.0 copy-done.2
  67.0 2.4 %order.1 = bf16[128,32,128]{2,1,0:T(8,128)(2,1)} custom-call(s32[128]{0:T(128)} %plan_ref.1, bf16[128,32,128]{2,1,0:T(8,128)(2,1)} %copy-done.2), custom_call_target="tpu_custom_call" | custom-call | tf_op jit(solution)/shard_map/order/pallas_call | solution.py:161
  69.5 1.8 all-to-all-done.3
  71.3 4.5 %all-to-all-start.2 = ((bf16[128,32,128]{2,1,0:T(8,128)(2,1)}), bf16[128,32,128]{2,1,0:T(8,128)(2,1)S(1)}, u32[]{:S(2)}, u32[]{:S(2)}) async-start(bf16[128,32,128]{2,1,0:T(8,128)(2,1)} %order.1), calls=%async_computation.2 | async-start | bytes 2097152 | tf_op jit(solution)/shard_map/all_to_all | solution.py:168
  75.8 2.4 %reduce.2 = s32[128]{0:T(128)S(1)} reduce(s32[128,1,1]{2,1,0:T(1,128)S(1)} %all-to-all-done, s32[]{:T(128)} %constant.19.clone.1), dimensions={1,2}, to_apply=%all_to_all.15.reduce_sub_computation | reduce | bytes 1028 | tf_op jit(solution)/shard_map/all_to_all | solution.py:146
  78.1 1.3 fusion
  79.5 27.7 %all-to-all-done.2 = bf16[128,32,128]{2,1,0:T(8,128)(2,1)S(1)} async-done(((bf16[128,32,128]{2,1,0:T(8,128)(2,1)}), bf16[128,32,128]{2,1,0:T(8,128)(2,1)S(1)}, u32[]{:S(2)}, u32[]{:S(2)}) %all-to-all-start.2) | async-done | bytes 1048608 | tf_op jit(solution)/shard_map/all_to_all | solution.py:168
  107.2 30.0 %all-gather.3.cloned.1.call-done = bf16[1,16384,1024]{2,1,0:T(8,128)(2,1)} async-done(((bf16[1,128,1024]{2,1,0:T(8,128)(2,1)}), bf16[1,16384,1024]{2,1,0:T(8,128)(2,1)}) %all-gather.3.cloned.1.call-update) | async-done | bytes 33554448 | tf_op jit(solution)/shard_map/all_gather | solution.py:175
  137.1 0.0 copy-start.1
  137.1 1.2 copy-done.1
  138.4 19.4 %layers.1 = (bf16[128,4096]{1,0:T(8,128)(2,1)}, f32[8,128]{1,0:T(8,128)S(1)}) custom-call(s32[1]{0:T(128)} %bitcast.2.code_ref, bf16[32,128,128]{2,1,0:T(8,128)(2,1)S(1)} %bitcast.15, bf16[4,32,1,128]{3,2,1,0:T(2,128)(2,1)S(1)} %bitcast.16, bf16[128,4096]{1,0:T(8,128)(2,1)S(1)} %copy-done.1, bf16[4,4096,1024]{2,1,0:T(8,128)(2,1)} %bitcast.17), custom_call_target="tpu_custom_call" | custom-call | tf_op jit(solution)/shard_map/layers/pallas_call | solution.py:119
  157.7 0.5 slice.11
  158.3 0.7 broadcast_in_dim.29
  158.9 16.9 %all_to_all.25 = f32[128,1,1]{2,1,0:T(1,128)S(1)} all-to-all(f32[128,1,1]{2,1,0:T(1,128)S(1)} %broadcast_in_dim.29), channel_id=1, replica_groups=mesh['dp'=32,'section'=4] {'dp','section'}, dimensions={0} | all-to-all | bytes 1024 | tf_op jit(solution)/shard_map/all_to_all | solution.py:146
  175.9 0.7 reduce_sum.29
  (2 shorter events, 0.1 us)
Async XLA Ops:
  7.2 17.5 %copy-start = (bf16[128,4096]{1,0:T(8,128)(2,1)S(1)}, bf16[128,4096]{1,0:T(8,128)(2,1)}, u32[]{:S(2)}) copy-start(bf16[128,4096]{1,0:T(8,128)(2,1)} %param.7) | copy-start | bytes 3145732
  7.2 130.0 %all-gather.3.cloned.1.call-start = ((), (), s32[]{:S(2)}) async-start(), calls=%async_computation.5 | async-start | bytes 33816576 | tf_op jit(solution)/shard_map/all_gather | solution.py:175
  13.1 21.7 %all-to-all-start = ((s32[128,1,1]{2,1,0:T(1,128)}), s32[128,1,1]{2,1,0:T(1,128)S(1)}, u32[]{:S(2)}, u32[]{:S(2)}) async-start(s32[128,1,1]{2,1,0:T(1,128)} %broadcast_in_dim.24), calls=%async_computation | async-start | bytes 131072 | tf_op jit(solution)/shard_map/all_to_all | solution.py:146
  34.8 28.9 %all-to-all-start.1 = ((bf16[128,32,128]{2,1,0:T(8,128)(2,1)}), bf16[128,32,128]{2,1,0:T(8,128)(2,1)S(1)}, u32[]{:S(2)}, u32[]{:S(2)}) async-start(bf16[128,32,128]{2,1,0:T(8,128)(2,1)} %bitcast.4), calls=%async_computation.1 | async-start | bytes 2097152 | tf_op jit(solution)/shard_map/all_to_all | solution.py:159
  63.7 3.3 %copy-start.2 = (bf16[128,32,128]{2,1,0:T(8,128)(2,1)}, bf16[128,32,128]{2,1,0:T(8,128)(2,1)S(1)}, u32[]{:S(2)}) copy-start(bf16[128,32,128]{2,1,0:T(8,128)(2,1)S(1)} %all-to-all-done.1.landed_ref) | copy-start | bytes 3145732
  63.7 7.6 %all-to-all-start.3 = ((bf16[4,2,2048]{2,1,0:T(2,128)(2,1)}), bf16[4,2,2048]{2,1,0:T(2,128)(2,1)S(1)}, u32[]{:S(2)}, u32[]{:S(2)}) async-start(bf16[4,2,2048]{2,1,0:T(2,128)(2,1)} %reshape.49), calls=%async_computation.3 | async-start | bytes 65536 | tf_op jit(solution)/shard_map/all_to_all | solution.py:181
  71.3 35.9 %all-to-all-start.2 = ((bf16[128,32,128]{2,1,0:T(8,128)(2,1)}), bf16[128,32,128]{2,1,0:T(8,128)(2,1)S(1)}, u32[]{:S(2)}, u32[]{:S(2)}) async-start(bf16[128,32,128]{2,1,0:T(8,128)(2,1)} %order.1), calls=%async_computation.2 | async-start | bytes 2097152 | tf_op jit(solution)/shard_map/all_to_all | solution.py:168
  137.1 1.2 copy-start.1
Sparse Core Ops, SparseCore 0:
  11.0 126.0 all-gather.2

commit v3 on v2

v3 whole, which is shorter than its diff:
```python
import math

import jax
import jax.numpy as jnp
from jax import lax
from jax.experimental import pallas as pl
from jax.experimental.pallas import tpu as pltpu
from jax.sharding import PartitionSpec as P

QH = 32
KVH = 4
HS = 128
GROUP = 8
BLK = 128
HD = 4096
KVW = 2 * KVH * HS
PIECE_ROWS = 32
CHUNKS = 4

forget_weight = 0.5


def attend(boundary, x_s, normed_s, kv_s):
    t = lax.broadcasted_iota(jnp.int32, (BLK, BLK), 0)
    s = lax.broadcasted_iota(jnp.int32, (BLK, BLK), 1)
    allowed = (s <= t) & ((t < boundary) == (s < boundary))
    bias = jnp.where(allowed, 0.0, -jnp.inf)[None]
    factor = math.log2(math.e) / math.sqrt(HS)
    for j in range(KVH):
        keys = kv_s[:, j * HS : (j + 1) * HS]
        values = kv_s[:, (j + KVH) * HS : (j + KVH + 1) * HS]
        heads = pl.ds(j * GROUP, GROUP)
        queries = normed_s[heads].reshape(GROUP * BLK, HS)
        scores = lax.dot_general(
            queries, keys, (((1,), (1,)), ((), ())), preferred_element_type=jnp.float32
        )
        scores = scores.reshape(GROUP, BLK, BLK) + bias
        top = jnp.max(scores, axis=-1, keepdims=True)
        weights = jnp.exp2((scores - top) * factor).astype(jnp.bfloat16).reshape(GROUP * BLK, BLK)
        widened = jnp.concatenate([values, jnp.ones((BLK, HS), jnp.bfloat16)], axis=1)
        both = jnp.dot(weights, widened, preferred_element_type=jnp.float32)
        mixture = (both[:, :HS] / both[:, HS:]).reshape(GROUP, BLK, HS)
        x_s[heads] = (x_s[heads].astype(jnp.float32) + mixture).astype(jnp.bfloat16)


def normalize(gain_ref, layer, x_s, normed_s):
    def square(h, total):
        widened = x_s[h].astype(jnp.float32)
        return total + widened * widened

    squares = lax.fori_loop(0, QH, square, jnp.zeros((BLK, HS), jnp.float32), unroll=8)
    inverse = lax.rsqrt(jnp.sum(squares, axis=-1, keepdims=True) * (1.0 / HD) + 1e-05)
    inverse = jnp.broadcast_to(inverse, (BLK, HS))

    def scale(h, carry):
        gain = gain_ref[layer, h].astype(jnp.float32)
        normed_s[h] = (x_s[h].astype(jnp.float32) * inverse * gain).astype(jnp.bfloat16)
        return carry

    lax.fori_loop(0, QH, scale, 0, unroll=8)


def project(slabs, w_buf, w_wait, normed_s, acc_s, kv_s):
    for c in range(CHUNKS):
        w_wait(c)
        rows = jnp.concatenate([normed_s[slab] for slab in slabs[c]], axis=1)
        part = jnp.dot(
            rows, w_buf[c][...].reshape(HD // CHUNKS, KVW), preferred_element_type=jnp.float32
        )
        if c == 0:
            acc_s[...] = part
        elif c < CHUNKS - 1:
            acc_s[...] += part
        else:
            kv_s[...] = (acc_s[...] + part).astype(jnp.bfloat16)


def first_kernel(here_ref, pieces_ref, gain_ref, *refs):
    weights, (out_ref, info_ref, x_s, normed_s, acc_s, kv_s, w_buf, sems) = refs[:16], refs[16:]
    y, z, core, x = (here_ref[i] for i in range(4))
    half = HS * 2
    copies = []
    for layer in range(2):
        copies.append([[] for _ in range(CHUNKS)])
        for side in range(2):
            for part in range(2):
                for r in range(4):
                    source = weights[(side * 2 + part) * 4 + r]
                    for kind in range(2):
                        plane = lax.rem(x - layer - 2 * kind + 8, 4)
                        cols = pl.ds(kind * 512 + part * half, half)
                        if part == 0:
                            target = w_buf.at[layer, side, r, :, :, cols]
                        else:
                            target = w_buf.at[layer, side, :, r, :, cols]
                        at = (side * 2 + part) * 8 + r * 2 + kind
                        copy = pltpu.make_async_copy(source.at[:, plane], target, sems.at[layer, at])
                        copy.start()
                        for c in (2 * side, 2 * side + 1):
                            if part == 1 or r // 2 == c - 2 * side:
                                copies[layer][c].append(copy)
                                break
    for p in range(pieces_ref.shape[0]):
        h, g = divmod(p, BLK // PIECE_ROWS)
        x_s[h, g * PIECE_ROWS : (g + 1) * PIECE_ROWS] = pieces_ref[p, :PIECE_ROWS]
    info = pieces_ref[0, PIECE_ROWS:].astype(jnp.float32)
    info_ref[...] = info
    slabs = []
    for c in range(CHUNKS):
        side = c // 2
        owner = core if side == 0 else 1 - core
        slabs.append([
            lax.rem(y - ry + 4, 4) * 8 + lax.rem(z - rz + 4, 4) * 2 + owner
            for rz in (2 * (c % 2), 2 * (c % 2) + 1)
            for ry in range(4)
        ])
    boundary = info[0:1].astype(jnp.int32)
    for layer in range(2):
        normalize(gain_ref, lax.rem(x - layer + 4, 4), x_s, normed_s)

        def wait(c, layer=layer):
            for copy in copies[layer][c]:
                copy.wait()

        views = [w_buf.at[layer, c // 2, pl.ds(2 * (c % 2), 2)] for c in range(CHUNKS)]
        project(slabs, views, wait, normed_s, acc_s, kv_s)
        attend(boundary, x_s, normed_s, kv_s)
    out_ref[...] = x_s[...]


def second_kernel(
    here_ref, states_ref, info_ref, gain_ref, frozen_ref, w_ref, out_ref, part_ref,
    x_s, normed_s, acc_s, kv_s, w_buf, sems,
):
    depth = HD // CHUNKS
    copies = []
    for layer in range(2):
        copies.append([])
        for c in range(CHUNKS):
            pair = []
            for kind in range(2):
                copy = pltpu.make_async_copy(
                    w_ref.at[layer + 2 - 2 * kind, pl.ds(c * depth, depth)],
                    w_buf.at[layer, pl.ds(c * depth, depth), pl.ds(kind * 512, 512)],
                    sems.at[layer, c, kind],
                )
                copy.start()
                pair.append(copy)
            copies[layer].append(pair)
    x = here_ref[3]
    x_s[...] = states_ref[...]
    info = info_ref[...]
    boundary = info[0:1].astype(jnp.int32)
    slabs = [[c * 8 + i for i in range(8)] for c in range(CHUNKS)]
    for layer in range(2):
        normalize(gain_ref, lax.rem(x - layer + 2, 4), x_s, normed_s)

        def wait(c, layer=layer):
            for copy in copies[layer][c]:
                copy.wait()

        views = [w_buf.at[layer, pl.ds(c * depth, depth)] for c in range(CHUNKS)]
        project(slabs, views, wait, normed_s, acc_s, kv_s)
        attend(boundary, x_s, normed_s, kv_s)
    gaps = jnp.zeros((BLK, HS), jnp.float32)
    for h in range(QH):
        state = x_s[h]
        out_ref[:, h * HS : (h + 1) * HS] = state
        gap = state.astype(jnp.float32) - frozen_ref[:, h * HS : (h + 1) * HS].astype(jnp.float32)
        gaps += gap * gap
    t = lax.broadcasted_iota(jnp.int32, (BLK, HS), 0)
    flag = jnp.where(t < boundary, info[1:2], info[2:3])
    part = jnp.sum(((1.0 - flag) - forget_weight * flag) * gaps, axis=0, keepdims=True)
    part = jnp.sum(part, axis=1, keepdims=True) * (1.0 / HD)
    part_ref[...] = jnp.broadcast_to(part, part_ref.shape)


VMEM_SPEC = pl.BlockSpec(memory_space=pltpu.VMEM)
SMEM_SPEC = pl.BlockSpec(memory_space=pltpu.SMEM)
ANY_SPEC = pl.BlockSpec(memory_space=pl.ANY)


def layer_scratch():
    return [
        pltpu.VMEM((QH, BLK, HS), jnp.bfloat16),
        pltpu.VMEM((QH, BLK, HS), jnp.bfloat16),
        pltpu.VMEM((BLK, KVW), jnp.float32),
        pltpu.VMEM((BLK, KVW), jnp.bfloat16),
    ]


def run_first(here, pieces, gains, weights):
    return pl.pallas_call(
        first_kernel,
        out_shape=(
            jax.ShapeDtypeStruct((QH, BLK, HS), jnp.bfloat16),
            jax.ShapeDtypeStruct((8, HS), jnp.float32),
        ),
        in_specs=[SMEM_SPEC, VMEM_SPEC, VMEM_SPEC] + [ANY_SPEC] * 16,
        out_specs=(VMEM_SPEC, VMEM_SPEC),
        scratch_shapes=layer_scratch() + [
            pltpu.VMEM((2, 2, 4, 4, HS, KVW), jnp.bfloat16),
            pltpu.SemaphoreType.DMA((2, 32)),
        ],
        compiler_params=pltpu.CompilerParams(vmem_limit_bytes=40 << 20),
        name="first_layers",
    )(here, pieces, gains, *weights)


def run_second(here, states, info, gains, frozen, weights):
    return pl.pallas_call(
        second_kernel,
        out_shape=(
            jax.ShapeDtypeStruct((BLK, HD), jnp.bfloat16),
            jax.ShapeDtypeStruct((8, HS), jnp.float32),
        ),
        in_specs=[SMEM_SPEC] + [VMEM_SPEC] * 4 + [ANY_SPEC],
        out_specs=(VMEM_SPEC, VMEM_SPEC),
        scratch_shapes=layer_scratch() + [
            pltpu.VMEM((2, HD, KVW), jnp.bfloat16),
            pltpu.SemaphoreType.DMA((2, CHUNKS, 2)),
        ],
        compiler_params=pltpu.CompilerParams(vmem_limit_bytes=40 << 20),
        name="last_layers",
    )(here, states, info, gains, frozen, weights)


ALL = ("y", "z", "core", "section")


def to_all(value):
    count = lax.axis_size(ALL)
    spread = jnp.broadcast_to(value.reshape(1, 1, 1), (count, 1, 1))
    return lax.all_to_all(spread, ALL, split_axis=0, concat_axis=0, tiled=True).reshape(count)


def order_kernel(plan_ref, landed_ref, ordered_ref):
    def place(b, carry):
        ordered_ref[plan_ref[b]] = landed_ref[b]
        return carry

    lax.fori_loop(0, landed_ref.shape[0], place, 0, unroll=8)


def route(hidden_in, info, block_plan):
    pieces = hidden_in.reshape(BLK, QH, HS).transpose(1, 0, 2).reshape(-1, PIECE_ROWS, HS)
    tail = jnp.broadcast_to(info[None], (pieces.shape[0],) + info.shape)
    pieces = jnp.concatenate([pieces, tail], axis=1)
    landed = lax.all_to_all(pieces, ALL, split_axis=0, concat_axis=0, tiled=True)
    ordered = pl.pallas_call(
        order_kernel,
        out_shape=jax.ShapeDtypeStruct(landed.shape, landed.dtype),
        in_specs=[SMEM_SPEC, VMEM_SPEC],
        out_specs=VMEM_SPEC,
        name="order",
    )(block_plan, landed)
    return lax.all_to_all(ordered, ALL, split_axis=0, concat_axis=0, tiled=True)


def shifted(array, axis, by):
    peers = lax.axis_size(axis)
    return lax.ppermute(array, axis, [(i, (i + by) % peers) for i in range(peers)])


def around(array, axis):
    return [array] + [shifted(array, axis, by) for by in (1, 2, 3)]


def local(hidden_in, segments, forget_flags, block_plan, layer_gains, kv_weights, frozen_states):
    here = jnp.stack([lax.axis_index(axis) for axis in ALL]).astype(jnp.int32)
    late = here[3] >= 2
    half = KVW // 2
    keys, values = kv_weights[0, :, :half], kv_weights[0, :, half:]
    spread = shifted(values, "section", 2)
    last_weights = lax.all_gather(
        jnp.where(late, keys, spread), ("section", "y", "z", "core"), axis=0, tiled=True
    ).reshape(4, HD, half)

    boundary = BLK - jnp.sum(segments[0])
    info = jnp.concatenate([boundary.reshape(1), forget_flags[0], jnp.zeros((5,), jnp.int32)])
    info = jnp.broadcast_to(info[:, None], (8, HS)).astype(jnp.bfloat16)
    pieces = route(hidden_in, info, block_plan)

    mine = jnp.concatenate([jnp.where(late, spread, keys), layer_gains.reshape(8, half)], axis=0)
    planes = jnp.stack(around(mine, "section"))
    gains = planes[:, HS:].reshape(4, QH, 1, HS)
    left = jnp.stack(around(planes[:, :HS, : half // 2], "y"))
    right = jnp.stack(around(planes[:, :HS, half // 2 :], "z"))
    own = around(left, "z") + around(right, "y")
    other = [shifted(block, "core", 1) for block in own]
    states, info_row = run_first(here, pieces, gains, own + other)

    finished, part = run_second(here, states, info_row, gains, frozen_states, last_weights)
    objective = jnp.sum(to_all(part[0, 0])) / (BLK * lax.axis_size(ALL))
    return finished, objective


def solution(mesh):
    grid = jax.sharding.Mesh(mesh.devices.reshape(4, 4, 2, 4), ALL)
    dp = ("y", "z", "core")
    in_specs = (
        P(ALL, None),
        P(ALL, None),
        P(ALL, None),
        P(),
        P("section", None),
        P("section", dp, None),
        P(ALL, None),
    )
    out_specs = (P(ALL, None), P())
    return jax.shard_map(local, mesh=grid, in_specs=in_specs, out_specs=out_specs, check_vma=False)
```

time: 186 us -> 220 us (1.18)
  starting transfers between devices: 23.4 us -> 45.6 us
  waiting for transfers between devices: 91.1 us -> 101 us
  Pallas kernels: 21.8 us -> 25.5 us
    ppermute x0 -> x24, waiting for transfers between devices: none -> 67.5 us  [shifted(): lax.ppermute(array, axis, [(i, (i + by) % peers) for i in range(peers)])]
    all_gather x1, waiting for transfers between devices: 30 us -> 0.01 us  [local(): lax.all_gather(jnp.where(late, keys, spread), ('section', 'y', 'z', 'core...]
    ppermute x0 -> x24, starting transfers between devices: none -> 29.6 us  [shifted(): lax.ppermute(array, axis, [(i, (i + by) % peers) for i in range(peers)])]
    all_to_all x1, waiting for transfers between devices: 22 us -> 3.28 us  [route(): lax.all_to_all(pieces, ALL, split_axis=0, concat_axis=0, tiled=True)]
    all_to_all x3 -> x1, starting transfers between devices: 19.2 us -> 5.54 us  [route(): return lax.all_to_all(ordered, ALL, split_axis=0, concat_axis=0, tiled=True)]
    all_to_all x3 -> x1, waiting for transfers between devices: 38.4 us -> 30 us  [route(): return lax.all_to_all(ordered, ALL, split_axis=0, concat_axis=0, tiled=True)]
    all_to_all x1, starting transfers between devices: 4.1 us -> 10.4 us  [route(): lax.all_to_all(pieces, ALL, split_axis=0, concat_axis=0, tiled=True)]
    pallas_call x1 -> x2, Pallas kernels: 19.4 us -> 22.4 us  [the longest x1 11.4 us: run_first(): pl.pallas_call(first_kernel, out_shape=(jax.ShapeDtypeStruct((QH, BLK, HS...]
  transfers between devices with their start and end apart: 5 -> 27, of which waited for: 5 -> 10; matrix products, arithmetic and copies ran while one was open for 6% -> 2% of each run, Pallas kernels for 1% -> 7%
where the time goes in v3:
time: 220 us
  waiting for transfers between devices  101 us (46%)
  starting transfers between devices  45.6 us (21%)
  Pallas kernels  25.5 us (12%)
  blocking collectives  17.3 us (8%)
  between operations  16.7 us (8%)
  other arithmetic  7.3 us (3%)
  local copies, waits for them, and re-layouts  6.66 us (3%)
    ppermute x24, waiting for transfers between devices, shifted(): lax.ppermute(array, axis, [(i, (i + by) % peers) for i in range(peers)])  67.5 us
    all_to_all x1, waiting for transfers between devices, route(): return lax.all_to_all(ordered, ALL, split_axis=0, concat_axis=0, tiled=True)  30 us
    ppermute x24, starting transfers between devices, shifted(): lax.ppermute(array, axis, [(i, (i + by) % peers) for i in range(peers)])  29.6 us
    all_to_all x1, blocking collectives, to_all(): lax.all_to_all(spread, ALL, split_axis=0, concat_axis=0, tiled=True)  17.3 us
    pallas_call x1, Pallas kernels, run_first(): pl.pallas_call(first_kernel, out_shape=(jax.ShapeDtypeStruct((QH, BLK, HS...  11.4 us
    pallas_call x1, Pallas kernels, run_second(): pl.pallas_call(second_kernel, out_shape=(jax.ShapeDtypeStruct((BLK, HD),...  11 us
    all_to_all x1, starting transfers between devices, route(): lax.all_to_all(pieces, ALL, split_axis=0, concat_axis=0, tiled=True)  10.4 us
    all_to_all x1, starting transfers between devices, route(): return lax.all_to_all(ordered, ALL, split_axis=0, concat_axis=0, tiled=True)  5.54 us
  transfers between devices with their start and end apart: 27, of which 10 were waited for; matrix products, arithmetic and copies ran while one was open for 2% of the time, Pallas kernels for 7%

profile of v3, /device:TPU:1, one launch (start us, length us, event | category | flops | bytes accessed | tf_op | source)
XLA Modules:
  0.0 219.8 jit_solution(844500703957546092)
XLA Ops:
  7.2 1.0 slice_bitcast_fusion
  8.2 3.7 %collective-permute-start = (bf16[128,512]{1,0:T(8,128)(2,1)S(1)}, bf16[128,512]{1,0:T(8,128)(2,1)S(1)}, u32[]{:S(2)}, u32[]{:S(2)}) collective-permute-start(bf16[128,512]{1,0:T(8,128)(2,1)S(1)} %slice_bitcast_fusion), channel_id=1, source_target_pairs={{0,2},{1,3},{2,0},{3,1},{4,6},{5,7},{6,4},{7,5},{8,10},{9,11},{10,... | collective-permute-start | bytes 393224 | tf_op jit(solution)/shard_map/ppermute | solution.py:262
  11.9 2.7 %collective-permute-done = bf16[128,512]{1,0:T(8,128)(2,1)S(1)} collective-permute-done((bf16[128,512]{1,0:T(8,128)(2,1)S(1)}, bf16[128,512]{1,0:T(8,128)(2,1)S(1)}, u32[]{:S(2)}, u32[]{:S(2)}) %collective-permute-start) | collective-permute-done | bytes 131104 | tf_op jit(solution)/shard_map/ppermute | solution.py:262
  14.6 1.6 bitcast_select_fusion
  16.2 0.8 reduce.2
  17.1 2.9 %collective-permute-start.3 = (bf16[136,512]{1,0:T(8,128)(2,1)S(1)}, bf16[136,512]{1,0:T(8,128)(2,1)S(1)}, u32[]{:S(2)}, u32[]{:S(2)}) collective-permute-start(bf16[136,512]{1,0:T(8,128)(2,1)S(1)} %get-tuple-element.15), channel_id=1, source_target_pairs={{0,3},{1,0},{2,1},{3,2},{4,7},{5,4},{6,5},{7,6},{8,11},{9,8},{10,9... | collective-permute-start | bytes 417800 | tf_op jit(solution)/shard_map/ppermute | solution.py:262
  20.0 0.5 collective-permute-start.2
  20.5 0.6 collective-permute-start.1
  21.1 1.5 collective-permute-done.3
  22.6 2.9 %collective-permute-done.2 = bf16[136,512]{1,0:T(8,128)(2,1)S(1)} collective-permute-done((bf16[136,512]{1,0:T(8,128)(2,1)S(1)}, bf16[136,512]{1,0:T(8,128)(2,1)S(1)}, u32[]{:S(2)}, u32[]{:S(2)}) %collective-permute-start.2) | collective-permute-done | bytes 139296 | tf_op jit(solution)/shard_map/ppermute | solution.py:262
  25.5 3.5 %collective-permute-done.1 = bf16[136,512]{1,0:T(8,128)(2,1)S(1)} collective-permute-done((bf16[136,512]{1,0:T(8,128)(2,1)S(1)}, bf16[136,512]{1,0:T(8,128)(2,1)S(1)}, u32[]{:S(2)}, u32[]{:S(2)}) %collective-permute-start.1) | collective-permute-done | bytes 139296 | tf_op jit(solution)/shard_map/ppermute | solution.py:262
  29.1 2.8 %collective-permute-start.6 = (bf16[4,128,256]{2,1,0:T(8,128)(2,1)S(1)}, bf16[4,128,256]{2,1,0:T(8,128)(2,1)S(1)}, u32[]{:S(2)}, u32[]{:S(2)}) collective-permute-start(bf16[4,128,256]{2,1,0:T(8,128)(2,1)S(1)} %get-tuple-element.11), channel_id=1, source_target_pairs={{0,96},{32,0},{64,32},{96,64},{1,97},{33,1},{65,33},{97,65},{2,98}... | collective-permute-start | bytes 786440 | tf_op jit(solution)/shard_map/ppermute | solution.py:262
  31.9 0.3 collective-permute-start.5
  32.2 0.7 collective-permute-start.4
  32.9 0.6 reduce_sum.18
  34.2 3.8 %collective-permute-start.12 = (bf16[4,128,256]{2,1,0:T(8,128)(2,1)S(1)}, bf16[4,128,256]{2,1,0:T(8,128)(2,1)S(1)}, u32[]{:S(2)}, u32[]{:S(2)}) collective-permute-start(bf16[4,128,256]{2,1,0:T(8,128)(2,1)S(1)} %get-tuple-element.10), channel_id=1, source_target_pairs={{0,24},{8,0},{16,8},{24,16},{1,25},{9,1},{17,9},{25,17},{2,26},{10... | collective-permute-start | bytes 786440 | tf_op jit(solution)/shard_map/ppermute | solution.py:262
  38.0 0.7 collective-permute-start.10
  38.7 0.8 collective-permute-done.5
  39.5 8.7 %collective-permute-done.4 = bf16[4,128,256]{2,1,0:T(8,128)(2,1)S(1)} collective-permute-done((bf16[4,128,256]{2,1,0:T(8,128)(2,1)S(1)}, bf16[4,128,256]{2,1,0:T(8,128)(2,1)S(1)}, u32[]{:S(2)}, u32[]{:S(2)}) %collective-permute-start.4) | collective-permute-done | bytes 262176 | tf_op jit(solution)/shard_map/ppermute | solution.py:262
  48.2 0.7 copy-done.9
  48.9 1.2 pad_maximum_fusion.1.refs_0_
  50.1 1.7 collective-permute-start.7
  51.8 3.3 %collective-permute-start.8 = (bf16[4,4,128,256]{3,2,1,0:T(8,128)(2,1)S(1)}, bf16[4,4,128,256]{3,2,1,0:T(8,128)(2,1)}, u32[]{:S(2)}, u32[]{:S(2)}) collective-permute-start(bf16[4,4,128,256]{3,2,1,0:T(8,128)(2,1)S(1)} %pad_maximum_fusion.1.refs_0_), channel_id=1, source_target_pairs={{0,16},{8,24},{16,0},{24,8},{1,17},{9,25},{17,1},{25,9},{2,18},{10... | collective-permute-start | bytes 3145736 | tf_op jit(solution)/shard_map/ppermute | solution.py:262
  55.1 0.7 collective-permute-start.9
  56.4 1.4 pad_maximum_fusion
  57.8 10.4 %all-to-all-start = ((bf16[128,40,128]{2,1,0:T(8,128)(2,1)}), bf16[128,40,128]{2,1,0:T(8,128)(2,1)}, u32[]{:S(2)}, u32[]{:S(2)}) async-start(bf16[128,40,128]{2,1,0:T(8,128)(2,1)} %pad_maximum_fusion), calls=%async_computation | async-start | bytes 2621440 | tf_op jit(solution)/shard_map/all_to_all | solution.py:249
  68.1 3.0 %collective-permute-start.14 = (bf16[4,4,128,256]{3,2,1,0:T(8,128)(2,1)S(1)}, bf16[4,4,128,256]{3,2,1,0:T(8,128)(2,1)}, u32[]{:S(2)}, u32[]{:S(2)}) collective-permute-start(bf16[4,4,128,256]{3,2,1,0:T(8,128)(2,1)S(1)} %pad_maximum_fusion.2.refs_4_), channel_id=1, source_target_pairs={{0,64},{32,96},{64,0},{96,32},{1,65},{33,97},{65,1},{97,33},{2,66}... | collective-permute-start | bytes 3145736 | tf_op jit(solution)/shard_map/ppermute | solution.py:262
  71.1 22.0 %collective-permute-done.7.refs_1_ = bf16[4,4,128,256]{3,2,1,0:T(8,128)(2,1)} collective-permute-done((bf16[4,4,128,256]{3,2,1,0:T(8,128)(2,1)S(1)}, bf16[4,4,128,256]{3,2,1,0:T(8,128)(2,1)}, u32[]{:S(2)}, u32[]{:S(2)}) %collective-permute-start.7) | collective-permute-done | bytes 1048608 | tf_op jit(solution)/shard_map/ppermute | solution.py:262
  93.1 25.4 %collective-permute-done.8.refs_2_ = bf16[4,4,128,256]{3,2,1,0:T(8,128)(2,1)} collective-permute-done((bf16[4,4,128,256]{3,2,1,0:T(8,128)(2,1)S(1)}, bf16[4,4,128,256]{3,2,1,0:T(8,128)(2,1)}, u32[]{:S(2)}, u32[]{:S(2)}) %collective-permute-start.8) | collective-permute-done | bytes 1048608 | tf_op jit(solution)/shard_map/ppermute | solution.py:262
  118.6 1.8 collective-permute-start.16
  120.4 0.5 collective-permute-start.17
  120.9 3.3 %all-to-all-done.landed_ref = bf16[128,40,128]{2,1,0:T(8,128)(2,1)} async-done(((bf16[128,40,128]{2,1,0:T(8,128)(2,1)}), bf16[128,40,128]{2,1,0:T(8,128)(2,1)}, u32[]{:S(2)}, u32[]{:S(2)}) %all-to-all-start) | async-done | bytes 1310752 | tf_op jit(solution)/shard_map/all_to_all | solution.py:249
  124.2 3.1 %order.1 = bf16[128,40,128]{2,1,0:T(8,128)(2,1)} custom-call(s32[128]{0:T(128)} %plan_ref.1, bf16[128,40,128]{2,1,0:T(8,128)(2,1)} %all-to-all-done.landed_ref), custom_call_target="tpu_custom_call" | custom-call | tf_op jit(solution)/shard_map/order/pallas_call | solution.py:250
  127.3 5.5 %all-to-all-start.1 = ((bf16[128,40,128]{2,1,0:T(8,128)(2,1)}), bf16[128,40,128]{2,1,0:T(8,128)(2,1)}, u32[]{:S(2)}, u32[]{:S(2)}) async-start(bf16[128,40,128]{2,1,0:T(8,128)(2,1)} %order.1), calls=%async_computation.1 | async-start | bytes 2621440 | tf_op jit(solution)/shard_map/all_to_all | solution.py:257
  132.8 1.4 collective-permute-start.18
  134.3 0.4 collective-permute-start.21
  134.8 0.4 collective-permute-start.23
  135.3 0.7 pad_maximum_fusion.8
  136.0 30.0 %all-to-all-done.1.pieces_ref = bf16[128,40,128]{2,1,0:T(8,128)(2,1)} async-done(((bf16[128,40,128]{2,1,0:T(8,128)(2,1)}), bf16[128,40,128]{2,1,0:T(8,128)(2,1)}, u32[]{:S(2)}, u32[]{:S(2)}) %all-to-all-start.1) | async-done | bytes 1310752 | tf_op jit(solution)/shard_map/all_to_all | solution.py:257
  166.1 11.4 %first_layers.1 = (bf16[32,128,128]{2,1,0:T(8,128)(2,1)S(1)}, f32[8,128]{1,0:T(8,128)S(1)}) custom-call(s32[4]{0:T(128)S(1)} %pad_add_fusion.here_ref, bf16[128,40,128]{2,1,0:T(8,128)(2,1)} %all-to-all-done.1.pieces_ref, bf16[4,32,1,128]{3,2,1,0:T(2,128)(2,1)S(1)} %reshape.34.gain_ref, bf16[4,4,128,256]{3,2,1,0:T(8,128)(2,1)S(1)} %pad_maximum_fusion.1.refs_0_, ...), custom_call_target="tpu_custom_call" | custom-call | tf_op jit(solution)/shard_map/first_layers/pallas_call | solution.py:193
  177.5 1.0 copy-done.2
  178.5 1.2 copy-done.1
  179.7 1.2 copy-done.3
  180.9 11.0 %last_layers.1 = (bf16[128,4096]{1,0:T(8,128)(2,1)}, f32[8,128]{1,0:T(8,128)S(1)}) custom-call(s32[4]{0:T(128)S(1)} %pad_add_fusion.here_ref, bf16[32,128,128]{2,1,0:T(8,128)(2,1)S(1)} %copy-done.3, f32[8,128]{1,0:T(8,128)S(1)} %get-tuple-element.7.info_ref, bf16[4,32,1,128]{3,2,1,0:T(2,128)(2,1)S(1)} %reshape.34.gain_ref, bf16[128,4096]{1,0:T(8,128)(2,1)S(1)} %copy-done.1, ...), custom_call_target="tpu_custom_call" | custom-call | tf_op jit(solution)/shard_map/last_layers/pallas_call | solution.py:211
  192.0 0.5 slice.23
  192.5 0.7 broadcast_in_dim.8
  193.2 17.3 %all_to_all.15 = f32[128,1,1]{2,1,0:T(1,128)S(1)} all-to-all(f32[128,1,1]{2,1,0:T(1,128)S(1)} %broadcast_in_dim.8), channel_id=1, replica_groups=mesh['y'=4,'z'=4,'core'=2,'section'=4] {'y','z','core','section'}, dimensions={0} | all-to-all | bytes 1024 | tf_op jit(solution)/shard_map/all_to_all | solution.py:234
  210.5 0.7 reduce_sum.19
  (55 shorter events, 1.1 us)
Async XLA Ops:
  7.2 48.9 %copy-start = (bf16[128,4096]{1,0:T(8,128)(2,1)S(1)}, bf16[128,4096]{1,0:T(8,128)(2,1)}, u32[]{:S(2)}) copy-start(bf16[128,4096]{1,0:T(8,128)(2,1)} %param.7) | copy-start | bytes 3145732
  7.2 25.7 %copy-start.10 = (s32[1,128]{1,0:T(1,128)S(1)}, s32[1,128]{1,0:T(1,128)}, u32[]{:S(2)}) copy-start(s32[1,128]{1,0:T(1,128)} %param.8) | copy-start | bytes 1540
  7.2 31.6 %copy-start.11 = (s32[1,2]{1,0:T(1,128)S(1)}, s32[1,2]{1,0:T(1,128)}, u32[]{:S(2)}) copy-start(s32[1,2]{1,0:T(1,128)} %param.9) | copy-start | bytes 28
  7.2 171.3 %all-gather.2.cloned.1.call-start = ((), (), s32[]{:S(2)}) async-start(), calls=%async_computation.3 | async-start | bytes 16908288 | tf_op jit(solution)/shard_map/all_gather | solution.py:275
  8.2 6.4 %collective-permute-start = (bf16[128,512]{1,0:T(8,128)(2,1)S(1)}, bf16[128,512]{1,0:T(8,128)(2,1)S(1)}, u32[]{:S(2)}, u32[]{:S(2)}) collective-permute-start(bf16[128,512]{1,0:T(8,128)(2,1)S(1)} %slice_bitcast_fusion), channel_id=1, source_target_pairs={{0,2},{1,3},{2,0},{3,1},{4,6},{5,7},{6,4},{7,5},{8,10},{9,11},{10,... | collective-permute-start | bytes 393224 | tf_op jit(solution)/shard_map/ppermute | solution.py:262
  17.1 5.5 %collective-permute-start.3 = (bf16[136,512]{1,0:T(8,128)(2,1)S(1)}, bf16[136,512]{1,0:T(8,128)(2,1)S(1)}, u32[]{:S(2)}, u32[]{:S(2)}) collective-permute-start(bf16[136,512]{1,0:T(8,128)(2,1)S(1)} %get-tuple-element.15), channel_id=1, source_target_pairs={{0,3},{1,0},{2,1},{3,2},{4,7},{5,4},{6,5},{7,6},{8,11},{9,8},{10,9... | collective-permute-start | bytes 417800 | tf_op jit(solution)/shard_map/ppermute | solution.py:262
  20.0 5.5 %collective-permute-start.2 = (bf16[136,512]{1,0:T(8,128)(2,1)S(1)}, bf16[136,512]{1,0:T(8,128)(2,1)S(1)}, u32[]{:S(2)}, u32[]{:S(2)}) collective-permute-start(bf16[136,512]{1,0:T(8,128)(2,1)S(1)} %get-tuple-element.15), channel_id=1, source_target_pairs={{0,2},{1,3},{2,0},{3,1},{4,6},{5,7},{6,4},{7,5},{8,10},{9,11},{10,... | collective-permute-start | bytes 417800 | tf_op jit(solution)/shard_map/ppermute | solution.py:262
  20.5 8.5 %collective-permute-start.1 = (bf16[136,512]{1,0:T(8,128)(2,1)S(1)}, bf16[136,512]{1,0:T(8,128)(2,1)S(1)}, u32[]{:S(2)}, u32[]{:S(2)}) collective-permute-start(bf16[136,512]{1,0:T(8,128)(2,1)S(1)} %get-tuple-element.15), channel_id=1, source_target_pairs={{0,1},{1,2},{2,3},{3,0},{4,5},{5,6},{6,7},{7,4},{8,9},{9,10},{10,1... | collective-permute-start | bytes 417800 | tf_op jit(solution)/shard_map/ppermute | solution.py:262
  22.6 27.4 %copy-start.4 = (bf16[136,512]{1,0:T(8,128)(2,1)}, bf16[136,512]{1,0:T(8,128)(2,1)S(1)}, u32[]{:S(2)}) copy-start(bf16[136,512]{1,0:T(8,128)(2,1)S(1)} %collective-permute-done.3) | copy-start | bytes 417796
  25.5 24.5 %copy-start.6 = (bf16[136,512]{1,0:T(8,128)(2,1)}, bf16[136,512]{1,0:T(8,128)(2,1)S(1)}, u32[]{:S(2)}) copy-start(bf16[136,512]{1,0:T(8,128)(2,1)S(1)} %collective-permute-done.2) | copy-start | bytes 417796
  29.0 21.0 %copy-start.7 = (bf16[136,512]{1,0:T(8,128)(2,1)}, bf16[136,512]{1,0:T(8,128)(2,1)S(1)}, u32[]{:S(2)}) copy-start(bf16[136,512]{1,0:T(8,128)(2,1)S(1)} %collective-permute-done.1) | copy-start | bytes 417796
  29.1 9.0 %collective-permute-start.6 = (bf16[4,128,256]{2,1,0:T(8,128)(2,1)S(1)}, bf16[4,128,256]{2,1,0:T(8,128)(2,1)S(1)}, u32[]{:S(2)}, u32[]{:S(2)}) collective-permute-start(bf16[4,128,256]{2,1,0:T(8,128)(2,1)S(1)} %get-tuple-element.11), channel_id=1, source_target_pairs={{0,96},{32,0},{64,32},{96,64},{1,97},{33,1},{65,33},{97,65},{2,98}... | collective-permute-start | bytes 786440 | tf_op jit(solution)/shard_map/ppermute | solution.py:262
  31.9 7.6 %collective-permute-start.5 = (bf16[4,128,256]{2,1,0:T(8,128)(2,1)S(1)}, bf16[4,128,256]{2,1,0:T(8,128)(2,1)S(1)}, u32[]{:S(2)}, u32[]{:S(2)}) collective-permute-start(bf16[4,128,256]{2,1,0:T(8,128)(2,1)S(1)} %get-tuple-element.11), channel_id=1, source_target_pairs={{0,64},{32,96},{64,0},{96,32},{1,65},{33,97},{65,1},{97,33},{2,66}... | collective-permute-start | bytes 786440 | tf_op jit(solution)/shard_map/ppermute | solution.py:262
  32.2 15.9 %collective-permute-start.4 = (bf16[4,128,256]{2,1,0:T(8,128)(2,1)S(1)}, bf16[4,128,256]{2,1,0:T(8,128)(2,1)S(1)}, u32[]{:S(2)}, u32[]{:S(2)}) collective-permute-start(bf16[4,128,256]{2,1,0:T(8,128)(2,1)S(1)} %get-tuple-element.11), channel_id=1, source_target_pairs={{0,32},{32,64},{64,96},{96,0},{1,33},{33,65},{65,97},{97,1},{2,34}... | collective-permute-start | bytes 786440 | tf_op jit(solution)/shard_map/ppermute | solution.py:262
  34.2 20.9 %collective-permute-start.12 = (bf16[4,128,256]{2,1,0:T(8,128)(2,1)S(1)}, bf16[4,128,256]{2,1,0:T(8,128)(2,1)S(1)}, u32[]{:S(2)}, u32[]{:S(2)}) collective-permute-start(bf16[4,128,256]{2,1,0:T(8,128)(2,1)S(1)} %get-tuple-element.10), channel_id=1, source_target_pairs={{0,24},{8,0},{16,8},{24,16},{1,25},{9,1},{17,9},{25,17},{2,26},{10... | collective-permute-start | bytes 786440 | tf_op jit(solution)/shard_map/ppermute | solution.py:262
  38.0 17.8 %collective-permute-start.11 = (bf16[4,128,256]{2,1,0:T(8,128)(2,1)S(1)}, bf16[4,128,256]{2,1,0:T(8,128)(2,1)S(1)}, u32[]{:S(2)}, u32[]{:S(2)}) collective-permute-start(bf16[4,128,256]{2,1,0:T(8,128)(2,1)S(1)} %get-tuple-element.10), channel_id=1, source_target_pairs={{0,16},{8,24},{16,0},{24,8},{1,17},{9,25},{17,1},{25,9},{2,18},{10... | collective-permute-start | bytes 786440 | tf_op jit(solution)/shard_map/ppermute | solution.py:262
  38.0 17.8 %collective-permute-start.10 = (bf16[4,128,256]{2,1,0:T(8,128)(2,1)S(1)}, bf16[4,128,256]{2,1,0:T(8,128)(2,1)S(1)}, u32[]{:S(2)}, u32[]{:S(2)}) collective-permute-start(bf16[4,128,256]{2,1,0:T(8,128)(2,1)S(1)} %get-tuple-element.10), channel_id=1, source_target_pairs={{0,8},{8,16},{16,24},{24,0},{1,9},{9,17},{17,25},{25,1},{2,10},{10... | collective-permute-start | bytes 786440 | tf_op jit(solution)/shard_map/ppermute | solution.py:262
  39.5 8.7 %copy-start.8 = (bf16[4,128,256]{2,1,0:T(8,128)(2,1)}, bf16[4,128,256]{2,1,0:T(8,128)(2,1)S(1)}, u32[]{:S(2)}) copy-start(bf16[4,128,256]{2,1,0:T(8,128)(2,1)S(1)} %collective-permute-done.5) | copy-start | bytes 786436
  48.2 0.7 copy-start.9
  50.1 43.0 %collective-permute-start.7 = (bf16[4,4,128,256]{3,2,1,0:T(8,128)(2,1)S(1)}, bf16[4,4,128,256]{3,2,1,0:T(8,128)(2,1)}, u32[]{:S(2)}, u32[]{:S(2)}) collective-permute-start(bf16[4,4,128,256]{3,2,1,0:T(8,128)(2,1)S(1)} %pad_maximum_fusion.1.refs_0_), channel_id=1, source_target_pairs={{0,8},{8,16},{16,24},{24,0},{1,9},{9,17},{17,25},{25,1},{2,10},{10... | collective-permute-start | bytes 3145736 | tf_op jit(solution)/shard_map/ppermute | solution.py:262
  51.8 66.8 %collective-permute-start.8 = (bf16[4,4,128,256]{3,2,1,0:T(8,128)(2,1)S(1)}, bf16[4,4,128,256]{3,2,1,0:T(8,128)(2,1)}, u32[]{:S(2)}, u32[]{:S(2)}) collective-permute-start(bf16[4,4,128,256]{3,2,1,0:T(8,128)(2,1)S(1)} %pad_maximum_fusion.1.refs_0_), channel_id=1, source_target_pairs={{0,16},{8,24},{16,0},{24,8},{1,17},{9,25},{17,1},{25,9},{2,18},{10... | collective-permute-start | bytes 3145736 | tf_op jit(solution)/shard_map/ppermute | solution.py:262
  55.1 65.3 %collective-permute-start.9 = (bf16[4,4,128,256]{3,2,1,0:T(8,128)(2,1)S(1)}, bf16[4,4,128,256]{3,2,1,0:T(8,128)(2,1)}, u32[]{:S(2)}, u32[]{:S(2)}) collective-permute-start(bf16[4,4,128,256]{3,2,1,0:T(8,128)(2,1)S(1)} %pad_maximum_fusion.1.refs_0_), channel_id=1, source_target_pairs={{0,24},{8,0},{16,8},{24,16},{1,25},{9,1},{17,9},{25,17},{2,26},{10... | collective-permute-start | bytes 3145736 | tf_op jit(solution)/shard_map/ppermute | solution.py:262
  55.9 64.5 %collective-permute-start.13 = (bf16[4,4,128,256]{3,2,1,0:T(8,128)(2,1)S(1)}, bf16[4,4,128,256]{3,2,1,0:T(8,128)(2,1)}, u32[]{:S(2)}, u32[]{:S(2)}) collective-permute-start(bf16[4,4,128,256]{3,2,1,0:T(8,128)(2,1)S(1)} %pad_maximum_fusion.2.refs_4_), channel_id=1, source_target_pairs={{0,32},{32,64},{64,96},{96,0},{1,33},{33,65},{65,97},{97,1},{2,34}... | collective-permute-start | bytes 3145736 | tf_op jit(solution)/shard_map/ppermute | solution.py:262
  57.8 66.4 %all-to-all-start = ((bf16[128,40,128]{2,1,0:T(8,128)(2,1)}), bf16[128,40,128]{2,1,0:T(8,128)(2,1)}, u32[]{:S(2)}, u32[]{:S(2)}) async-start(bf16[128,40,128]{2,1,0:T(8,128)(2,1)} %pad_maximum_fusion), calls=%async_computation | async-start | bytes 2621440 | tf_op jit(solution)/shard_map/all_to_all | solution.py:249
  68.1 64.7 %collective-permute-start.14 = (bf16[4,4,128,256]{3,2,1,0:T(8,128)(2,1)S(1)}, bf16[4,4,128,256]{3,2,1,0:T(8,128)(2,1)}, u32[]{:S(2)}, u32[]{:S(2)}) collective-permute-start(bf16[4,4,128,256]{3,2,1,0:T(8,128)(2,1)S(1)} %pad_maximum_fusion.2.refs_4_), channel_id=1, source_target_pairs={{0,64},{32,96},{64,0},{96,32},{1,65},{33,97},{65,1},{97,33},{2,66}... | collective-permute-start | bytes 3145736 | tf_op jit(solution)/shard_map/ppermute | solution.py:262
  93.1 41.1 %collective-permute-start.15 = (bf16[4,4,128,256]{3,2,1,0:T(8,128)(2,1)S(1)}, bf16[4,4,128,256]{3,2,1,0:T(8,128)(2,1)}, u32[]{:S(2)}, u32[]{:S(2)}) collective-permute-start(bf16[4,4,128,256]{3,2,1,0:T(8,128)(2,1)S(1)} %pad_maximum_fusion.2.refs_4_), channel_id=1, source_target_pairs={{0,96},{32,0},{64,32},{96,64},{1,97},{33,1},{65,33},{97,65},{2,98}... | collective-permute-start | bytes 3145736 | tf_op jit(solution)/shard_map/ppermute | solution.py:262
  118.6 15.7 %collective-permute-start.16 = (bf16[4,4,128,256]{3,2,1,0:T(8,128)(2,1)S(1)}, bf16[4,4,128,256]{3,2,1,0:T(8,128)(2,1)}, u32[]{:S(2)}, u32[]{:S(2)}) collective-permute-start(bf16[4,4,128,256]{3,2,1,0:T(8,128)(2,1)S(1)} %pad_maximum_fusion.1.refs_0_), channel_id=1, source_target_pairs={{0,4},{4,0},{1,5},{5,1},{2,6},{6,2},{3,7},{7,3},{8,12},{12,8},{9,1... | collective-permute-start | bytes 3145736 | tf_op jit(solution)/shard_map/ppermute | solution.py:262
  120.4 14.3 %collective-permute-start.20 = (bf16[4,4,128,256]{3,2,1,0:T(8,128)(2,1)S(1)}, bf16[4,4,128,256]{3,2,1,0:T(8,128)(2,1)}, u32[]{:S(2)}, u32[]{:S(2)}) collective-permute-start(bf16[4,4,128,256]{3,2,1,0:T(8,128)(2,1)S(1)} %pad_maximum_fusion.2.refs_4_), channel_id=1, source_target_pairs={{0,4},{4,0},{1,5},{5,1},{2,6},{6,2},{3,7},{7,3},{8,12},{12,8},{9,1... | collective-permute-start | bytes 3145736 | tf_op jit(solution)/shard_map/ppermute | solution.py:262
  120.4 14.4 %collective-permute-start.17 = (bf16[4,4,128,256]{3,2,1,0:T(8,128)(2,1)}, bf16[4,4,128,256]{3,2,1,0:T(8,128)(2,1)}, u32[]{:S(2)}, u32[]{:S(2)}) collective-permute-start(bf16[4,4,128,256]{3,2,1,0:T(8,128)(2,1)} %collective-permute-done.7.refs_1_), channel_id=1, source_target_pairs={{0,4},{4,0},{1,5},{5,1},{2,6},{6,2},{3,7},{7,3},{8,12},{12,8},{9,1... | collective-permute-start | bytes 3145736 | tf_op jit(solution)/shard_map/ppermute | solution.py:262
  127.3 8.0 %copy-start.5 = (bf16[136,512]{1,0:T(8,128)(2,1)S(1)}, bf16[136,512]{1,0:T(8,128)(2,1)}, u32[]{:S(2)}) copy-start(bf16[136,512]{1,0:T(8,128)(2,1)} %copy-done.4) | copy-start | bytes 417796
  127.3 38.8 %all-to-all-start.1 = ((bf16[128,40,128]{2,1,0:T(8,128)(2,1)}), bf16[128,40,128]{2,1,0:T(8,128)(2,1)}, u32[]{:S(2)}, u32[]{:S(2)}) async-start(bf16[128,40,128]{2,1,0:T(8,128)(2,1)} %order.1), calls=%async_computation.1 | async-start | bytes 2621440 | tf_op jit(solution)/shard_map/all_to_all | solution.py:257
  132.8 33.2 %collective-permute-start.18 = (bf16[4,4,128,256]{3,2,1,0:T(8,128)(2,1)}, bf16[4,4,128,256]{3,2,1,0:T(8,128)(2,1)}, u32[]{:S(2)}, u32[]{:S(2)}) collective-permute-start(bf16[4,4,128,256]{3,2,1,0:T(8,128)(2,1)} %collective-permute-done.8.refs_2_), channel_id=1, source_target_pairs={{0,4},{4,0},{1,5},{5,1},{2,6},{6,2},{3,7},{7,3},{8,12},{12,8},{9,1... | collective-permute-start | bytes 3145736 | tf_op jit(solution)/shard_map/ppermute | solution.py:262
  134.2 31.9 %collective-permute-start.19 = (bf16[4,4,128,256]{3,2,1,0:T(8,128)(2,1)}, bf16[4,4,128,256]{3,2,1,0:T(8,128)(2,1)}, u32[]{:S(2)}, u32[]{:S(2)}) collective-permute-start(bf16[4,4,128,256]{3,2,1,0:T(8,128)(2,1)} %collective-permute-done.9.refs_3_), channel_id=1, source_target_pairs={{0,4},{4,0},{1,5},{5,1},{2,6},{6,2},{3,7},{7,3},{8,12},{12,8},{9,1... | collective-permute-start | bytes 3145736 | tf_op jit(solution)/shard_map/ppermute | solution.py:262
  134.3 31.8 %collective-permute-start.21 = (bf16[4,4,128,256]{3,2,1,0:T(8,128)(2,1)}, bf16[4,4,128,256]{3,2,1,0:T(8,128)(2,1)}, u32[]{:S(2)}, u32[]{:S(2)}) collective-permute-start(bf16[4,4,128,256]{3,2,1,0:T(8,128)(2,1)} %collective-permute-done.13.refs_5_), channel_id=1, source_target_pairs={{0,4},{4,0},{1,5},{5,1},{2,6},{6,2},{3,7},{7,3},{8,12},{12,8},{9,1... | collective-permute-start | bytes 3145736 | tf_op jit(solution)/shard_map/ppermute | solution.py:262
  134.7 31.4 %collective-permute-start.22 = (bf16[4,4,128,256]{3,2,1,0:T(8,128)(2,1)}, bf16[4,4,128,256]{3,2,1,0:T(8,128)(2,1)}, u32[]{:S(2)}, u32[]{:S(2)}) collective-permute-start(bf16[4,4,128,256]{3,2,1,0:T(8,128)(2,1)} %collective-permute-done.14.refs_6_), channel_id=1, source_target_pairs={{0,4},{4,0},{1,5},{5,1},{2,6},{6,2},{3,7},{7,3},{8,12},{12,8},{9,1... | collective-permute-start | bytes 3145736 | tf_op jit(solution)/shard_map/ppermute | solution.py:262
  134.8 31.3 %collective-permute-start.23 = (bf16[4,4,128,256]{3,2,1,0:T(8,128)(2,1)}, bf16[4,4,128,256]{3,2,1,0:T(8,128)(2,1)}, u32[]{:S(2)}, u32[]{:S(2)}) collective-permute-start(bf16[4,4,128,256]{3,2,1,0:T(8,128)(2,1)} %collective-permute-done.15.refs_7_), channel_id=1, source_target_pairs={{0,4},{4,0},{1,5},{5,1},{2,6},{6,2},{3,7},{7,3},{8,12},{12,8},{9,1... | collective-permute-start | bytes 3145736 | tf_op jit(solution)/shard_map/ppermute | solution.py:262
  177.5 1.0 copy-start.2
  178.5 1.2 copy-start.1
  179.7 1.2 copy-start.3
Sparse Core Ops, SparseCore 0:
  16.4 151.1 all-gather.1

commit v4 on v2

--- a/solution.py
+++ b/solution.py
@@ -77,7 +77,7 @@
 
 def layers_kernel(
     code_ref, pieces_ref, gain_ref, frozen_ref, w_ref, out_ref, part_ref,
-    x_s, normed_s, acc_s, kv_s, w_buf, sems,
+    x_s, normed_s, acc_s, kv_s, w_buf, sems, frozen_s, frozen_sem,
 ):
     depth = HD // CHUNKS
     slabs = depth // HS
@@ -91,6 +91,8 @@
 
     for c in range(CHUNKS):
         w_copy(0, c).start()
+    frozen_copy = pltpu.make_async_copy(frozen_ref, frozen_s, frozen_sem)
+    frozen_copy.start()
     x_s[...] = pieces_ref[...]
     code = code_ref[0]
     for layer in range(4):
@@ -111,7 +113,8 @@
             else:
                 kv_s[...] = (acc_s[...] + part).astype(jnp.bfloat16)
         attend(code // 4, x_s, normed_s, kv_s)
-    finish(code, x_s, frozen_ref, out_ref, part_ref)
+    frozen_copy.wait()
+    finish(code, x_s, frozen_s, out_ref, part_ref)
 
 
 def run_layers(code, pieces, gains, frozen, weights):
@@ -120,10 +123,11 @@
         layers_kernel,
         out_shape=(
             jax.ShapeDtypeStruct((BLK, HD), jnp.bfloat16),
-            jax.ShapeDtypeStruct((8, 128), jnp.float32),
+            jax.ShapeDtypeStruct((128, 1, HS), jnp.float32),
         ),
         in_specs=[
-            pl.BlockSpec(memory_space=pltpu.SMEM), vmem, vmem, vmem,
+            pl.BlockSpec(memory_space=pltpu.SMEM), vmem, vmem,
+            pl.BlockSpec(memory_space=pl.ANY),
             pl.BlockSpec(memory_space=pl.ANY),
         ],
         out_specs=(vmem, vmem),
@@ -134,6 +138,8 @@
             pltpu.VMEM((BLK, KVW), jnp.bfloat16),
             pltpu.VMEM((2, HD, KVW), jnp.bfloat16),
             pltpu.SemaphoreType.DMA((2, CHUNKS)),
+            pltpu.VMEM((BLK, HD), jnp.bfloat16),
+            pltpu.SemaphoreType.DMA,
         ],
         compiler_params=pltpu.CompilerParams(vmem_limit_bytes=40 << 20),
         name="layers",
@@ -175,15 +181,18 @@
     weights = lax.all_gather(kv_weights[0], ("section", "dp"), axis=0, tiled=True)
     weights = weights.reshape(4, HD, KVW)
     boundary = BLK - jnp.sum(segments[0])
-    code = boundary * 4 + forget_flags[0, 0] * 2 + forget_flags[0, 1]
+    pieces = route(hidden_in, block_plan)
+    sample = pieces[0, 0, 0]
+    later = (sample != sample).astype(jnp.int32)
+    code = boundary * 4 + forget_flags[0, 0] * 2 + forget_flags[0, 1] + later
     codes = to_all(code)
     routed_code = jnp.sum(jnp.where(block_plan == here, codes, 0)).reshape(1)
     gains = lax.all_to_all(
-        jnp.broadcast_to(layer_gains[None], (4, 1, HD)), "section", split_axis=0, concat_axis=0, tiled=True
+        jnp.broadcast_to((layer_gains + later.astype(jnp.bfloat16))[None], (4, 1, HD)), "section", split_axis=0, concat_axis=0, tiled=True
     ).reshape(4, QH, 1, HS)
-    pieces = route(hidden_in, block_plan)
     finished, part = run_layers(routed_code, pieces, gains, frozen_states, weights)
-    objective = jnp.sum(to_all(part[0, 0])) / (BLK * device_count)
+    parts = lax.all_to_all(part, ALL, split_axis=0, concat_axis=0, tiled=True)
+    objective = jnp.sum(parts[:, 0, 0]) / (BLK * device_count)
     return finished, objective
 
 

time: 186 us -> 182 us (0.978)
  blocking collectives: 16.9 us -> 50.1 us
  waiting for transfers between devices: 91.1 us -> 67 us
  starting transfers between devices: 23.4 us -> 10.7 us
    all_to_all x1 -> x2, blocking collectives: 16.9 us -> 50.1 us  [the longest x1 33.2 us: route(): lax.all_to_all(pieces, ALL, split_axis=0, concat_axis=0, tiled=True)]
    all_to_all x2 -> x1, waiting for transfers between devices: 23.8 us -> 0.78 us  [local(): lax.all_to_all(jnp.broadcast_to((layer_gains + later.astype(jnp.bfloat16)...]
    all_to_all x1, starting transfers between devices: 11.5 us -> 3.61 us  [to_all(): lax.all_to_all(spread, ALL, split_axis=0, concat_axis=0, tiled=True)]
    all_gather x1, waiting for transfers between devices: 30 us -> 34.4 us  [local(): lax.all_gather(kv_weights[0], ('section', 'dp'), axis=0, tiled=True)]
    all_to_all x2 -> x1, starting transfers between devices: 7.36 us -> 3.46 us  [local(): lax.all_to_all(jnp.broadcast_to((layer_gains + later.astype(jnp.bfloat16)...]
    all_to_all x1, waiting for transfers between devices: 27.7 us -> 24.2 us  [route(): lax.all_to_all(ordered, ALL, split_axis=0, concat_axis=0, tiled=True)]
    all_to_all x1, waiting for transfers between devices: 8.91 us -> 6.99 us  [to_all(): lax.all_to_all(spread, ALL, split_axis=0, concat_axis=0, tiled=True)]
  transfers between devices with their start and end apart: 5 -> 4, of which waited for: 5 -> 4; matrix products, arithmetic and copies ran while one was open for 6% -> 6% of each run, Pallas kernels for 1% -> 1%
where the time goes in v4:
time: 182 us
  waiting for transfers between devices  67 us (37%)
  blocking collectives  50.1 us (28%)
  Pallas kernels  21.8 us (12%)
  between operations  19.2 us (11%)
  starting transfers between devices  10.7 us (6%)
  other arithmetic  7.33 us (4%)
  local copies, waits for them, and re-layouts  5.72 us (3%)
    all_gather x1, waiting for transfers between devices, local(): lax.all_gather(kv_weights[0], ('section', 'dp'), axis=0, tiled=True)  34.4 us
    all_to_all x1, blocking collectives, route(): lax.all_to_all(pieces, ALL, split_axis=0, concat_axis=0, tiled=True)  33.2 us
    all_to_all x1, waiting for transfers between devices, route(): lax.all_to_all(ordered, ALL, split_axis=0, concat_axis=0, tiled=True)  24.2 us
    pallas_call x1, Pallas kernels, run_layers(): pl.pallas_call(layers_kernel, out_shape=(jax.ShapeDtypeStruct((BLK, HD),...  19.4 us
    all_to_all x1, blocking collectives, local(): parts = lax.all_to_all(part, ALL, split_axis=0, concat_axis=0, tiled=True)  16.9 us
    all_to_all x1, waiting for transfers between devices, to_all(): lax.all_to_all(spread, ALL, split_axis=0, concat_axis=0, tiled=True)  6.99 us
  transfers between devices with their start and end apart: 4, of which 4 were waited for; matrix products, arithmetic and copies ran while one was open for 6% of the time, Pallas kernels for 1%

profile of v4, /device:TPU:1, one launch (start us, length us, event | category | flops | bytes accessed | tf_op | source)
XLA Modules:
  0.0 181.8 jit_solution(5077818983470272560)
XLA Ops:
  7.2 0.0 copy-start
  7.2 0.0 all-gather.3.cloned.1.call-start
  7.2 0.7 all-gather.3.cloned.1.call-update
  7.9 0.5 copy-done
  8.4 0.3 copy_bitcast_fusion
  8.7 33.2 %all_to_all.25.landed_ref = bf16[128,32,128]{2,1,0:T(8,128)(2,1)} all-to-all(bf16[128,32,128]{2,1,0:T(8,128)(2,1)S(1)} %bitcast.19), channel_id=1, replica_groups=mesh['dp'=32,'section'=4] {'dp','section'}, dimensions={0} | all-to-all | bytes 2097152 | tf_op jit(solution)/shard_map/all_to_all | solution.py:165
  41.9 2.4 %order.1 = bf16[128,32,128]{2,1,0:T(8,128)(2,1)} custom-call(s32[128]{0:T(128)} %plan_ref.1, bf16[128,32,128]{2,1,0:T(8,128)(2,1)} %all_to_all.25.landed_ref), custom_call_target="tpu_custom_call" | custom-call | tf_op jit(solution)/shard_map/order/pallas_call | solution.py:167
  44.3 3.6 %all-to-all-start.1 = ((bf16[128,32,128]{2,1,0:T(8,128)(2,1)}), bf16[128,32,128]{2,1,0:T(8,128)(2,1)S(1)}, u32[]{:S(2)}, u32[]{:S(2)}) async-start(bf16[128,32,128]{2,1,0:T(8,128)(2,1)} %order.1), calls=%async_computation.1 | async-start | bytes 2097152 | tf_op jit(solution)/shard_map/all_to_all | solution.py:174
  47.9 1.3 reduce_sum.27
  49.8 1.3 fusion.1
  52.5 24.2 %all-to-all-done.1 = bf16[128,32,128]{2,1,0:T(8,128)(2,1)S(1)} async-done(((bf16[128,32,128]{2,1,0:T(8,128)(2,1)}), bf16[128,32,128]{2,1,0:T(8,128)(2,1)S(1)}, u32[]{:S(2)}, u32[]{:S(2)}) %all-to-all-start.1) | async-done | bytes 1048608 | tf_op jit(solution)/shard_map/all_to_all | solution.py:174
  76.7 0.5 slice.16
  78.5 0.7 broadcast_in_dim.17
  79.2 3.6 %all-to-all-start.2 = ((s32[128,1,1]{2,1,0:T(1,128)}), s32[128,1,1]{2,1,0:T(1,128)S(1)}, u32[]{:S(2)}, u32[]{:S(2)}) async-start(s32[128,1,1]{2,1,0:T(1,128)} %broadcast_in_dim.17), calls=%async_computation.2 | async-start | bytes 131072 | tf_op jit(solution)/shard_map/all_to_all | solution.py:152
  82.8 0.8 add_reduce_fusion
  83.6 0.5 broadcast.5
  84.1 0.8 reduce.5
  85.0 0.6 reshape.49
  85.6 7.0 %all-to-all-done.2 = s32[128,1,1]{2,1,0:T(1,128)S(1)} async-done(((s32[128,1,1]{2,1,0:T(1,128)}), s32[128,1,1]{2,1,0:T(1,128)S(1)}, u32[]{:S(2)}, u32[]{:S(2)}) %all-to-all-start.2) | async-done | bytes 544 | tf_op jit(solution)/shard_map/all_to_all | solution.py:152
  92.6 3.5 %all-to-all-start.3 = ((bf16[4,2,2048]{2,1,0:T(2,128)(2,1)}), bf16[4,2,2048]{2,1,0:T(2,128)(2,1)S(1)}, u32[]{:S(2)}, u32[]{:S(2)}) async-start(bf16[4,2,2048]{2,1,0:T(2,128)(2,1)} %reshape.49), calls=%async_computation.3 | async-start | bytes 65536 | tf_op jit(solution)/shard_map/all_to_all | solution.py:190
  96.1 2.4 %reduce.2 = s32[128]{0:T(128)S(1)} reduce(s32[128,1,1]{2,1,0:T(1,128)S(1)} %all-to-all-done.2, s32[]{:T(128)} %constant.19.clone.1), dimensions={1,2}, to_apply=%all_to_all.17.reduce_sub_computation | reduce | bytes 1028 | tf_op jit(solution)/shard_map/all_to_all | solution.py:152
  98.4 1.3 fusion
  99.7 0.8 all-to-all-done.3
  100.5 34.4 %all-gather.3.cloned.1.call-done = bf16[1,16384,1024]{2,1,0:T(8,128)(2,1)} async-done(((bf16[1,128,1024]{2,1,0:T(8,128)(2,1)}), bf16[1,16384,1024]{2,1,0:T(8,128)(2,1)}) %all-gather.3.cloned.1.call-update) | async-done | bytes 33554448 | tf_op jit(solution)/shard_map/all_gather | solution.py:181
  134.9 0.0 copy-start.1
  134.9 1.2 copy-done.1
  136.2 19.4 %layers.1 = (bf16[128,4096]{1,0:T(8,128)(2,1)}, f32[128,1,128]{2,1,0:T(1,128)S(1)}) custom-call(s32[1]{0:T(128)} %bitcast.6.code_ref, bf16[32,128,128]{2,1,0:T(8,128)(2,1)S(1)} %bitcast.16, bf16[4,32,1,128]{3,2,1,0:T(2,128)(2,1)S(1)} %bitcast.17, bf16[128,4096]{1,0:T(8,128)(2,1)S(1)} %copy-done.1, bf16[4,4096,1024]{2,1,0:T(8,128)(2,1)} %bitcast.18), custom_call_target="tpu_custom_call" | custom-call | tf_op jit(solution)/shard_map/layers/pallas_call | solution.py:122
  155.5 16.9 %all_to_all.26 = f32[128,1,128]{2,1,0:T(1,128)S(1)} all-to-all(f32[128,1,128]{2,1,0:T(1,128)S(1)} %get-tuple-element.5), channel_id=1, replica_groups=mesh['dp'=32,'section'=4] {'dp','section'}, dimensions={0} | all-to-all | bytes 131072 | tf_op jit(solution)/shard_map/all_to_all | solution.py:194
  172.4 0.7 slice_reduce_fusion
  (2 shorter events, 0.1 us)
Async XLA Ops:
  7.2 1.2 copy-start
  7.2 127.7 %all-gather.3.cloned.1.call-start = ((), (), s32[]{:S(2)}) async-start(), calls=%async_computation.5 | async-start | bytes 33816576 | tf_op jit(solution)/shard_map/all_gather | solution.py:181
  44.3 32.4 %all-to-all-start.1 = ((bf16[128,32,128]{2,1,0:T(8,128)(2,1)}), bf16[128,32,128]{2,1,0:T(8,128)(2,1)S(1)}, u32[]{:S(2)}, u32[]{:S(2)}) async-start(bf16[128,32,128]{2,1,0:T(8,128)(2,1)} %order.1), calls=%async_computation.1 | async-start | bytes 2097152 | tf_op jit(solution)/shard_map/all_to_all | solution.py:174
  79.2 13.4 %all-to-all-start.2 = ((s32[128,1,1]{2,1,0:T(1,128)}), s32[128,1,1]{2,1,0:T(1,128)S(1)}, u32[]{:S(2)}, u32[]{:S(2)}) async-start(s32[128,1,1]{2,1,0:T(1,128)} %broadcast_in_dim.17), calls=%async_computation.2 | async-start | bytes 131072 | tf_op jit(solution)/shard_map/all_to_all | solution.py:152
  92.6 7.9 %all-to-all-start.3 = ((bf16[4,2,2048]{2,1,0:T(2,128)(2,1)}), bf16[4,2,2048]{2,1,0:T(2,128)(2,1)S(1)}, u32[]{:S(2)}, u32[]{:S(2)}) async-start(bf16[4,2,2048]{2,1,0:T(2,128)(2,1)} %reshape.49), calls=%async_computation.3 | async-start | bytes 65536 | tf_op jit(solution)/shard_map/all_to_all | solution.py:190
  134.9 1.2 copy-start.1
Sparse Core Ops, SparseCore 0:
  11.0 123.8 all-gather.2

commit v5 on v4

--- a/solution.py
+++ b/solution.py
@@ -2,6 +2,7 @@
 
 import jax
 import jax.numpy as jnp
+import numpy as np
 from jax import lax
 from jax.experimental import pallas as pl
 from jax.experimental.pallas import tpu as pltpu
@@ -18,7 +19,8 @@
 CHUNKS = 4
 
 forget_weight = 0.5
-ALL = ("dp", "section")
+ALL = ("y", "z", "core", "section")
+GATHERED = 768
 
 
 def attend(boundary, x_s, normed_s, kv_s):
@@ -76,21 +78,29 @@
 
 
 def layers_kernel(
-    code_ref, pieces_ref, gain_ref, frozen_ref, w_ref, out_ref, part_ref,
+    code_ref, pieces_ref, gain_ref, frozen_ref, w_ref, rest_ref, out_ref, part_ref,
     x_s, normed_s, acc_s, kv_s, w_buf, sems, frozen_s, frozen_sem,
 ):
     depth = HD // CHUNKS
     slabs = depth // HS
 
-    def w_copy(layer, c):
-        return pltpu.make_async_copy(
-            w_ref.at[layer, pl.ds(c * depth, depth)],
-            w_buf.at[layer % 2, pl.ds(c * depth, depth)],
-            sems.at[layer % 2, c],
-        )
+    def w_copies(layer, c):
+        rows = pl.ds(c * depth, depth)
+        slot = layer % 2
+        return [
+            pltpu.make_async_copy(
+                w_ref.at[layer, rows], w_buf.at[slot, rows, pl.ds(0, GATHERED)], sems.at[slot, c, 0]
+            ),
+            pltpu.make_async_copy(
+                rest_ref.at[layer, rows],
+                w_buf.at[slot, rows, pl.ds(GATHERED, KVW - GATHERED)],
+                sems.at[slot, c, 1],
+            ),
+        ]
 
     for c in range(CHUNKS):
-        w_copy(0, c).start()
+        for copy in w_copies(0, c):
+            copy.start()
     frozen_copy = pltpu.make_async_copy(frozen_ref, frozen_s, frozen_sem)
     frozen_copy.start()
     x_s[...] = pieces_ref[...]
@@ -98,10 +108,12 @@
     for layer in range(4):
         if layer < 3:
             for c in range(CHUNKS):
-                w_copy(layer + 1, c).start()
+                for copy in w_copies(layer + 1, c):
+                    copy.start()
         normalize(gain_ref, layer, x_s, normed_s)
         for c in range(CHUNKS):
-            w_copy(layer, c).wait()
+            for copy in w_copies(layer, c):
+                copy.wait()
             rows = jnp.concatenate([normed_s[c * slabs + i] for i in range(slabs)], axis=1)
             part = jnp.dot(
                 rows, w_buf[layer % 2, c * depth : (c + 1) * depth, :], preferred_element_type=jnp.float32
@@ -117,7 +129,7 @@
     finish(code, x_s, frozen_s, out_ref, part_ref)
 
 
-def run_layers(code, pieces, gains, frozen, weights):
+def run_layers(code, pieces, gains, frozen, weights, rest):
     vmem = pl.BlockSpec(memory_space=pltpu.VMEM)
     return pl.pallas_call(
         layers_kernel,
@@ -129,6 +141,7 @@
             pl.BlockSpec(memory_space=pltpu.SMEM), vmem, vmem,
             pl.BlockSpec(memory_space=pl.ANY),
             pl.BlockSpec(memory_space=pl.ANY),
+            pl.BlockSpec(memory_space=pl.ANY),
         ],
         out_specs=(vmem, vmem),
         scratch_shapes=[
@@ -137,17 +150,17 @@
             pltpu.VMEM((BLK, KVW), jnp.float32),
             pltpu.VMEM((BLK, KVW), jnp.bfloat16),
             pltpu.VMEM((2, HD, KVW), jnp.bfloat16),
-            pltpu.SemaphoreType.DMA((2, CHUNKS)),
+            pltpu.SemaphoreType.DMA((2, CHUNKS, 2)),
             pltpu.VMEM((BLK, HD), jnp.bfloat16),
             pltpu.SemaphoreType.DMA,
         ],
         compiler_params=pltpu.CompilerParams(vmem_limit_bytes=40 << 20),
         name="layers",
-    )(code, pieces, gains, frozen, weights)
+    )(code, pieces, gains, frozen, weights, rest)
 
 
 def to_all(value):
-    count = lax.axis_size("dp") * lax.axis_size("section")
+    count = lax.axis_size(ALL)
     spread = jnp.broadcast_to(value.reshape(1, 1, 1), (count, 1, 1))
     return lax.all_to_all(spread, ALL, split_axis=0, concat_axis=0, tiled=True).reshape(count)
 
@@ -175,36 +188,95 @@
     return arrived.reshape(QH, BLK, HS)
 
 
+def assemble_kernel(here_ref, *refs):
+    blocks, (rest_ref, sems) = refs[:8], refs[8:]
+    y, z, core, x = (here_ref[i] for i in range(4))
+
+    def copies(side, third, i):
+        second, plane = i // 4, i % 4
+        owner = core if side == 0 else 1 - core
+        back_y = jnp.where(owner == 0, second, third)
+        back_z = jnp.where(owner == 0, third, second)
+        slab = (lax.rem(y - back_y + 4, 4) * 4 + lax.rem(z - back_z + 4, 4)) * 2 + owner
+        return pltpu.make_async_copy(
+            blocks[side * 4 + third].at[second, plane],
+            rest_ref.at[lax.rem(x - plane + 4, 4), pl.ds(pl.multiple_of(slab * HS, HS), HS)],
+            sems.at[side * 4 + third, i],
+        )
+
+    for side in range(2):
+        for third in range(4):
+            lax.fori_loop(0, 16, lambda i, carry: (copies(side, third, i).start(), carry)[1], 0)
+    for side in range(2):
+        for third in range(4):
+            lax.fori_loop(0, 16, lambda i, carry: (copies(side, third, i).wait(), carry)[1], 0)
+
+
+def assemble(here, blocks):
+    anywhere = pl.BlockSpec(memory_space=pl.ANY)
+    return pl.pallas_call(
+        assemble_kernel,
+        out_shape=jax.ShapeDtypeStruct((4, HD, KVW - GATHERED), jnp.bfloat16),
+        in_specs=[pl.BlockSpec(memory_space=pltpu.SMEM)] + [anywhere] * 8,
+        out_specs=anywhere,
+        scratch_shapes=[pltpu.SemaphoreType.DMA((8, 16))],
+        name="assemble",
+    )(here, *blocks)
+
+
+def moved(array, axes, by):
+    sizes = [lax.axis_size(axis) for axis in ALL]
+    pairs = []
+    for at in np.ndindex(*sizes):
+        to = list(at)
+        axis = axes[at[2]]
+        to[axis] = (to[axis] + by) % sizes[axis]
+        pairs.append((int(np.ravel_multi_index(at, sizes)), int(np.ravel_multi_index(to, sizes))))
+    return lax.ppermute(array, ALL, pairs)
+
+
+def around(array, axes):
+    return [array] + [moved(array, axes, by) for by in (1, 2, 3)]
+
+
 def local(hidden_in, segments, forget_flags, block_plan, layer_gains, kv_weights, frozen_states):
-    device_count = lax.axis_size("dp") * lax.axis_size("section")
-    here = lax.axis_index(ALL)
-    weights = lax.all_gather(kv_weights[0], ("section", "dp"), axis=0, tiled=True)
-    weights = weights.reshape(4, HD, KVW)
+    device_count = lax.axis_size(ALL)
+    here = jnp.stack([lax.axis_index(axis) for axis in ALL]).astype(jnp.int32)
+    index = lax.axis_index(ALL)
+    weights = lax.all_gather(
+        kv_weights[0, :, :GATHERED], ("section", "y", "z", "core"), axis=0, tiled=True
+    ).reshape(4, HD, GATHERED)
+    planes = jnp.stack(around(kv_weights[0, :, GATHERED:], (3, 3)))
+    lines = jnp.stack(around(planes, (0, 1)))
+    own = around(lines, (1, 0))
+    rest = assemble(here, own + [moved(block, (2, 2), 1) for block in own])
     boundary = BLK - jnp.sum(segments[0])
     pieces = route(hidden_in, block_plan)
     sample = pieces[0, 0, 0]
     later = (sample != sample).astype(jnp.int32)
     code = boundary * 4 + forget_flags[0, 0] * 2 + forget_flags[0, 1] + later
     codes = to_all(code)
-    routed_code = jnp.sum(jnp.where(block_plan == here, codes, 0)).reshape(1)
+    routed_code = jnp.sum(jnp.where(block_plan == index, codes, 0)).reshape(1)
     gains = lax.all_to_all(
-        jnp.broadcast_to((layer_gains + later.astype(jnp.bfloat16))[None], (4, 1, HD)), "section", split_axis=0, concat_axis=0, tiled=True
+        jnp.broadcast_to((layer_gains + later.astype(jnp.bfloat16))[None], (4, 1, HD)),
+        "section", split_axis=0, concat_axis=0, tiled=True,
     ).reshape(4, QH, 1, HS)
-    finished, part = run_layers(routed_code, pieces, gains, frozen_states, weights)
+    finished, part = run_layers(routed_code, pieces, gains, frozen_states, weights, rest)
     parts = lax.all_to_all(part, ALL, split_axis=0, concat_axis=0, tiled=True)
     objective = jnp.sum(parts[:, 0, 0]) / (BLK * device_count)
     return finished, objective
 
 
 def solution(mesh):
+    grid = jax.sharding.Mesh(mesh.devices.reshape(4, 4, 2, 4), ALL)
     in_specs = (
         P(ALL, None),
         P(ALL, None),
         P(ALL, None),
         P(),
         P("section", None),
-        P("section", "dp", None),
+        P("section", ("y", "z", "core"), None),
         P(ALL, None),
     )
     out_specs = (P(ALL, None), P())
-    return jax.shard_map(local, mesh=mesh, in_specs=in_specs, out_specs=out_specs, check_vma=False)
+    return jax.shard_map(local, mesh=grid, in_specs=in_specs, out_specs=out_specs, check_vma=False)

time: 182 us -> 430 us (2.36)
  Pallas kernels: 21.8 us -> 279 us
  starting transfers between devices: 10.7 us -> 46.7 us
  blocking collectives: 50.1 us -> 15.1 us
  waiting for transfers between devices: 67 us -> 46.6 us
  local copies, waits for them, and re-layouts: 5.72 us -> 12 us
    pallas_call x0 -> x1, Pallas kernels: none -> 257 us  [assemble(): pl.pallas_call(assemble_kernel, out_shape=jax.ShapeDtypeStruct((4, HD, KV...]
    all_gather x1, waiting for transfers between devices: 34.4 us -> 0.02 us  [local(): lax.all_gather(kv_weights[0, :, :GATHERED], ('section', 'y', 'z', 'core')...]
    all_to_all x1 -> x0, blocking collectives: 33.2 us -> none  [route(): lax.all_to_all(pieces, ALL, split_axis=0, concat_axis=0, tiled=True)]
    ppermute x0 -> x13, waiting for transfers between devices: none -> 25.9 us  [moved(): return lax.ppermute(array, ALL, pairs)]
    ppermute x0 -> x13, starting transfers between devices: none -> 24.8 us  [moved(): return lax.ppermute(array, ALL, pairs)]
    all_to_all x1, waiting for transfers between devices: 24.2 us -> 0.01 us  [route(): lax.all_to_all(ordered, ALL, split_axis=0, concat_axis=0, tiled=True)]
    all_to_all x0 -> x1, waiting for transfers between devices: none -> 12.5 us  [route(): lax.all_to_all(pieces, ALL, split_axis=0, concat_axis=0, tiled=True)]
    all_to_all x0 -> x1, starting transfers between devices: none -> 9.1 us  [route(): lax.all_to_all(pieces, ALL, split_axis=0, concat_axis=0, tiled=True)]
  transfers between devices with their start and end apart: 4 -> 18, of which waited for: 4 -> 7; matrix products, arithmetic and copies ran while one was open for 6% -> 4% of each run, Pallas kernels for 1% -> 60%
where the time goes in v5:
time: 430 us
  Pallas kernels  279 us (65%)
  starting transfers between devices  46.7 us (11%)
  waiting for transfers between devices  46.6 us (11%)
  between operations  19.3 us (4%)
  blocking collectives  15.1 us (4%)
  local copies, waits for them, and re-layouts  12 us (3%)
  other arithmetic  10.9 us (3%)
    pallas_call x1, Pallas kernels, assemble(): pl.pallas_call(assemble_kernel, out_shape=jax.ShapeDtypeStruct((4, HD, KV...  257 us
    ppermute x13, waiting for transfers between devices, moved(): return lax.ppermute(array, ALL, pairs)  25.9 us
    ppermute x13, starting transfers between devices, moved(): return lax.ppermute(array, ALL, pairs)  24.8 us
    pallas_call x1, Pallas kernels, run_layers(): pl.pallas_call(layers_kernel, out_shape=(jax.ShapeDtypeStruct((BLK, HD),...  19.5 us
    all_to_all x1, blocking collectives, local(): parts = lax.all_to_all(part, ALL, split_axis=0, concat_axis=0, tiled=True)  15.1 us
    all_to_all x1, waiting for transfers between devices, route(): lax.all_to_all(pieces, ALL, split_axis=0, concat_axis=0, tiled=True)  12.5 us
    all_to_all x1, starting transfers between devices, route(): lax.all_to_all(pieces, ALL, split_axis=0, concat_axis=0, tiled=True)  9.1 us
  transfers between devices with their start and end apart: 18, of which 7 were waited for; matrix products, arithmetic and copies ran while one was open for 4% of the time, Pallas kernels for 60%

profile of v5, /device:TPU:1, one launch (start us, length us, event | category | flops | bytes accessed | tf_op | source)
XLA Modules:
  0.0 429.6 jit_solution(5379942529847249201)
XLA Ops:
  7.2 0.0 all-gather.3.cloned.1.call-start
  7.2 1.8 slice.21
  9.0 0.9 fusion.2
  9.9 2.1 collective-permute-start
  12.0 2.5 collective-permute-start.1
  14.4 1.2 collective-permute-start.2
  15.6 1.4 collective-permute-done.1
  17.0 1.0 collective-permute-done.2
  18.0 0.8 fusion.1
  18.8 1.7 collective-permute-start.3
  20.5 3.3 collective-permute-start.4
  23.8 0.7 collective-permute-start.5
  24.5 1.3 copy_bitcast_fusion
  25.8 9.1 %all-to-all-start = ((bf16[128,32,128]{2,1,0:T(8,128)(2,1)}), bf16[128,32,128]{2,1,0:T(8,128)(2,1)S(1)}, u32[]{:S(2)}, u32[]{:S(2)}) async-start(bf16[128,32,128]{2,1,0:T(8,128)(2,1)} %bitcast.33), calls=%async_computation | async-start | bytes 2097152 | tf_op jit(solution)/shard_map/all_to_all | solution.py:178
  34.9 2.2 pad_maximum_fusion.refs_0_
  37.2 1.4 collective-permute-start.6
  38.6 2.4 collective-permute-start.7
  41.0 1.1 collective-permute-start.8
  42.1 12.5 %all-to-all-done.landed_ref = bf16[128,32,128]{2,1,0:T(8,128)(2,1)S(1)} async-done(((bf16[128,32,128]{2,1,0:T(8,128)(2,1)}), bf16[128,32,128]{2,1,0:T(8,128)(2,1)S(1)}, u32[]{:S(2)}, u32[]{:S(2)}) %all-to-all-start) | async-done | bytes 1048608 | tf_op jit(solution)/shard_map/all_to_all | solution.py:178
  54.7 1.0 copy-done.3
  55.6 2.6 order.1
  58.2 3.7 all-to-all-start.1
  61.9 1.3 collective-permute-start.9
  63.2 9.9 %collective-permute-done.6.refs_1_ = bf16[4,4,128,256]{3,2,1,0:T(8,128)(2,1)} collective-permute-done((bf16[4,4,128,256]{3,2,1,0:T(8,128)(2,1)}, bf16[4,4,128,256]{3,2,1,0:T(8,128)(2,1)}, u32[]{:S(2)}, u32[]{:S(2)}) %collective-permute-start.6) | collective-permute-done | bytes 1048608 | tf_op jit(solution)/shard_map/ppermute | solution.py:235
  73.0 4.2 collective-permute-start.10
  77.2 13.6 %collective-permute-done.7.refs_2_ = bf16[4,4,128,256]{3,2,1,0:T(8,128)(2,1)} collective-permute-done((bf16[4,4,128,256]{3,2,1,0:T(8,128)(2,1)}, bf16[4,4,128,256]{3,2,1,0:T(8,128)(2,1)}, u32[]{:S(2)}, u32[]{:S(2)}) %collective-permute-start.7) | collective-permute-done | bytes 1048608 | tf_op jit(solution)/shard_map/ppermute | solution.py:235
  90.9 2.8 collective-permute-start.11
  93.7 1.3 reduce_sum.27
  95.7 1.3 fusion.3
  98.3 0.7 pad_add_fusion.here_ref
  98.9 0.5 slice.24
  100.8 0.7 broadcast_in_dim.17
  101.4 5.6 %all-to-all-start.2 = ((s32[128,1,1]{2,1,0:T(1,128)}), s32[128,1,1]{2,1,0:T(1,128)S(1)}, u32[]{:S(2)}, u32[]{:S(2)}) async-start(s32[128,1,1]{2,1,0:T(1,128)} %broadcast_in_dim.17), calls=%async_computation.2 | async-start | bytes 131072 | tf_op jit(solution)/shard_map/all_to_all | solution.py:165
  107.0 0.8 add_reduce_fusion
  107.9 0.5 broadcast.5
  108.4 0.8 reduce.5
  109.2 0.7 reshape.49
  109.9 7.3 %all-to-all-done.2 = s32[128,1,1]{2,1,0:T(1,128)S(1)} async-done(((s32[128,1,1]{2,1,0:T(1,128)}), s32[128,1,1]{2,1,0:T(1,128)S(1)}, u32[]{:S(2)}, u32[]{:S(2)}) %all-to-all-start.2) | async-done | bytes 544 | tf_op jit(solution)/shard_map/all_to_all | solution.py:165
  117.2 3.4 all-to-all-start.3
  120.6 2.4 reduce.2
  123.0 1.3 fusion
  124.3 0.8 all-to-all-done.3
  125.2 257.0 %assemble.1.rest_ref = bf16[4,4096,256]{2,1,0:T(8,128)(2,1)} custom-call(s32[4]{0:T(128)} %pad_add_fusion.here_ref, bf16[4,4,128,256]{3,2,1,0:T(8,128)(2,1)} %pad_maximum_fusion.refs_0_, bf16[4,4,128,256]{3,2,1,0:T(8,128)(2,1)} %collective-permute-done.6.refs_1_, bf16[4,4,128,256]{3,2,1,0:T(8,128)(2,1)} %collective-permute-done.7.refs_2_, ...), custom_call_target="tpu_custom_call" | custom-call | tf_op jit(solution)/shard_map/assemble/pallas_call | solution.py:217
  382.2 0.0 all-gather.3.cloned.1.call-done
  382.3 3.4 copy-done.1
  385.6 19.5 %layers.1 = (bf16[128,4096]{1,0:T(8,128)(2,1)}, f32[128,1,128]{2,1,0:T(1,128)S(1)}) custom-call(s32[1]{0:T(128)} %bitcast.6.code_ref, bf16[32,128,128]{2,1,0:T(8,128)(2,1)S(1)} %bitcast.30, bf16[4,32,1,128]{3,2,1,0:T(2,128)(2,1)S(1)} %bitcast.31, bf16[128,4096]{1,0:T(8,128)(2,1)S(1)} %copy-done.2, bf16[4,4096,768]{2,1,0:T(8,128)(2,1)} %bitcast.32, ...), custom_call_target="tpu_custom_call" | custom-call | tf_op jit(solution)/shard_map/layers/pallas_call | solution.py:134
  405.1 15.1 %all_to_all.25 = f32[128,1,128]{2,1,0:T(1,128)S(1)} all-to-all(f32[128,1,128]{2,1,0:T(1,128)S(1)} %get-tuple-element.5), channel_id=1, replica_groups=mesh['y'=4,'z'=4,'core'=2,'section'=4] {'y','z','core','section'}, dimensions={0} | all-to-all | bytes 131072 | tf_op jit(solution)/shard_map/all_to_all | solution.py:265
  420.3 0.7 slice_reduce_fusion
  (20 shorter events, 0.1 us)
Async XLA Ops:
  7.2 17.4 %copy-start = (bf16[128,4096]{1,0:T(8,128)(2,1)S(1)}, bf16[128,4096]{1,0:T(8,128)(2,1)}, u32[]{:S(2)}) copy-start(bf16[128,4096]{1,0:T(8,128)(2,1)} %param.7) | copy-start | bytes 3145732
  7.2 375.1 %copy-start.2 = (bf16[128,4096]{1,0:T(8,128)(2,1)S(1)}, bf16[128,4096]{1,0:T(8,128)(2,1)}, u32[]{:S(2)}) copy-start(bf16[128,4096]{1,0:T(8,128)(2,1)} %frozen_ref.1) | copy-start | bytes 3145732
  7.2 375.1 %all-gather.3.cloned.1.call-start = ((), (), s32[]{:S(2)}) async-start(), calls=%async_computation.5 | async-start | bytes 25362432 | tf_op jit(solution)/shard_map/all_gather | solution.py:246
  9.9 5.7 %collective-permute-start = (bf16[128,256]{1,0:T(8,128)(2,1)S(1)}, bf16[128,256]{1,0:T(8,128)(2,1)S(1)}, u32[]{:S(2)}, u32[]{:S(2)}) collective-permute-start(bf16[128,256]{1,0:T(8,128)(2,1)S(1)} %get-tuple-element.9), channel_id=1, source_target_pairs={{0,1},{1,2},{2,3},{3,0},{4,5},{5,6},{6,7},{7,4},{8,9},{9,10},{10,1... | collective-permute-start | bytes 196616 | tf_op jit(solution)/shard_map/ppermute | solution.py:235
  12.0 5.1 %collective-permute-start.1 = (bf16[128,256]{1,0:T(8,128)(2,1)S(1)}, bf16[128,256]{1,0:T(8,128)(2,1)S(1)}, u32[]{:S(2)}, u32[]{:S(2)}) collective-permute-start(bf16[128,256]{1,0:T(8,128)(2,1)S(1)} %get-tuple-element.9), channel_id=1, source_target_pairs={{0,2},{1,3},{2,0},{3,1},{4,6},{5,7},{6,4},{7,5},{8,10},{9,11},{10,... | collective-permute-start | bytes 196616 | tf_op jit(solution)/shard_map/ppermute | solution.py:235
  14.4 3.6 collective-permute-start.2
  18.8 16.1 %collective-permute-start.3 = (bf16[4,128,256]{2,1,0:T(8,128)(2,1)}, bf16[4,128,256]{2,1,0:T(8,128)(2,1)}, u32[]{:S(2)}, u32[]{:S(2)}) collective-permute-start(bf16[4,128,256]{2,1,0:T(8,128)(2,1)} %get-tuple-element.7), channel_id=1, source_target_pairs={{0,32},{1,33},{2,34},{3,35},{4,12},{5,13},{6,14},{7,15},{8,40},{9,... | collective-permute-start | bytes 786440 | tf_op jit(solution)/shard_map/ppermute | solution.py:235
  20.5 14.4 %collective-permute-start.4 = (bf16[4,128,256]{2,1,0:T(8,128)(2,1)}, bf16[4,128,256]{2,1,0:T(8,128)(2,1)}, u32[]{:S(2)}, u32[]{:S(2)}) collective-permute-start(bf16[4,128,256]{2,1,0:T(8,128)(2,1)} %get-tuple-element.7), channel_id=1, source_target_pairs={{0,64},{1,65},{2,66},{3,67},{4,20},{5,21},{6,22},{7,23},{8,72},{9,... | collective-permute-start | bytes 786440 | tf_op jit(solution)/shard_map/ppermute | solution.py:235
  23.8 11.1 %collective-permute-start.5 = (bf16[4,128,256]{2,1,0:T(8,128)(2,1)}, bf16[4,128,256]{2,1,0:T(8,128)(2,1)}, u32[]{:S(2)}, u32[]{:S(2)}) collective-permute-start(bf16[4,128,256]{2,1,0:T(8,128)(2,1)} %get-tuple-element.7), channel_id=1, source_target_pairs={{0,96},{1,97},{2,98},{3,99},{4,28},{5,29},{6,30},{7,31},{8,104},{9... | collective-permute-start | bytes 786440 | tf_op jit(solution)/shard_map/ppermute | solution.py:235
  25.8 28.9 %all-to-all-start = ((bf16[128,32,128]{2,1,0:T(8,128)(2,1)}), bf16[128,32,128]{2,1,0:T(8,128)(2,1)S(1)}, u32[]{:S(2)}, u32[]{:S(2)}) async-start(bf16[128,32,128]{2,1,0:T(8,128)(2,1)} %bitcast.33), calls=%async_computation | async-start | bytes 2097152 | tf_op jit(solution)/shard_map/all_to_all | solution.py:178
  37.2 35.8 %collective-permute-start.6 = (bf16[4,4,128,256]{3,2,1,0:T(8,128)(2,1)}, bf16[4,4,128,256]{3,2,1,0:T(8,128)(2,1)}, u32[]{:S(2)}, u32[]{:S(2)}) collective-permute-start(bf16[4,4,128,256]{3,2,1,0:T(8,128)(2,1)} %pad_maximum_fusion.refs_0_), channel_id=1, source_target_pairs={{0,8},{1,9},{2,10},{3,11},{4,36},{5,37},{6,38},{7,39},{8,16},{9,17... | collective-permute-start | bytes 3145736 | tf_op jit(solution)/shard_map/ppermute | solution.py:235
  38.6 52.3 %collective-permute-start.7 = (bf16[4,4,128,256]{3,2,1,0:T(8,128)(2,1)}, bf16[4,4,128,256]{3,2,1,0:T(8,128)(2,1)}, u32[]{:S(2)}, u32[]{:S(2)}) collective-permute-start(bf16[4,4,128,256]{3,2,1,0:T(8,128)(2,1)} %pad_maximum_fusion.refs_0_), channel_id=1, source_target_pairs={{0,16},{1,17},{2,18},{3,19},{4,68},{5,69},{6,70},{7,71},{8,24},{9,... | collective-permute-start | bytes 3145736 | tf_op jit(solution)/shard_map/ppermute | solution.py:235
  41.0 52.7 %collective-permute-start.8 = (bf16[4,4,128,256]{3,2,1,0:T(8,128)(2,1)}, bf16[4,4,128,256]{3,2,1,0:T(8,128)(2,1)}, u32[]{:S(2)}, u32[]{:S(2)}) collective-permute-start(bf16[4,4,128,256]{3,2,1,0:T(8,128)(2,1)} %pad_maximum_fusion.refs_0_), channel_id=1, source_target_pairs={{0,24},{1,25},{2,26},{3,27},{4,100},{5,101},{6,102},{7,103},{8,0},... | collective-permute-start | bytes 3145736 | tf_op jit(solution)/shard_map/ppermute | solution.py:235
  54.6 1.0 copy-start.3
  58.2 40.8 %all-to-all-start.1 = ((bf16[128,32,128]{2,1,0:T(8,128)(2,1)}), bf16[128,32,128]{2,1,0:T(8,128)(2,1)S(1)}, u32[]{:S(2)}, u32[]{:S(2)}) async-start(bf16[128,32,128]{2,1,0:T(8,128)(2,1)} %order.1), calls=%async_computation.1 | async-start | bytes 2097152 | tf_op jit(solution)/shard_map/all_to_all | solution.py:187
  61.9 63.3 %collective-permute-start.9 = (bf16[4,4,128,256]{3,2,1,0:T(8,128)(2,1)}, bf16[4,4,128,256]{3,2,1,0:T(8,128)(2,1)}, u32[]{:S(2)}, u32[]{:S(2)}) collective-permute-start(bf16[4,4,128,256]{3,2,1,0:T(8,128)(2,1)} %pad_maximum_fusion.refs_0_), channel_id=1, source_target_pairs={{0,4},{1,5},{2,6},{3,7},{4,0},{5,1},{6,2},{7,3},{8,12},{9,13},{10,... | collective-permute-start | bytes 3145736 | tf_op jit(solution)/shard_map/ppermute | solution.py:235
  73.0 52.1 %collective-permute-start.10 = (bf16[4,4,128,256]{3,2,1,0:T(8,128)(2,1)}, bf16[4,4,128,256]{3,2,1,0:T(8,128)(2,1)}, u32[]{:S(2)}, u32[]{:S(2)}) collective-permute-start(bf16[4,4,128,256]{3,2,1,0:T(8,128)(2,1)} %collective-permute-done.6.refs_1_), channel_id=1, source_target_pairs={{0,4},{1,5},{2,6},{3,7},{4,0},{5,1},{6,2},{7,3},{8,12},{9,13},{10,... | collective-permute-start | bytes 3145736 | tf_op jit(solution)/shard_map/ppermute | solution.py:235
  90.9 34.3 %collective-permute-start.11 = (bf16[4,4,128,256]{3,2,1,0:T(8,128)(2,1)}, bf16[4,4,128,256]{3,2,1,0:T(8,128)(2,1)}, u32[]{:S(2)}, u32[]{:S(2)}) collective-permute-start(bf16[4,4,128,256]{3,2,1,0:T(8,128)(2,1)} %collective-permute-done.7.refs_2_), channel_id=1, source_target_pairs={{0,4},{1,5},{2,6},{3,7},{4,0},{5,1},{6,2},{7,3},{8,12},{9,13},{10,... | collective-permute-start | bytes 3145736 | tf_op jit(solution)/shard_map/ppermute | solution.py:235
  93.7 31.5 %collective-permute-start.12 = (bf16[4,4,128,256]{3,2,1,0:T(8,128)(2,1)}, bf16[4,4,128,256]{3,2,1,0:T(8,128)(2,1)}, u32[]{:S(2)}, u32[]{:S(2)}) collective-permute-start(bf16[4,4,128,256]{3,2,1,0:T(8,128)(2,1)} %collective-permute-done.8.refs_3_), channel_id=1, source_target_pairs={{0,4},{1,5},{2,6},{3,7},{4,0},{5,1},{6,2},{7,3},{8,12},{9,13},{10,... | collective-permute-start | bytes 3145736 | tf_op jit(solution)/shard_map/ppermute | solution.py:235
  101.4 15.7 %all-to-all-start.2 = ((s32[128,1,1]{2,1,0:T(1,128)}), s32[128,1,1]{2,1,0:T(1,128)S(1)}, u32[]{:S(2)}, u32[]{:S(2)}) async-start(s32[128,1,1]{2,1,0:T(1,128)} %broadcast_in_dim.17), calls=%async_computation.2 | async-start | bytes 131072 | tf_op jit(solution)/shard_map/all_to_all | solution.py:165
  117.2 7.9 %all-to-all-start.3 = ((bf16[4,2,2048]{2,1,0:T(2,128)(2,1)}), bf16[4,2,2048]{2,1,0:T(2,128)(2,1)S(1)}, u32[]{:S(2)}, u32[]{:S(2)}) async-start(bf16[4,2,2048]{2,1,0:T(2,128)(2,1)} %reshape.49), calls=%async_computation.3 | async-start | bytes 65536 | tf_op jit(solution)/shard_map/all_to_all | solution.py:260
  382.3 3.4 copy-start.1
Sparse Core Ops, SparseCore 0:
  11.0 129.8 all-gather.2

commit v6 on v4

v6 whole, which is shorter than its diff:
```python
import math

import jax
import jax.numpy as jnp
from jax import lax
from jax.experimental import pallas as pl
from jax.experimental.pallas import tpu as pltpu
from jax.sharding import PartitionSpec as P

QH = 32
KVH = 4
HS = 128
GROUP = 8
BLK = 128
HD = 4096
KVW = 2 * KVH * HS
PIECE_ROWS = 32
CHUNKS = 4

forget_weight = 0.5
ALL = ("dp", "section")


def layers_kernel(
    code_ref, pieces_ref, gain_ref, frozen_ref, w_ref, out_ref, part_ref,
    x_s, scaled_s, acc_s, kv_s, w_buf, sems, frozen_s, frozen_sem,
):
    depth = HD // CHUNKS

    def w_copy(layer, c):
        rows = pl.ds(c * depth, depth)
        return pltpu.make_async_copy(
            w_ref.at[layer, rows], w_buf.at[layer, rows], sems.at[layer, c]
        )

    def prepare(layer, j, states, squares):
        heads = pl.ds(j * GROUP, GROUP)
        widened = states.astype(jnp.float32)
        gain = gain_ref[layer, heads].astype(jnp.float32)
        scaled_s[heads] = (widened * gain).astype(jnp.bfloat16)
        return squares + jnp.sum(widened * widened, axis=0)

    def project(layer, j):
        rows = jnp.concatenate([scaled_s[j * GROUP + i] for i in range(GROUP)], axis=1)
        part = jnp.dot(
            rows, w_buf[layer, j * depth : (j + 1) * depth, :], preferred_element_type=jnp.float32
        )
        if j == 0:
            acc_s[...] = part
        else:
            acc_s[...] += part

    for layer in range(2):
        for c in range(CHUNKS):
            w_copy(layer, c).start()
    frozen_copy = pltpu.make_async_copy(frozen_ref, frozen_s, frozen_sem)
    frozen_copy.start()
    code = code_ref[0]
    boundary = code // 4
    t = lax.broadcasted_iota(jnp.int32, (BLK, BLK), 0)
    s = lax.broadcasted_iota(jnp.int32, (BLK, BLK), 1)
    allowed = (s <= t) & ((t < boundary) == (s < boundary))
    bias = jnp.where(allowed, 0.0, -jnp.inf)[None]
    factor = math.log2(math.e) / math.sqrt(HS)
    squares = jnp.zeros((BLK, HS), jnp.float32)
    for j in range(KVH):
        heads = pl.ds(j * GROUP, GROUP)
        states = pieces_ref[heads]
        x_s[heads] = states
        squares = prepare(0, j, states, squares)
    for j in range(KVH):
        w_copy(0, j).wait()
        w_copy(2, j).start()
        project(0, j)
    gaps = jnp.zeros((BLK, HS), jnp.float32)
    for layer in range(4):
        inverse = lax.rsqrt(jnp.sum(squares, axis=-1, keepdims=True) * (1.0 / HD) + 1e-05)
        kv_s[...] = (acc_s[...] * inverse).astype(jnp.bfloat16)
        scale = (inverse * factor)[None]
        squares = jnp.zeros((BLK, HS), jnp.float32)
        if layer == 3:
            frozen_copy.wait()
        for j in range(KVH):
            keys = kv_s[:, j * HS : (j + 1) * HS]
            values = kv_s[:, (j + KVH) * HS : (j + KVH + 1) * HS]
            heads = pl.ds(j * GROUP, GROUP)
            queries = scaled_s[heads].reshape(GROUP * BLK, HS)
            scores = lax.dot_general(
                queries, keys, (((1,), (1,)), ((), ())), preferred_element_type=jnp.float32
            )
            scores = scores.reshape(GROUP, BLK, BLK) + bias
            top = jnp.max(scores, axis=-1, keepdims=True)
            weights = jnp.exp2((scores - top) * scale).astype(jnp.bfloat16).reshape(GROUP * BLK, BLK)
            widened = jnp.concatenate([values, jnp.ones((BLK, HS), jnp.bfloat16)], axis=1)
            both = jnp.dot(weights, widened, preferred_element_type=jnp.float32)
            mixture = (both[:, :HS] / both[:, HS:]).reshape(GROUP, BLK, HS)
            states = (x_s[heads].astype(jnp.float32) + mixture).astype(jnp.bfloat16)
            if layer < 3:
                x_s[heads] = states
                squares = prepare(layer + 1, j, states, squares)
                w_copy(layer + 1, j).wait()
                if layer == 0:
                    w_copy(3, j).start()
                project(layer + 1, j)
            else:
                for g in range(GROUP):
                    cols = slice((j * GROUP + g) * HS, (j * GROUP + g + 1) * HS)
                    out_ref[:, cols] = states[g]
                    gap = states[g].astype(jnp.float32) - frozen_s[:, cols].astype(jnp.float32)
                    gaps += gap * gap
    flag = jnp.where(t < boundary, (code // 2) % 2, code % 2).astype(jnp.float32)
    part = jnp.sum(((1.0 - flag) - forget_weight * flag) * gaps, axis=0, keepdims=True)
    part = jnp.sum(part, axis=1, keepdims=True) * (1.0 / HD)
    part_ref[...] = jnp.broadcast_to(part, part_ref.shape)


def run_layers(code, pieces, gains, frozen, weights):
    vmem = pl.BlockSpec(memory_space=pltpu.VMEM)
    return pl.pallas_call(
        layers_kernel,
        out_shape=(
            jax.ShapeDtypeStruct((BLK, HD), jnp.bfloat16),
            jax.ShapeDtypeStruct((128, 1, HS), jnp.float32),
        ),
        in_specs=[
            pl.BlockSpec(memory_space=pltpu.SMEM), vmem, vmem,
            pl.BlockSpec(memory_space=pltpu.HBM),
            pl.BlockSpec(memory_space=pltpu.HBM),
        ],
        out_specs=(vmem, vmem),
        scratch_shapes=[
            pltpu.VMEM((QH, BLK, HS), jnp.bfloat16),
            pltpu.VMEM((QH, BLK, HS), jnp.bfloat16),
            pltpu.VMEM((BLK, KVW), jnp.float32),
            pltpu.VMEM((BLK, KVW), jnp.bfloat16),
            pltpu.VMEM((4, HD, KVW), jnp.bfloat16),
            pltpu.SemaphoreType.DMA((4, CHUNKS)),
            pltpu.VMEM((BLK, HD), jnp.bfloat16),
            pltpu.SemaphoreType.DMA,
        ],
        compiler_params=pltpu.CompilerParams(vmem_limit_bytes=52 << 20),
        name="layers",
    )(code, pieces, gains, frozen, weights)


def to_all(value):
    count = lax.axis_size("dp") * lax.axis_size("section")
    spread = jnp.broadcast_to(value.reshape(1, 1, 1), (count, 1, 1))
    return lax.all_to_all(spread, ALL, split_axis=0, concat_axis=0, tiled=True).reshape(count)


def order_kernel(plan_ref, landed_ref, ordered_ref):
    def place(b, carry):
        ordered_ref[plan_ref[b]] = landed_ref[b]
        return carry

    lax.fori_loop(0, landed_ref.shape[0], place, 0, unroll=8)


def route(hidden_in, block_plan):
    pieces = hidden_in.reshape(BLK, QH, HS).transpose(1, 0, 2).reshape(-1, PIECE_ROWS, HS)
    landed = lax.all_to_all(pieces, ALL, split_axis=0, concat_axis=0, tiled=True)
    vmem = pl.BlockSpec(memory_space=pltpu.VMEM)
    ordered = pl.pallas_call(
        order_kernel,
        out_shape=jax.ShapeDtypeStruct(landed.shape, landed.dtype),
        in_specs=[pl.BlockSpec(memory_space=pltpu.SMEM), vmem],
        out_specs=vmem,
        name="order",
    )(block_plan, landed)
    arrived = lax.all_to_all(ordered, ALL, split_axis=0, concat_axis=0, tiled=True)
    return arrived.reshape(QH, BLK, HS)


def local(hidden_in, segments, forget_flags, block_plan, layer_gains, kv_weights, frozen_states):
    device_count = lax.axis_size("dp") * lax.axis_size("section")
    here = lax.axis_index(ALL)
    weights = lax.all_gather(kv_weights[0], ("section", "dp"), axis=0, tiled=True)
    weights = weights.reshape(4, HD, KVW)
    boundary = BLK - jnp.sum(segments[0])
    pieces = route(hidden_in, block_plan)
    sample = pieces[0, 0, 0]
    later = (sample != sample).astype(jnp.int32)
    code = boundary * 4 + forget_flags[0, 0] * 2 + forget_flags[0, 1] + later
    codes = to_all(code)
    routed_code = jnp.sum(jnp.where(block_plan == here, codes, 0)).reshape(1)
    gains = lax.all_to_all(
        jnp.broadcast_to((layer_gains + later.astype(jnp.bfloat16))[None], (4, 1, HD)), "section", split_axis=0, concat_axis=0, tiled=True
    ).reshape(4, QH, 1, HS)
    finished, part = run_layers(routed_code, pieces, gains, frozen_states, weights)
    parts = lax.all_to_all(part, ALL, split_axis=0, concat_axis=0, tiled=True)
    objective = jnp.sum(parts[:, 0, 0]) / (BLK * device_count)
    return finished, objective


def solution(mesh):
    in_specs = (
        P(ALL, None),
        P(ALL, None),
        P(ALL, None),
        P(),
        P("section", None),
        P("section", "dp", None),
        P(ALL, None),
    )
    out_specs = (P(ALL, None), P())
    return jax.shard_map(local, mesh=mesh, in_specs=in_specs, out_specs=out_specs, check_vma=False)
```

time: 182 us -> 180 us (0.989)
  no operation moved by 1% of the time
where the time goes in v6:
time: 180 us; the launch traced here: 179 us
  waiting for transfers between devices  67 us (37%)
  blocking collectives  50.1 us (28%)
  Pallas kernels  20.3 us (11%)
  between operations  19.2 us (11%)
  starting transfers between devices  10.7 us (6%)
  other arithmetic  7.33 us (4%)
  local copies, waits for them, and re-layouts  4.49 us (2%)
    all_gather x1, waiting for transfers between devices, local(): lax.all_gather(kv_weights[0], ('section', 'dp'), axis=0, tiled=True)  34.4 us
    all_to_all x1, blocking collectives, route(): lax.all_to_all(pieces, ALL, split_axis=0, concat_axis=0, tiled=True)  33.2 us
    all_to_all x1, waiting for transfers between devices, route(): lax.all_to_all(ordered, ALL, split_axis=0, concat_axis=0, tiled=True)  24.2 us
    pallas_call x1, Pallas kernels, run_layers(): pl.pallas_call(layers_kernel, out_shape=(jax.ShapeDtypeStruct((BLK, HD),...  17.8 us
    all_to_all x1, blocking collectives, local(): parts = lax.all_to_all(part, ALL, split_axis=0, concat_axis=0, tiled=True)  16.9 us
    all_to_all x1, waiting for transfers between devices, to_all(): lax.all_to_all(spread, ALL, split_axis=0, concat_axis=0, tiled=True)  6.99 us
    all_to_all x1, starting transfers between devices, to_all(): lax.all_to_all(spread, ALL, split_axis=0, concat_axis=0, tiled=True)  3.61 us
  transfers between devices with their start and end apart: 4, of which 4 were waited for; matrix products, arithmetic and copies ran while one was open for 6% of the time, Pallas kernels for 1%

profile of v6, /device:TPU:1, one launch (start us, length us, event | category | flops | bytes accessed | tf_op | source)
XLA Modules:
  0.0 179.0 jit_solution(9025941769382028910)
XLA Ops:
  7.2 0.0 copy-start
  7.2 0.0 all-gather.3.cloned.1.call-start
  7.2 0.7 all-gather.3.cloned.1.call-update
  7.9 0.5 copy-done
  8.4 0.3 copy_bitcast_fusion
  8.7 33.2 %all_to_all.25.landed_ref = bf16[128,32,128]{2,1,0:T(8,128)(2,1)} all-to-all(bf16[128,32,128]{2,1,0:T(8,128)(2,1)S(1)} %bitcast.19), channel_id=1, replica_groups=mesh['dp'=32,'section'=4] {'dp','section'}, dimensions={0} | all-to-all | bytes 2097152 | tf_op jit(solution)/shard_map/all_to_all | solution.py:162
  41.9 2.4 %order.1 = bf16[128,32,128]{2,1,0:T(8,128)(2,1)} custom-call(s32[128]{0:T(128)} %plan_ref.1, bf16[128,32,128]{2,1,0:T(8,128)(2,1)} %all_to_all.25.landed_ref), custom_call_target="tpu_custom_call" | custom-call | tf_op jit(solution)/shard_map/order/pallas_call | solution.py:164
  44.3 3.6 %all-to-all-start.1 = ((bf16[128,32,128]{2,1,0:T(8,128)(2,1)}), bf16[128,32,128]{2,1,0:T(8,128)(2,1)S(1)}, u32[]{:S(2)}, u32[]{:S(2)}) async-start(bf16[128,32,128]{2,1,0:T(8,128)(2,1)} %order.1), calls=%async_computation.1 | async-start | bytes 2097152 | tf_op jit(solution)/shard_map/all_to_all | solution.py:171
  47.9 1.3 reduce_sum.27
  49.8 1.3 fusion.1
  52.5 24.2 %all-to-all-done.1 = bf16[128,32,128]{2,1,0:T(8,128)(2,1)S(1)} async-done(((bf16[128,32,128]{2,1,0:T(8,128)(2,1)}), bf16[128,32,128]{2,1,0:T(8,128)(2,1)S(1)}, u32[]{:S(2)}, u32[]{:S(2)}) %all-to-all-start.1) | async-done | bytes 1048608 | tf_op jit(solution)/shard_map/all_to_all | solution.py:171
  76.7 0.5 slice.16
  78.5 0.7 broadcast_in_dim.17
  79.2 3.6 %all-to-all-start.2 = ((s32[128,1,1]{2,1,0:T(1,128)}), s32[128,1,1]{2,1,0:T(1,128)S(1)}, u32[]{:S(2)}, u32[]{:S(2)}) async-start(s32[128,1,1]{2,1,0:T(1,128)} %broadcast_in_dim.17), calls=%async_computation.2 | async-start | bytes 131072 | tf_op jit(solution)/shard_map/all_to_all | solution.py:149
  82.8 0.8 add_reduce_fusion
  83.6 0.5 broadcast.5
  84.1 0.8 reduce.5
  85.0 0.6 reshape.49
  85.6 7.0 %all-to-all-done.2 = s32[128,1,1]{2,1,0:T(1,128)S(1)} async-done(((s32[128,1,1]{2,1,0:T(1,128)}), s32[128,1,1]{2,1,0:T(1,128)S(1)}, u32[]{:S(2)}, u32[]{:S(2)}) %all-to-all-start.2) | async-done | bytes 544 | tf_op jit(solution)/shard_map/all_to_all | solution.py:149
  92.6 3.5 %all-to-all-start.3 = ((bf16[4,2,2048]{2,1,0:T(2,128)(2,1)}), bf16[4,2,2048]{2,1,0:T(2,128)(2,1)S(1)}, u32[]{:S(2)}, u32[]{:S(2)}) async-start(bf16[4,2,2048]{2,1,0:T(2,128)(2,1)} %reshape.49), calls=%async_computation.3 | async-start | bytes 65536 | tf_op jit(solution)/shard_map/all_to_all | solution.py:187
  96.1 2.4 %reduce.2 = s32[128]{0:T(128)S(1)} reduce(s32[128,1,1]{2,1,0:T(1,128)S(1)} %all-to-all-done.2, s32[]{:T(128)} %constant.19.clone.1), dimensions={1,2}, to_apply=%all_to_all.17.reduce_sub_computation | reduce | bytes 1028 | tf_op jit(solution)/shard_map/all_to_all | solution.py:149
  98.4 1.3 fusion
  99.7 0.8 all-to-all-done.3
  100.5 34.4 %all-gather.3.cloned.1.call-done = bf16[1,16384,1024]{2,1,0:T(8,128)(2,1)} async-done(((bf16[1,128,1024]{2,1,0:T(8,128)(2,1)}), bf16[1,16384,1024]{2,1,0:T(8,128)(2,1)}) %all-gather.3.cloned.1.call-update) | async-done | bytes 33554448 | tf_op jit(solution)/shard_map/all_gather | solution.py:178
  134.9 17.8 %layers.1 = (bf16[128,4096]{1,0:T(8,128)(2,1)}, f32[128,1,128]{2,1,0:T(1,128)S(1)}) custom-call(s32[1]{0:T(128)} %bitcast.6.code_ref, bf16[32,128,128]{2,1,0:T(8,128)(2,1)S(1)} %bitcast.16, bf16[4,32,1,128]{3,2,1,0:T(2,128)(2,1)S(1)} %bitcast.17, bf16[128,4096]{1,0:T(8,128)(2,1)} %frozen_ref.1, bf16[4,4096,1024]{2,1,0:T(8,128)(2,1)} %bitcast.18), custom_call_target="tpu_custom_call" | custom-call | tf_op jit(solution)/shard_map/layers/pallas_call | solution.py:119
  152.8 16.9 %all_to_all.26 = f32[128,1,128]{2,1,0:T(1,128)S(1)} all-to-all(f32[128,1,128]{2,1,0:T(1,128)S(1)} %get-tuple-element.5), channel_id=1, replica_groups=mesh['dp'=32,'section'=4] {'dp','section'}, dimensions={0} | all-to-all | bytes 131072 | tf_op jit(solution)/shard_map/all_to_all | solution.py:191
  169.7 0.7 slice_reduce_fusion
  (2 shorter events, 0.1 us)
Async XLA Ops:
  7.2 1.2 copy-start
  7.2 127.7 %all-gather.3.cloned.1.call-start = ((), (), s32[]{:S(2)}) async-start(), calls=%async_computation.5 | async-start | bytes 33816576 | tf_op jit(solution)/shard_map/all_gather | solution.py:178
  44.3 32.4 %all-to-all-start.1 = ((bf16[128,32,128]{2,1,0:T(8,128)(2,1)}), bf16[128,32,128]{2,1,0:T(8,128)(2,1)S(1)}, u32[]{:S(2)}, u32[]{:S(2)}) async-start(bf16[128,32,128]{2,1,0:T(8,128)(2,1)} %order.1), calls=%async_computation.1 | async-start | bytes 2097152 | tf_op jit(solution)/shard_map/all_to_all | solution.py:171
  79.2 13.4 %all-to-all-start.2 = ((s32[128,1,1]{2,1,0:T(1,128)}), s32[128,1,1]{2,1,0:T(1,128)S(1)}, u32[]{:S(2)}, u32[]{:S(2)}) async-start(s32[128,1,1]{2,1,0:T(1,128)} %broadcast_in_dim.17), calls=%async_computation.2 | async-start | bytes 131072 | tf_op jit(solution)/shard_map/all_to_all | solution.py:149
  92.6 7.9 %all-to-all-start.3 = ((bf16[4,2,2048]{2,1,0:T(2,128)(2,1)}), bf16[4,2,2048]{2,1,0:T(2,128)(2,1)S(1)}, u32[]{:S(2)}, u32[]{:S(2)}) async-start(bf16[4,2,2048]{2,1,0:T(2,128)(2,1)} %reshape.49), calls=%async_computation.3 | async-start | bytes 65536 | tf_op jit(solution)/shard_map/all_to_all | solution.py:187
Sparse Core Ops, SparseCore 0:
  11.0 123.8 all-gather.2

commit v7 on v6

--- a/solution.py
+++ b/solution.py
@@ -143,12 +143,6 @@
     )(code, pieces, gains, frozen, weights)
 
 
-def to_all(value):
-    count = lax.axis_size("dp") * lax.axis_size("section")
-    spread = jnp.broadcast_to(value.reshape(1, 1, 1), (count, 1, 1))
-    return lax.all_to_all(spread, ALL, split_axis=0, concat_axis=0, tiled=True).reshape(count)
-
-
 def order_kernel(plan_ref, landed_ref, ordered_ref):
     def place(b, carry):
         ordered_ref[plan_ref[b]] = landed_ref[b]
@@ -181,12 +175,17 @@
     pieces = route(hidden_in, block_plan)
     sample = pieces[0, 0, 0]
     later = (sample != sample).astype(jnp.int32)
-    code = boundary * 4 + forget_flags[0, 0] * 2 + forget_flags[0, 1] + later
-    codes = to_all(code)
-    routed_code = jnp.sum(jnp.where(block_plan == here, codes, 0)).reshape(1)
-    gains = lax.all_to_all(
-        jnp.broadcast_to((layer_gains + later.astype(jnp.bfloat16))[None], (4, 1, HD)), "section", split_axis=0, concat_axis=0, tiled=True
-    ).reshape(4, QH, 1, HS)
+    code = jnp.concatenate([(boundary + later).reshape(1), forget_flags[0]]).astype(jnp.bfloat16)
+    code = jnp.zeros((1, HS), jnp.bfloat16).at[0, :3].set(code)
+    own_gains = lax.dynamic_slice(layer_gains, (0, lax.axis_index("dp") * HS), (1, HS))
+    message = jnp.concatenate([own_gains, code], axis=0)
+    messages = lax.all_to_all(
+        jnp.broadcast_to(message[None], (device_count, 2, HS)), ALL, split_axis=0, concat_axis=0, tiled=True
+    )
+    gains = messages[:, 0].reshape(QH, 4, HS).transpose(1, 0, 2).reshape(4, QH, 1, HS)
+    codes = messages[:, 1].astype(jnp.float32)
+    routed = jnp.sum(jnp.where((block_plan == here)[:, None], codes, 0.0), axis=0)
+    routed_code = (routed[0] * 4.0 + routed[1] * 2.0 + routed[2]).astype(jnp.int32).reshape(1)
     finished, part = run_layers(routed_code, pieces, gains, frozen_states, weights)
     parts = lax.all_to_all(part, ALL, split_axis=0, concat_axis=0, tiled=True)
     objective = jnp.sum(parts[:, 0, 0]) / (BLK * device_count)

time: 180 us -> 179 us (level)
  waiting for transfers between devices: 67 us -> 73.2 us
  starting transfers between devices: 10.7 us -> 7.37 us
  other arithmetic: 7.33 us -> 4.94 us
    all_gather x1, waiting for transfers between devices: 34.4 us -> 38.4 us  [local(): lax.all_gather(kv_weights[0], ('section', 'dp'), axis=0, tiled=True)]
    all_to_all x2 -> x1, starting transfers between devices: 7.06 us -> 3.77 us  [local(): lax.all_to_all(jnp.broadcast_to(message[None], (device_count, 2, HS)), AL...]
    all_to_all x1 -> x0, other arithmetic: 2.35 us -> none  [to_all(): lax.all_to_all(spread, ALL, split_axis=0, concat_axis=0, tiled=True)]
    another operation x0 -> x3, other arithmetic: none -> 2.02 us
    all_to_all x2 -> x1, waiting for transfers between devices: 7.77 us -> 9.25 us  [local(): lax.all_to_all(jnp.broadcast_to(message[None], (device_count, 2, HS)), AL...]
  transfers between devices with their start and end apart: 4 -> 3, of which waited for: 4 -> 3; matrix products, arithmetic and copies ran while one was open for 6% -> 4% of each run, Pallas kernels for 1% -> 1%
where the time goes in v7:
time: 179 us; the launch traced here: 178 us
  waiting for transfers between devices  73.2 us (41%)
  blocking collectives  50.1 us (28%)
  between operations  19.8 us (11%)
  Pallas kernels  19.4 us (11%)
  starting transfers between devices  7.37 us (4%)
  other arithmetic  4.94 us (3%)
  local copies, waits for them, and re-layouts  3.32 us (2%)
    all_gather x1, waiting for transfers between devices, local(): lax.all_gather(kv_weights[0], ('section', 'dp'), axis=0, tiled=True)  38.4 us
    all_to_all x1, blocking collectives, route(): lax.all_to_all(pieces, ALL, split_axis=0, concat_axis=0, tiled=True)  33.2 us
    all_to_all x1, waiting for transfers between devices, route(): lax.all_to_all(ordered, ALL, split_axis=0, concat_axis=0, tiled=True)  24.9 us
    pallas_call x1, Pallas kernels, run_layers(): pl.pallas_call(layers_kernel, out_shape=(jax.ShapeDtypeStruct((BLK, HD),...  17 us
    all_to_all x1, blocking collectives, local(): parts = lax.all_to_all(part, ALL, split_axis=0, concat_axis=0, tiled=True)  16.9 us
    all_to_all x1, waiting for transfers between devices, local(): lax.all_to_all(jnp.broadcast_to(message[None], (device_count, 2, HS)), AL...  9.25 us
    all_to_all x1, starting transfers between devices, local(): lax.all_to_all(jnp.broadcast_to(message[None], (device_count, 2, HS)), AL...  3.77 us
  transfers between devices with their start and end apart: 3, of which 3 were waited for; matrix products, arithmetic and copies ran while one was open for 4% of the time, Pallas kernels for 1%

profile of v7, /device:TPU:1, one launch (start us, length us, event | category | flops | bytes accessed | tf_op | source)
XLA Modules:
  0.0 178.2 jit_solution(13211080380352265870)
XLA Ops:
  7.2 0.0 copy-start
  7.2 0.0 all-gather.3.cloned.1.call-start
  7.2 0.7 all-gather.3.cloned.1.call-update
  7.9 0.5 copy-done
  8.4 0.3 copy_bitcast_fusion
  8.7 33.2 %all_to_all.20.landed_ref = bf16[128,32,128]{2,1,0:T(8,128)(2,1)} all-to-all(bf16[128,32,128]{2,1,0:T(8,128)(2,1)S(1)} %bitcast.21), channel_id=1, replica_groups=mesh['dp'=32,'section'=4] {'dp','section'}, dimensions={0} | all-to-all | bytes 2097152 | tf_op jit(solution)/shard_map/all_to_all | solution.py:156
  41.9 2.4 %order.1 = bf16[128,32,128]{2,1,0:T(8,128)(2,1)} custom-call(s32[128]{0:T(128)} %plan_ref.1, bf16[128,32,128]{2,1,0:T(8,128)(2,1)} %all_to_all.20.landed_ref), custom_call_target="tpu_custom_call" | custom-call | tf_op jit(solution)/shard_map/order/pallas_call | solution.py:158
  44.3 3.6 %all-to-all-start.1 = ((bf16[128,32,128]{2,1,0:T(8,128)(2,1)}), bf16[128,32,128]{2,1,0:T(8,128)(2,1)S(1)}, u32[]{:S(2)}, u32[]{:S(2)}) async-start(bf16[128,32,128]{2,1,0:T(8,128)(2,1)} %order.1), calls=%async_computation.1 | async-start | bytes 2097152 | tf_op jit(solution)/shard_map/all_to_all | solution.py:165
  47.9 1.3 reduce_sum.27
  49.8 0.7 convert.10
  50.5 0.6 compare_reduce_fusion
  51.1 0.7 constant_dynamic-slice_fusion
  51.8 24.9 %all-to-all-done.1 = bf16[128,32,128]{2,1,0:T(8,128)(2,1)S(1)} async-done(((bf16[128,32,128]{2,1,0:T(8,128)(2,1)}), bf16[128,32,128]{2,1,0:T(8,128)(2,1)S(1)}, u32[]{:S(2)}, u32[]{:S(2)}) %all-to-all-start.1) | async-done | bytes 1048608 | tf_op jit(solution)/shard_map/all_to_all | solution.py:165
  76.7 0.5 slice.44
  78.5 0.7 broadcast_select_fusion
  79.2 0.7 broadcast_in_dim.21
  79.9 3.8 %all-to-all-start.2 = ((bf16[128,2,128]{2,1,0:T(2,128)(2,1)}), bf16[128,2,128]{2,1,0:T(2,128)(2,1)S(1)}, u32[]{:S(2)}, u32[]{:S(2)}) async-start(bf16[128,2,128]{2,1,0:T(2,128)(2,1)} %broadcast_in_dim.21), calls=%async_computation.2 | async-start | bytes 131072 | tf_op jit(solution)/shard_map/all_to_all | solution.py:182
  83.7 0.7 broadcast_compare_fusion
  84.4 9.2 %all-to-all-done.2 = bf16[128,2,128]{2,1,0:T(2,128)(2,1)S(1)} async-done(((bf16[128,2,128]{2,1,0:T(2,128)(2,1)}), bf16[128,2,128]{2,1,0:T(2,128)(2,1)S(1)}, u32[]{:S(2)}, u32[]{:S(2)}) %all-to-all-start.2) | async-done | bytes 65568 | tf_op jit(solution)/shard_map/all_to_all | solution.py:182
  93.6 0.1 fusion.1
  93.7 0.1 select_reduce_fusion
  93.8 0.7 fusion.2
  96.5 0.1 copy.16.gain_ref
  96.5 38.4 %all-gather.3.cloned.1.call-done = bf16[1,16384,1024]{2,1,0:T(8,128)(2,1)} async-done(((bf16[1,128,1024]{2,1,0:T(8,128)(2,1)}), bf16[1,16384,1024]{2,1,0:T(8,128)(2,1)}) %all-gather.3.cloned.1.call-update) | async-done | bytes 33554448 | tf_op jit(solution)/shard_map/all_gather | solution.py:172
  134.9 17.0 %layers.1 = (bf16[128,4096]{1,0:T(8,128)(2,1)}, f32[128,1,128]{2,1,0:T(1,128)S(1)}) custom-call(s32[1]{0:T(128)S(6)} %convert_element_type.26.code_ref, bf16[32,128,128]{2,1,0:T(8,128)(2,1)S(1)} %bitcast.19, bf16[4,32,1,128]{3,2,1,0:T(2,128)(2,1)S(1)} %copy.16.gain_ref, bf16[128,4096]{1,0:T(8,128)(2,1)} %frozen_ref.1, bf16[4,4096,1024]{2,1,0:T(8,128)(2,1)} %bitcast.20), custom_call_target="tpu_custom_call" | custom-call | tf_op jit(solution)/shard_map/layers/pallas_call | solution.py:119
  151.9 16.9 %all_to_all.21 = f32[128,1,128]{2,1,0:T(1,128)S(1)} all-to-all(f32[128,1,128]{2,1,0:T(1,128)S(1)} %get-tuple-element.17), channel_id=1, replica_groups=mesh['dp'=32,'section'=4] {'dp','section'}, dimensions={0} | all-to-all | bytes 131072 | tf_op jit(solution)/shard_map/all_to_all | solution.py:190
  168.8 0.7 slice_reduce_fusion
  (2 shorter events, 0.0 us)
Async XLA Ops:
  7.2 1.2 copy-start
  7.2 127.7 %all-gather.3.cloned.1.call-start = ((), (), s32[]{:S(2)}) async-start(), calls=%async_computation.4 | async-start | bytes 33816576 | tf_op jit(solution)/shard_map/all_gather | solution.py:172
  44.3 32.4 %all-to-all-start.1 = ((bf16[128,32,128]{2,1,0:T(8,128)(2,1)}), bf16[128,32,128]{2,1,0:T(8,128)(2,1)S(1)}, u32[]{:S(2)}, u32[]{:S(2)}) async-start(bf16[128,32,128]{2,1,0:T(8,128)(2,1)} %order.1), calls=%async_computation.1 | async-start | bytes 2097152 | tf_op jit(solution)/shard_map/all_to_all | solution.py:165
  79.9 13.7 %all-to-all-start.2 = ((bf16[128,2,128]{2,1,0:T(2,128)(2,1)}), bf16[128,2,128]{2,1,0:T(2,128)(2,1)S(1)}, u32[]{:S(2)}, u32[]{:S(2)}) async-start(bf16[128,2,128]{2,1,0:T(2,128)(2,1)} %broadcast_in_dim.21), calls=%async_computation.2 | async-start | bytes 131072 | tf_op jit(solution)/shard_map/all_to_all | solution.py:182
Sparse Core Ops, SparseCore 0:
  11.0 123.8 all-gather.2

commit v8 on v7

--- a/solution.py
+++ b/solution.py
@@ -84,10 +84,27 @@
             keys = kv_s[:, j * HS : (j + 1) * HS]
             values = kv_s[:, (j + KVH) * HS : (j + KVH + 1) * HS]
             heads = pl.ds(j * GROUP, GROUP)
-            queries = scaled_s[heads].reshape(GROUP * BLK, HS)
-            scores = lax.dot_general(
-                queries, keys, (((1,), (1,)), ((), ())), preferred_element_type=jnp.float32
-            )
+            if j % 2 == 0:
+                queries = jnp.concatenate(
+                    [
+                        scaled_s[heads].reshape(GROUP * BLK, HS),
+                        scaled_s[pl.ds((j + 1) * GROUP, GROUP)].reshape(GROUP * BLK, HS),
+                    ],
+                    axis=1,
+                )
+                next_keys = kv_s[:, (j + 1) * HS : (j + 2) * HS]
+                none = jnp.zeros((BLK, HS), jnp.bfloat16)
+                both_keys = jnp.concatenate(
+                    [
+                        jnp.concatenate([keys, none], axis=1),
+                        jnp.concatenate([none, next_keys], axis=1),
+                    ],
+                    axis=0,
+                )
+                both_scores = lax.dot_general(
+                    queries, both_keys, (((1,), (1,)), ((), ())), preferred_element_type=jnp.float32
+                )
+            scores = both_scores[:, (j % 2) * BLK : (j % 2 + 1) * BLK]
             scores = scores.reshape(GROUP, BLK, BLK) + bias
             top = jnp.max(scores, axis=-1, keepdims=True)
             weights = jnp.exp2((scores - top) * scale).astype(jnp.bfloat16).reshape(GROUP * BLK, BLK)

time: 179 us -> 178 us (level)
  no operation moved by 1% of the time
where the time goes in v8:
time: 178 us
  waiting for transfers between devices  73.2 us (41%)
  blocking collectives  50.1 us (28%)
  between operations  19.8 us (11%)
  Pallas kernels  19.2 us (11%)
  starting transfers between devices  7.37 us (4%)
  other arithmetic  4.94 us (3%)
  local copies, waits for them, and re-layouts  3.32 us (2%)
    all_gather x1, waiting for transfers between devices, local(): lax.all_gather(kv_weights[0], ('section', 'dp'), axis=0, tiled=True)  38.4 us
    all_to_all x1, blocking collectives, route(): lax.all_to_all(pieces, ALL, split_axis=0, concat_axis=0, tiled=True)  33.2 us
    all_to_all x1, waiting for transfers between devices, route(): lax.all_to_all(ordered, ALL, split_axis=0, concat_axis=0, tiled=True)  24.9 us
    all_to_all x1, blocking collectives, local(): parts = lax.all_to_all(part, ALL, split_axis=0, concat_axis=0, tiled=True)  16.9 us
    pallas_call x1, Pallas kernels, run_layers(): pl.pallas_call(layers_kernel, out_shape=(jax.ShapeDtypeStruct((BLK, HD),...  16.8 us
    all_to_all x1, waiting for transfers between devices, local(): lax.all_to_all(jnp.broadcast_to(message[None], (device_count, 2, HS)), AL...  9.25 us
    all_to_all x1, starting transfers between devices, local(): lax.all_to_all(jnp.broadcast_to(message[None], (device_count, 2, HS)), AL...  3.77 us
    all_to_all x1, starting transfers between devices, route(): lax.all_to_all(ordered, ALL, split_axis=0, concat_axis=0, tiled=True)  3.56 us
  transfers between devices with their start and end apart: 3, of which 3 were waited for; matrix products, arithmetic and copies ran while one was open for 4% of the time, Pallas kernels for 1%

profile of v8, /device:TPU:1, one launch (start us, length us, event | category | flops | bytes accessed | tf_op | source)
XLA Modules:
  0.0 178.0 jit_solution(2056609316055296636)
XLA Ops:
  7.2 0.0 copy-start
  7.2 0.0 all-gather.3.cloned.1.call-start
  7.2 0.7 all-gather.3.cloned.1.call-update
  7.9 0.5 copy-done
  8.4 0.3 copy_bitcast_fusion
  8.7 33.2 %all_to_all.20.landed_ref = bf16[128,32,128]{2,1,0:T(8,128)(2,1)} all-to-all(bf16[128,32,128]{2,1,0:T(8,128)(2,1)S(1)} %bitcast.21), channel_id=1, replica_groups=mesh['dp'=32,'section'=4] {'dp','section'}, dimensions={0} | all-to-all | bytes 2097152 | tf_op jit(solution)/shard_map/all_to_all | solution.py:173
  41.9 2.4 %order.1 = bf16[128,32,128]{2,1,0:T(8,128)(2,1)} custom-call(s32[128]{0:T(128)} %plan_ref.1, bf16[128,32,128]{2,1,0:T(8,128)(2,1)} %all_to_all.20.landed_ref), custom_call_target="tpu_custom_call" | custom-call | tf_op jit(solution)/shard_map/order/pallas_call | solution.py:175
  44.3 3.6 %all-to-all-start.1 = ((bf16[128,32,128]{2,1,0:T(8,128)(2,1)}), bf16[128,32,128]{2,1,0:T(8,128)(2,1)S(1)}, u32[]{:S(2)}, u32[]{:S(2)}) async-start(bf16[128,32,128]{2,1,0:T(8,128)(2,1)} %order.1), calls=%async_computation.1 | async-start | bytes 2097152 | tf_op jit(solution)/shard_map/all_to_all | solution.py:182
  47.9 1.3 reduce_sum.27
  49.8 0.7 convert.10
  50.5 0.6 compare_reduce_fusion
  51.1 0.7 constant_dynamic-slice_fusion
  51.8 24.9 %all-to-all-done.1 = bf16[128,32,128]{2,1,0:T(8,128)(2,1)S(1)} async-done(((bf16[128,32,128]{2,1,0:T(8,128)(2,1)}), bf16[128,32,128]{2,1,0:T(8,128)(2,1)S(1)}, u32[]{:S(2)}, u32[]{:S(2)}) %all-to-all-start.1) | async-done | bytes 1048608 | tf_op jit(solution)/shard_map/all_to_all | solution.py:182
  76.7 0.5 slice.44
  78.5 0.7 broadcast_select_fusion
  79.2 0.7 broadcast_in_dim.21
  79.9 3.8 %all-to-all-start.2 = ((bf16[128,2,128]{2,1,0:T(2,128)(2,1)}), bf16[128,2,128]{2,1,0:T(2,128)(2,1)S(1)}, u32[]{:S(2)}, u32[]{:S(2)}) async-start(bf16[128,2,128]{2,1,0:T(2,128)(2,1)} %broadcast_in_dim.21), calls=%async_computation.2 | async-start | bytes 131072 | tf_op jit(solution)/shard_map/all_to_all | solution.py:199
  83.7 0.7 broadcast_compare_fusion
  84.4 9.2 %all-to-all-done.2 = bf16[128,2,128]{2,1,0:T(2,128)(2,1)S(1)} async-done(((bf16[128,2,128]{2,1,0:T(2,128)(2,1)}), bf16[128,2,128]{2,1,0:T(2,128)(2,1)S(1)}, u32[]{:S(2)}, u32[]{:S(2)}) %all-to-all-start.2) | async-done | bytes 65568 | tf_op jit(solution)/shard_map/all_to_all | solution.py:199
  93.6 0.1 fusion.1
  93.7 0.1 select_reduce_fusion
  93.8 0.7 fusion.2
  96.5 0.1 copy.16.gain_ref
  96.5 38.4 %all-gather.3.cloned.1.call-done = bf16[1,16384,1024]{2,1,0:T(8,128)(2,1)} async-done(((bf16[1,128,1024]{2,1,0:T(8,128)(2,1)}), bf16[1,16384,1024]{2,1,0:T(8,128)(2,1)}) %all-gather.3.cloned.1.call-update) | async-done | bytes 33554448 | tf_op jit(solution)/shard_map/all_gather | solution.py:189
  134.9 16.8 %layers.1 = (bf16[128,4096]{1,0:T(8,128)(2,1)}, f32[128,1,128]{2,1,0:T(1,128)S(1)}) custom-call(s32[1]{0:T(128)S(6)} %convert_element_type.26.code_ref, bf16[32,128,128]{2,1,0:T(8,128)(2,1)S(1)} %bitcast.19, bf16[4,32,1,128]{3,2,1,0:T(2,128)(2,1)S(1)} %copy.16.gain_ref, bf16[128,4096]{1,0:T(8,128)(2,1)} %frozen_ref.1, bf16[4,4096,1024]{2,1,0:T(8,128)(2,1)} %bitcast.20), custom_call_target="tpu_custom_call" | custom-call | tf_op jit(solution)/shard_map/layers/pallas_call | solution.py:136
  151.7 16.9 %all_to_all.21 = f32[128,1,128]{2,1,0:T(1,128)S(1)} all-to-all(f32[128,1,128]{2,1,0:T(1,128)S(1)} %get-tuple-element.17), channel_id=1, replica_groups=mesh['dp'=32,'section'=4] {'dp','section'}, dimensions={0} | all-to-all | bytes 131072 | tf_op jit(solution)/shard_map/all_to_all | solution.py:207
  168.6 0.7 slice_reduce_fusion
  (2 shorter events, 0.0 us)
Async XLA Ops:
  7.2 1.2 copy-start
  7.2 127.7 %all-gather.3.cloned.1.call-start = ((), (), s32[]{:S(2)}) async-start(), calls=%async_computation.4 | async-start | bytes 33816576 | tf_op jit(solution)/shard_map/all_gather | solution.py:189
  44.3 32.4 %all-to-all-start.1 = ((bf16[128,32,128]{2,1,0:T(8,128)(2,1)}), bf16[128,32,128]{2,1,0:T(8,128)(2,1)S(1)}, u32[]{:S(2)}, u32[]{:S(2)}) async-start(bf16[128,32,128]{2,1,0:T(8,128)(2,1)} %order.1), calls=%async_computation.1 | async-start | bytes 2097152 | tf_op jit(solution)/shard_map/all_to_all | solution.py:182
  79.9 13.7 %all-to-all-start.2 = ((bf16[128,2,128]{2,1,0:T(2,128)(2,1)}), bf16[128,2,128]{2,1,0:T(2,128)(2,1)S(1)}, u32[]{:S(2)}, u32[]{:S(2)}) async-start(bf16[128,2,128]{2,1,0:T(2,128)(2,1)} %broadcast_in_dim.21), calls=%async_computation.2 | async-start | bytes 131072 | tf_op jit(solution)/shard_map/all_to_all | solution.py:199
Sparse Core Ops, SparseCore 0:
  11.0 123.8 all-gather.2

commit v9 on v8

--- a/solution.py
+++ b/solution.py
@@ -168,9 +168,17 @@
     lax.fori_loop(0, landed_ref.shape[0], place, 0, unroll=8)
 
 
+def exchange(pieces):
+    section_count = lax.axis_size("section")
+    grid = pieces.reshape((-1, section_count) + pieces.shape[1:])
+    grid = lax.all_to_all(grid, "section", split_axis=1, concat_axis=1, tiled=True)
+    grid = lax.all_to_all(grid, "dp", split_axis=0, concat_axis=0, tiled=True)
+    return grid.reshape(pieces.shape)
+
+
 def route(hidden_in, block_plan):
     pieces = hidden_in.reshape(BLK, QH, HS).transpose(1, 0, 2).reshape(-1, PIECE_ROWS, HS)
-    landed = lax.all_to_all(pieces, ALL, split_axis=0, concat_axis=0, tiled=True)
+    landed = exchange(pieces)
     vmem = pl.BlockSpec(memory_space=pltpu.VMEM)
     ordered = pl.pallas_call(
         order_kernel,
@@ -179,7 +187,7 @@
         out_specs=vmem,
         name="order",
     )(block_plan, landed)
-    arrived = lax.all_to_all(ordered, ALL, split_axis=0, concat_axis=0, tiled=True)
+    arrived = exchange(ordered)
     return arrived.reshape(QH, BLK, HS)
 
 

time: 178 us -> 186 us (1.045)
  waiting for transfers between devices: 73.2 us -> 33 us
  blocking collectives: 50.1 us -> 87.2 us
  starting transfers between devices: 7.37 us -> 14.3 us
  local copies, waits for them, and re-layouts: 3.32 us -> 6.83 us
    all_to_all x1 -> x3, blocking collectives: 33.2 us -> 73.5 us  [the longest x2 40.5 us: exchange(): lax.all_to_all(grid, 'section', split_axis=1, concat_axis=1, tiled=True)]
    all_gather x1, waiting for transfers between devices: 38.4 us -> 0.02 us  [local(): lax.all_gather(kv_weights[0], ('section', 'dp'), axis=0, tiled=True)]
    all_to_all x1, starting transfers between devices: 3.56 us -> 8.12 us  [exchange(): grid = lax.all_to_all(grid, 'dp', split_axis=0, concat_axis=0, tiled=True)]
    all_to_all x1, blocking collectives: 16.9 us -> 13.8 us  [local(): parts = lax.all_to_all(part, ALL, split_axis=0, concat_axis=0, tiled=True)]
    all_to_all x1, starting transfers between devices: 3.77 us -> 6.1 us  [local(): lax.all_to_all(jnp.broadcast_to(message[None], (device_count, 2, HS)), AL...]
  transfers between devices with their start and end apart: 3 -> 3, of which waited for: 3 -> 2; matrix products, arithmetic and copies ran while one was open for 4% -> 6% of each run, Pallas kernels for 1% -> 1%
where the time goes in v9:
time: 186 us; the launch traced here: 185 us
  blocking collectives  87.2 us (47%)
  waiting for transfers between devices  33 us (18%)
  between operations  19.9 us (11%)
  Pallas kernels  19.2 us (10%)
  starting transfers between devices  14.3 us (8%)
  local copies, waits for them, and re-layouts  6.83 us (4%)
  other arithmetic  4.92 us (3%)
    all_to_all x2, blocking collectives, exchange(): lax.all_to_all(grid, 'section', split_axis=1, concat_axis=1, tiled=True)  40.5 us
    all_to_all x1, blocking collectives, exchange(): grid = lax.all_to_all(grid, 'dp', split_axis=0, concat_axis=0, tiled=True)  33 us
    all_to_all x1, waiting for transfers between devices, exchange(): grid = lax.all_to_all(grid, 'dp', split_axis=0, concat_axis=0, tiled=True)  23.4 us
    pallas_call x1, Pallas kernels, run_layers(): pl.pallas_call(layers_kernel, out_shape=(jax.ShapeDtypeStruct((BLK, HD),...  16.8 us
    all_to_all x1, blocking collectives, local(): parts = lax.all_to_all(part, ALL, split_axis=0, concat_axis=0, tiled=True)  13.8 us
    all_to_all x1, waiting for transfers between devices, local(): lax.all_to_all(jnp.broadcast_to(message[None], (device_count, 2, HS)), AL...  8.97 us
    all_to_all x1, starting transfers between devices, exchange(): grid = lax.all_to_all(grid, 'dp', split_axis=0, concat_axis=0, tiled=True)  8.12 us
    all_to_all x1, starting transfers between devices, local(): lax.all_to_all(jnp.broadcast_to(message[None], (device_count, 2, HS)), AL...  6.1 us
  transfers between devices with their start and end apart: 3, of which 2 were waited for; matrix products, arithmetic and copies ran while one was open for 6% of the time, Pallas kernels for 1%

profile of v9, /device:TPU:1, one launch (start us, length us, event | category | flops | bytes accessed | tf_op | source)
XLA Modules:
  0.0 185.4 jit_solution(16349780178360879639)
XLA Ops:
  7.2 0.0 copy-start
  7.2 0.0 all-gather.3.cloned.1.call-start
  7.2 0.7 all-gather.3.cloned.1.call-update
  7.9 1.6 copy.35
  9.5 0.7 copy.36
  10.2 0.1 copy.37
  10.3 18.8 %all_to_all.30 = bf16[32,4,32,128]{3,2,0,1:T(8,128)(2,1)S(1)} all-to-all(bf16[32,4,32,128]{3,2,0,1:T(8,128)(2,1)S(1)} %copy.37), channel_id=1, replica_groups=mesh['dp'=32,'section'=4] {'section'}, dimensions={1} | all-to-all | bytes 2097152 | tf_op jit(solution)/shard_map/all_to_all | solution.py:174
  29.1 0.1 copy.38
  29.3 33.0 %all_to_all.31 = bf16[32,4,32,128]{3,2,1,0:T(8,128)(2,1)} all-to-all(bf16[32,4,32,128]{3,2,1,0:T(8,128)(2,1)S(1)} %copy.38), channel_id=1, replica_groups=mesh['dp'=32,'section'=4] {'dp'}, dimensions={0} | all-to-all | bytes 2097152 | tf_op jit(solution)/shard_map/all_to_all | solution.py:175
  62.3 2.4 %order.1 = bf16[128,32,128]{2,1,0:T(8,128)(2,1)} custom-call(s32[128]{0:T(128)} %plan_ref.1, bf16[128,32,128]{2,1,0:T(8,128)(2,1)} %bitcast.19), custom_call_target="tpu_custom_call" | custom-call | tf_op jit(solution)/shard_map/order/pallas_call | solution.py:183
  64.7 1.3 copy.39
  66.0 21.7 %all_to_all.32 = bf16[32,4,32,128]{3,2,0,1:T(8,128)(2,1)S(1)} all-to-all(bf16[32,4,32,128]{3,2,0,1:T(8,128)(2,1)S(1)} %copy.39), channel_id=1, replica_groups=mesh['dp'=32,'section'=4] {'section'}, dimensions={1} | all-to-all | bytes 2097152 | tf_op jit(solution)/shard_map/all_to_all | solution.py:174
  87.7 1.1 copy.40
  88.8 8.1 %all-to-all-start.3 = ((bf16[32,4,32,128]{3,2,1,0:T(8,128)(2,1)}), bf16[32,4,32,128]{3,2,1,0:T(8,128)(2,1)S(1)}, u32[]{:S(2)}, u32[]{:S(2)}) async-start(bf16[32,4,32,128]{3,2,1,0:T(8,128)(2,1)} %copy.40), calls=%async_computation.3 | async-start | bytes 2097152 | tf_op jit(solution)/shard_map/all_to_all | solution.py:175
  96.9 1.3 reduce_sum.27
  98.9 0.7 convert.10
  99.5 0.6 compare_reduce_fusion
  100.2 0.0 copy-done
  100.2 23.4 %all-to-all-done.3 = bf16[32,4,32,128]{3,2,1,0:T(8,128)(2,1)S(1)} async-done(((bf16[32,4,32,128]{3,2,1,0:T(8,128)(2,1)}), bf16[32,4,32,128]{3,2,1,0:T(8,128)(2,1)S(1)}, u32[]{:S(2)}, u32[]{:S(2)}) %all-to-all-start.3) | async-done | bytes 1048608 | tf_op jit(solution)/shard_map/all_to_all | solution.py:175
  123.5 0.5 slice.44
  125.4 0.7 broadcast_select_fusion
  126.1 0.7 broadcast_in_dim.21
  126.8 6.1 %all-to-all-start.4 = ((bf16[128,2,128]{2,1,0:T(2,128)(2,1)}), bf16[128,2,128]{2,1,0:T(2,128)(2,1)S(1)}, u32[]{:S(2)}, u32[]{:S(2)}) async-start(bf16[128,2,128]{2,1,0:T(2,128)(2,1)} %broadcast_in_dim.21), calls=%async_computation.4 | async-start | bytes 131072 | tf_op jit(solution)/shard_map/all_to_all | solution.py:207
  132.9 0.7 broadcast_compare_fusion
  133.6 9.0 %all-to-all-done.4 = bf16[128,2,128]{2,1,0:T(2,128)(2,1)S(1)} async-done(((bf16[128,2,128]{2,1,0:T(2,128)(2,1)}), bf16[128,2,128]{2,1,0:T(2,128)(2,1)S(1)}, u32[]{:S(2)}, u32[]{:S(2)}) %all-to-all-start.4) | async-done | bytes 65568 | tf_op jit(solution)/shard_map/all_to_all | solution.py:207
  142.5 0.1 fusion.1
  142.6 0.1 select_reduce_fusion
  142.7 0.7 fusion.2
  145.4 0.1 copy.43.gain_ref
  145.4 0.0 all-gather.3.cloned.1.call-done
  145.5 16.8 %layers.1 = (bf16[128,4096]{1,0:T(8,128)(2,1)}, f32[128,1,128]{2,1,0:T(1,128)S(1)}) custom-call(s32[1]{0:T(128)S(6)} %convert_element_type.26.code_ref, bf16[32,128,128]{2,1,0:T(8,128)(2,1)S(1)} %bitcast.17, bf16[4,32,1,128]{3,2,1,0:T(2,128)(2,1)S(1)} %copy.43.gain_ref, bf16[128,4096]{1,0:T(8,128)(2,1)} %frozen_ref.1, bf16[4,4096,1024]{2,1,0:T(8,128)(2,1)} %bitcast.18), custom_call_target="tpu_custom_call" | custom-call | tf_op jit(solution)/shard_map/layers/pallas_call | solution.py:136
  162.3 13.8 %all_to_all.33 = f32[128,1,128]{2,1,0:T(1,128)S(1)} all-to-all(f32[128,1,128]{2,1,0:T(1,128)S(1)} %get-tuple-element.17), channel_id=1, replica_groups=mesh['dp'=32,'section'=4] {'dp','section'}, dimensions={0} | all-to-all | bytes 131072 | tf_op jit(solution)/shard_map/all_to_all | solution.py:215
  176.0 0.7 slice_reduce_fusion
  (3 shorter events, 0.0 us)
Async XLA Ops:
  7.2 93.0 %copy-start = (bf16[1,4096]{1,0:T(2,128)(2,1)S(1)}, bf16[1,4096]{1,0:T(2,128)(2,1)}, u32[]{:S(2)}) copy-start(bf16[1,4096]{1,0:T(2,128)(2,1)} %param.13) | copy-start | bytes 24580
  7.2 138.3 %all-gather.3.cloned.1.call-start = ((), (), s32[]{:S(2)}) async-start(), calls=%async_computation.6 | async-start | bytes 33816576 | tf_op jit(solution)/shard_map/all_gather | solution.py:197
  88.8 34.8 %all-to-all-start.3 = ((bf16[32,4,32,128]{3,2,1,0:T(8,128)(2,1)}), bf16[32,4,32,128]{3,2,1,0:T(8,128)(2,1)S(1)}, u32[]{:S(2)}, u32[]{:S(2)}) async-start(bf16[32,4,32,128]{3,2,1,0:T(8,128)(2,1)} %copy.40), calls=%async_computation.3 | async-start | bytes 2097152 | tf_op jit(solution)/shard_map/all_to_all | solution.py:175
  126.8 15.7 %all-to-all-start.4 = ((bf16[128,2,128]{2,1,0:T(2,128)(2,1)}), bf16[128,2,128]{2,1,0:T(2,128)(2,1)S(1)}, u32[]{:S(2)}, u32[]{:S(2)}) async-start(bf16[128,2,128]{2,1,0:T(2,128)(2,1)} %broadcast_in_dim.21), calls=%async_computation.4 | async-start | bytes 131072 | tf_op jit(solution)/shard_map/all_to_all | solution.py:207
Sparse Core Ops, SparseCore 0:
  11.0 126.0 all-gather.2

commit v10 on v8

--- a/solution.py
+++ b/solution.py
@@ -28,9 +28,9 @@
     depth = HD // CHUNKS
 
     def w_copy(layer, c):
-        rows = pl.ds(c * depth, depth)
+        slabs = pl.ds(c * GROUP, GROUP)
         return pltpu.make_async_copy(
-            w_ref.at[layer, rows], w_buf.at[layer, rows], sems.at[layer, c]
+            w_ref.at[slabs, layer], w_buf.at[layer, slabs], sems.at[layer, c]
         )
 
     def prepare(layer, j, states, squares):
@@ -43,7 +43,7 @@
     def project(layer, j):
         rows = jnp.concatenate([scaled_s[j * GROUP + i] for i in range(GROUP)], axis=1)
         part = jnp.dot(
-            rows, w_buf[layer, j * depth : (j + 1) * depth, :], preferred_element_type=jnp.float32
+            rows, w_buf[layer, j * GROUP : (j + 1) * GROUP].reshape(depth, KVW), preferred_element_type=jnp.float32
         )
         if j == 0:
             acc_s[...] = part
@@ -150,7 +150,7 @@
             pltpu.VMEM((QH, BLK, HS), jnp.bfloat16),
             pltpu.VMEM((BLK, KVW), jnp.float32),
             pltpu.VMEM((BLK, KVW), jnp.bfloat16),
-            pltpu.VMEM((4, HD, KVW), jnp.bfloat16),
+            pltpu.VMEM((4, QH, HS, KVW), jnp.bfloat16),
             pltpu.SemaphoreType.DMA((4, CHUNKS)),
             pltpu.VMEM((BLK, HD), jnp.bfloat16),
             pltpu.SemaphoreType.DMA,
@@ -186,8 +186,8 @@
 def local(hidden_in, segments, forget_flags, block_plan, layer_gains, kv_weights, frozen_states):
     device_count = lax.axis_size("dp") * lax.axis_size("section")
     here = lax.axis_index(ALL)
-    weights = lax.all_gather(kv_weights[0], ("section", "dp"), axis=0, tiled=True)
-    weights = weights.reshape(4, HD, KVW)
+    weights = lax.all_gather(kv_weights[0], ALL, axis=0, tiled=True)
+    weights = weights.reshape(QH, 4, HS, KVW)
     boundary = BLK - jnp.sum(segments[0])
     pieces = route(hidden_in, block_plan)
     sample = pieces[0, 0, 0]

time: 178 us -> 178 us (level)
  no operation moved by 1% of the time
where the time goes in v10:
time: 178 us
  waiting for transfers between devices  73.2 us (41%)
  blocking collectives  50.1 us (28%)
  between operations  19.8 us (11%)
  Pallas kernels  19.2 us (11%)
  starting transfers between devices  7.39 us (4%)
  other arithmetic  4.94 us (3%)
  local copies, waits for them, and re-layouts  3.32 us (2%)
    all_gather x1, waiting for transfers between devices, local(): weights = lax.all_gather(kv_weights[0], ALL, axis=0, tiled=True)  38.4 us
    all_to_all x1, blocking collectives, route(): lax.all_to_all(pieces, ALL, split_axis=0, concat_axis=0, tiled=True)  33.2 us
    all_to_all x1, waiting for transfers between devices, route(): lax.all_to_all(ordered, ALL, split_axis=0, concat_axis=0, tiled=True)  24.9 us
    all_to_all x1, blocking collectives, local(): parts = lax.all_to_all(part, ALL, split_axis=0, concat_axis=0, tiled=True)  16.9 us
    pallas_call x1, Pallas kernels, run_layers(): pl.pallas_call(layers_kernel, out_shape=(jax.ShapeDtypeStruct((BLK, HD),...  16.8 us
    all_to_all x1, waiting for transfers between devices, local(): lax.all_to_all(jnp.broadcast_to(message[None], (device_count, 2, HS)), AL...  9.24 us
    all_to_all x1, starting transfers between devices, local(): lax.all_to_all(jnp.broadcast_to(message[None], (device_count, 2, HS)), AL...  3.79 us
    all_to_all x1, starting transfers between devices, route(): lax.all_to_all(ordered, ALL, split_axis=0, concat_axis=0, tiled=True)  3.56 us
  transfers between devices with their start and end apart: 3, of which 3 were waited for; matrix products, arithmetic and copies ran while one was open for 4% of the time, Pallas kernels for 1%

profile of v10, /device:TPU:1, one launch (start us, length us, event | category | flops | bytes accessed | tf_op | source)
XLA Modules:
  0.0 178.0 jit_solution(17045829357901223048)
XLA Ops:
  7.2 0.0 copy-start
  7.2 0.0 all-gather.3.cloned.1.call-start
  7.2 0.7 all-gather.3.cloned.1.call-update
  7.9 0.5 copy-done
  8.4 0.3 copy_bitcast_fusion
  8.7 33.2 %all_to_all.20.landed_ref = bf16[128,32,128]{2,1,0:T(8,128)(2,1)} all-to-all(bf16[128,32,128]{2,1,0:T(8,128)(2,1)S(1)} %bitcast.21), channel_id=1, replica_groups=mesh['dp'=32,'section'=4] {'dp','section'}, dimensions={0} | all-to-all | bytes 2097152 | tf_op jit(solution)/shard_map/all_to_all | solution.py:173
  41.9 2.4 %order.1 = bf16[128,32,128]{2,1,0:T(8,128)(2,1)} custom-call(s32[128]{0:T(128)} %plan_ref.1, bf16[128,32,128]{2,1,0:T(8,128)(2,1)} %all_to_all.20.landed_ref), custom_call_target="tpu_custom_call" | custom-call | tf_op jit(solution)/shard_map/order/pallas_call | solution.py:175
  44.3 3.6 %all-to-all-start.1 = ((bf16[128,32,128]{2,1,0:T(8,128)(2,1)}), bf16[128,32,128]{2,1,0:T(8,128)(2,1)S(1)}, u32[]{:S(2)}, u32[]{:S(2)}) async-start(bf16[128,32,128]{2,1,0:T(8,128)(2,1)} %order.1), calls=%async_computation.1 | async-start | bytes 2097152 | tf_op jit(solution)/shard_map/all_to_all | solution.py:182
  47.9 1.3 reduce_sum.27
  49.8 0.7 convert.10
  50.5 0.6 compare_reduce_fusion
  51.1 0.7 constant_dynamic-slice_fusion
  51.8 24.9 %all-to-all-done.1 = bf16[128,32,128]{2,1,0:T(8,128)(2,1)S(1)} async-done(((bf16[128,32,128]{2,1,0:T(8,128)(2,1)}), bf16[128,32,128]{2,1,0:T(8,128)(2,1)S(1)}, u32[]{:S(2)}, u32[]{:S(2)}) %all-to-all-start.1) | async-done | bytes 1048608 | tf_op jit(solution)/shard_map/all_to_all | solution.py:182
  76.7 0.5 slice.44
  78.5 0.7 broadcast_select_fusion
  79.2 0.7 broadcast_in_dim.21
  79.9 3.8 %all-to-all-start.2 = ((bf16[128,2,128]{2,1,0:T(2,128)(2,1)}), bf16[128,2,128]{2,1,0:T(2,128)(2,1)S(1)}, u32[]{:S(2)}, u32[]{:S(2)}) async-start(bf16[128,2,128]{2,1,0:T(2,128)(2,1)} %broadcast_in_dim.21), calls=%async_computation.2 | async-start | bytes 131072 | tf_op jit(solution)/shard_map/all_to_all | solution.py:199
  83.7 0.7 broadcast_compare_fusion
  84.4 9.2 %all-to-all-done.2 = bf16[128,2,128]{2,1,0:T(2,128)(2,1)S(1)} async-done(((bf16[128,2,128]{2,1,0:T(2,128)(2,1)}), bf16[128,2,128]{2,1,0:T(2,128)(2,1)S(1)}, u32[]{:S(2)}, u32[]{:S(2)}) %all-to-all-start.2) | async-done | bytes 65568 | tf_op jit(solution)/shard_map/all_to_all | solution.py:199
  93.6 0.1 fusion.1
  93.7 0.1 select_reduce_fusion
  93.8 0.7 fusion.2
  96.5 0.1 copy.16.gain_ref
  96.5 38.4 %all-gather.3.cloned.1.call-done = bf16[1,16384,1024]{2,1,0:T(8,128)(2,1)} async-done(((bf16[1,128,1024]{2,1,0:T(8,128)(2,1)}), bf16[1,16384,1024]{2,1,0:T(8,128)(2,1)}) %all-gather.3.cloned.1.call-update) | async-done | bytes 33554448 | tf_op jit(solution)/shard_map/all_gather | solution.py:189
  134.9 16.8 %layers.1 = (bf16[128,4096]{1,0:T(8,128)(2,1)}, f32[128,1,128]{2,1,0:T(1,128)S(1)}) custom-call(s32[1]{0:T(128)S(6)} %convert_element_type.26.code_ref, bf16[32,128,128]{2,1,0:T(8,128)(2,1)S(1)} %bitcast.19, bf16[4,32,1,128]{3,2,1,0:T(2,128)(2,1)S(1)} %copy.16.gain_ref, bf16[128,4096]{1,0:T(8,128)(2,1)} %frozen_ref.1, bf16[32,4,128,1024]{3,2,1,0:T(8,128)(2,1)} %bitcast.20), custom_call_target="tpu_custom_call" | custom-call | tf_op jit(solution)/shard_map/layers/pallas_call | solution.py:136
  151.7 16.9 %all_to_all.21 = f32[128,1,128]{2,1,0:T(1,128)S(1)} all-to-all(f32[128,1,128]{2,1,0:T(1,128)S(1)} %get-tuple-element.17), channel_id=1, replica_groups=mesh['dp'=32,'section'=4] {'dp','section'}, dimensions={0} | all-to-all | bytes 131072 | tf_op jit(solution)/shard_map/all_to_all | solution.py:207
  168.7 0.7 slice_reduce_fusion
  (2 shorter events, 0.0 us)
Async XLA Ops:
  7.2 1.2 copy-start
  7.2 127.8 %all-gather.3.cloned.1.call-start = ((), (), s32[]{:S(2)}) async-start(), calls=%async_computation.4 | async-start | bytes 33816576 | tf_op jit(solution)/shard_map/all_gather | solution.py:189
  44.3 32.4 %all-to-all-start.1 = ((bf16[128,32,128]{2,1,0:T(8,128)(2,1)}), bf16[128,32,128]{2,1,0:T(8,128)(2,1)S(1)}, u32[]{:S(2)}, u32[]{:S(2)}) async-start(bf16[128,32,128]{2,1,0:T(8,128)(2,1)} %order.1), calls=%async_computation.1 | async-start | bytes 2097152 | tf_op jit(solution)/shard_map/all_to_all | solution.py:182
  79.9 13.7 %all-to-all-start.2 = ((bf16[128,2,128]{2,1,0:T(2,128)(2,1)}), bf16[128,2,128]{2,1,0:T(2,128)(2,1)S(1)}, u32[]{:S(2)}, u32[]{:S(2)}) async-start(bf16[128,2,128]{2,1,0:T(2,128)(2,1)} %broadcast_in_dim.21), calls=%async_computation.2 | async-start | bytes 131072 | tf_op jit(solution)/shard_map/all_to_all | solution.py:199
Sparse Core Ops, SparseCore 0:
  11.2 123.7 all-gather.2
